TPU v7x, 32 devices: a whole 2x2x4 slice. The times are simulated.
32 devices in a mesh: ctx: 8 (over z, y), head: 4 (over x, core).
Axes of the slice: x: 2, y: 2, z: 4, core: 2. Of those that a mesh axis runs over, the one named last changes fastest.
Arguments:
- tokens: bfloat16 [4096, 2048], P('ctx', 'head'), may hold values from -6 to 6
- value_weight: bfloat16 [2048, 4096], P('ctx', 'head'), may hold values from -0.125 to 0.125
- queries: bfloat16 [4096, 128], P('ctx'), may hold values from -2.390625 to 2.390625
- key_vectors: bfloat16 [4096, 128], P('ctx'), may hold values from -2.390625 to 2.390625
- level_weight: float32 [13, 64, 4096], P(None, 'head', 'ctx'), may hold values from 0.2 to 1
Outputs:
- attended: bfloat16 [4096, 4096], P('ctx', 'head')
All inputs are finite; a program needn't handle non-finite values.
Results may differ from a plain program's by a relative error of at most 0.006.
Values may be sent and summed in bfloat16 or wider, within the bound.
No kernel may reach another device: no remote copies, remote signals or barrier semaphores. Data moves between devices by JAX's collectives and lax.ppermute only.
A program may use at most 64 MiB of HBM per device.

v0:
```python
import functools

import jax
import jax.numpy as jnp
from jax import lax
from jax.experimental import pallas as pl
from jax.experimental.pallas import tpu as pltpu
from jax.sharding import PartitionSpec as P


F32 = jnp.float32
BF16 = jnp.bfloat16


def from_partner(block, axis, distance):
    count = lax.axis_size(axis)
    route = []
    for low in range(count):
        high = low | 1 << distance
        if high != low and high < count:
            route += [(low, high), (high, low)]
    return lax.ppermute(block, axis, route)


def gather_pieces(block, axis):
    pieces = [block]
    masks = [0]
    for bit in reversed(range(lax.axis_size(axis).bit_length() - 1)):
        for mask, piece in zip(list(masks), list(pieces)):
            pieces.append(from_partner(piece, axis, bit))
            masks.append(mask | 1 << bit)
    return [piece for _, piece in sorted(zip(masks, pieces), key=lambda pair: pair[0])]


def level_scale(level_num):
    return 1.0 if level_num == 0 else 2.0 ** (-(level_num - 1) / 2.0)


def on_chip(*arrays):
    return [pltpu.with_memory_space_constraint(array, pltpu.VMEM) for array in arrays]


def dot_last(left, right):
    return lax.dot_general(left, right, (((1,), (1,)), ((), ())), preferred_element_type=F32)


def spread_rows(row, count):
    return jnp.broadcast_to(row, (count, row.shape[1]))


def prepare_kernel(q_ref, k_ref, w_ref, *rest):
    near_refs, (score_ref, row_ref) = rest[:-2], rest[-2:]
    length = q_ref.shape[0]
    heads = w_ref.shape[1]
    rows = near_refs[0].shape[2]
    tile = min(128, length)
    sub = 8
    tile_levels = tile.bit_length() - 1
    sub_levels = sub.bit_length() - 1
    score_ref[...] = dot_last(k_ref[...], q_ref[...]).astype(BF16).astype(F32)

    for num in range(length.bit_length()):
        for head in range(heads):
            row_ref[head, num : num + 1, :] = w_ref[num, head : head + 1, :] * level_scale(num)

    def grid_level(shape, shift):
        s_pos = lax.broadcasted_iota(jnp.int32, shape, 0)
        t_pos = jnp.right_shift(lax.broadcasted_iota(jnp.int32, shape, 1), shift)
        if shift == 0:
            t_pos = jnp.bitwise_and(t_pos, sub - 1)
        differ = jnp.bitwise_xor(s_pos, t_pos)
        level = jnp.zeros(shape, jnp.int32)
        for bit in range(tile_levels):
            level = level + (jnp.right_shift(differ, bit) > 0).astype(jnp.int32)
        return jnp.where(s_pos <= t_pos, level, -1)

    fine = grid_level((sub, tile), 0)
    coarse = grid_level((tile // sub, tile), sub_levels)
    near_diag = lax.broadcasted_iota(jnp.int32, (tile, tile), 0) // sub == (
        lax.broadcasted_iota(jnp.int32, (tile, tile), 1) // sub
    )

    def one_head(head, carry):
        for t_tile in range(length // tile):
            t0 = t_tile * tile
            block = t0 // rows
            near_ref = near_refs[block]
            c0 = t0 - block * rows
            weight_rows = [
                row_ref[head, num : num + 1, t0 : t0 + tile]
                for num in range(length.bit_length())
            ]
            for s_tile in range((block + 1) * rows // tile):
                s0 = s_tile * tile
                if s_tile > t_tile:
                    near_ref[head, s0 : s0 + tile, c0 : c0 + tile] = jnp.zeros((tile, tile), BF16)
                    continue
                if s_tile == t_tile:
                    small = jnp.zeros((sub, tile), F32)
                    for num in range(sub_levels + 1):
                        small = jnp.where(fine == num, spread_rows(weight_rows[num], sub), small)
                    big = jnp.zeros((tile // sub, tile), F32)
                    for num in range(sub_levels + 1, tile_levels + 1):
                        big = jnp.where(
                            coarse == num - sub_levels,
                            spread_rows(weight_rows[num], tile // sub),
                            big,
                        )
                    big = jnp.concatenate(
                        [spread_rows(big[row : row + 1], sub) for row in range(tile // sub)], axis=0
                    )
                    weight = jnp.where(near_diag, jnp.concatenate([small] * (tile // sub), 0), big)
                else:
                    num = tile_levels + (s_tile ^ t_tile).bit_length()
                    weight = spread_rows(weight_rows[num], tile)
                score = score_ref[s0 : s0 + tile, t0 : t0 + tile]
                near_ref[head, s0 : s0 + tile, c0 : c0 + tile] = (weight * score).astype(BF16)
        return carry

    lax.fori_loop(0, heads, one_head, 0)


def prepare(queries, key_vectors, level_weight):
    length = queries.shape[0]
    heads = level_weight.shape[1]
    rows = min(256, length)
    return pl.pallas_call(
        prepare_kernel,
        out_shape=[
            pltpu.VMEM((heads, (block + 1) * rows, rows), BF16) for block in range(length // rows)
        ],
        scratch_shapes=[
            pltpu.VMEM((length, length), F32),
            pltpu.VMEM((heads, length.bit_length(), length), F32),
        ],
        compiler_params=pltpu.CompilerParams(vmem_limit_bytes=16 << 20),
        name="prepare",
    )(queries, key_vectors, level_weight)


def choose(where_ref, pieces, depth, chosen_ref, first, count):
    for num in range(count):
        piece = where_ref[2 * (first + num)]
        start = pl.multiple_of(where_ref[2 * (first + num) + 1], 128)
        for index, ref in enumerate(pieces):

            @pl.when(piece == index)
            def _():
                chosen_ref[:, num * depth : (num + 1) * depth] = ref[:, pl.ds(start, depth)]


def extend_kernel(piece_count, count, started, where_ref, *refs):
    pieces = refs[:piece_count]
    blocks = refs[piece_count : piece_count + count]
    out_ref, chosen_ref = refs[-2], refs[-1]
    depth = blocks[0].shape[1]
    choose(where_ref, pieces, depth, chosen_ref, 0, count)
    width = out_ref.shape[0]
    step = min(256, width)
    for c0 in range(0, width, step):
        left = jnp.concatenate([block[c0 : c0 + step, :] for block in blocks], axis=1)
        total = dot_last(left, chosen_ref[...])
        if started:
            total = total + refs[piece_count + count][c0 : c0 + step, :]
        out_ref[c0 : c0 + step, :] = total


def extend(total, pieces, parts):
    where = jnp.stack([num for pair, _ in parts for num in pair])
    blocks = [block for _, block in parts]
    rows = pieces[0].shape[0]
    width, depth = blocks[0].shape
    arrays = on_chip(*pieces, *blocks, *([] if total is None else [total]))
    return pl.pallas_call(
        functools.partial(extend_kernel, len(pieces), len(blocks), total is not None),
        in_specs=[pl.BlockSpec(memory_space=pltpu.SMEM)]
        + [pl.BlockSpec(memory_space=pltpu.VMEM)] * len(arrays),
        out_shape=pltpu.VMEM((width, rows), F32),
        scratch_shapes=[pltpu.VMEM((rows, depth * len(blocks)), BF16)],
        compiler_params=pltpu.CompilerParams(vmem_limit_bytes=12 << 20),
    )(where, *arrays)


def finish_kernel(piece_count, last_count, near_count, head_size, where_ref, *refs):
    refs = list(refs)
    take = lambda count: [refs.pop(0) for _ in range(count)]
    token_refs, sum_refs = take(piece_count), take(piece_count)
    last_refs = take(last_count)
    value_ref, state_ref, q_ref, w_ref = take(4)
    near_refs = take(near_count)
    out_ref = refs.pop(0)
    length, state_rows = q_ref.shape
    width = value_ref.shape[0]
    near_levels = length.bit_length()
    far_levels = w_ref.shape[0] - near_levels
    rows = length // near_count
    if last_count:
        token_chosen, sum_chosen = refs
        depth = token_chosen.shape[1]
        choose(where_ref, token_refs, depth, token_chosen, 0, 1)
        choose(where_ref, sum_refs, depth, sum_chosen, 0, 1)
    queries = q_ref[...]
    twice = jnp.concatenate([queries, queries], axis=1)
    step = min(256, width)
    unit = (
        lax.broadcasted_iota(jnp.int32, (rows, rows), 0)
        == lax.broadcasted_iota(jnp.int32, (rows, rows), 1)
    ).astype(BF16)
    for c0 in range(0, width, step):
        values, states = value_ref[c0 : c0 + step, :], state_ref[c0 : c0 + step, :]
        if last_count:
            share = width // last_count
            left = last_refs[c0 // share][c0 % share : c0 % share + step, :]
            values = values + dot_last(left, token_chosen[...])
            states = states + dot_last(left, sum_chosen[...])
        values = values.astype(BF16)
        heads = range(c0 // head_size, (c0 + step) // head_size)
        far = None
        for num in range(far_levels):
            state = states[:, num * state_rows : (num + 1) * state_rows]
            high = state.astype(BF16)
            low = (state - high.astype(F32)).astype(BF16)
            reading = dot_last(jnp.concatenate([high, low], axis=1), twice)
            level = near_levels + num
            weight = jnp.concatenate(
                [
                    spread_rows(w_ref[level, head : head + 1, :] * level_scale(level), head_size)
                    for head in heads
                ],
                axis=0,
            )
            far = weight * reading if far is None else far + weight * reading
        for block, near_ref in enumerate(near_refs):
            near = jnp.concatenate(
                [
                    jnp.dot(
                        values[
                            head * head_size - c0 : (head + 1) * head_size - c0,
                            : (block + 1) * rows,
                        ],
                        near_ref[head],
                        preferred_element_type=F32,
                    )
                    for head in heads
                ],
                axis=0,
            )
            total = (near + far[:, block * rows : (block + 1) * rows]).astype(BF16)
            out_ref[block * rows : (block + 1) * rows, c0 : c0 + step] = dot_last(
                unit, total
            ).astype(BF16)


def finish(values, states, where, last, token_pieces, sum_pieces, queries, level_weight, near, head_size):
    width, length = values.shape
    arrays = on_chip(*token_pieces, *sum_pieces, *last, values, states, queries, level_weight, *near)
    scratch = []
    if last:
        depth = last[0].shape[1]
        scratch = [pltpu.VMEM((length, depth), BF16), pltpu.VMEM((states.shape[1], depth), BF16)]
    return pl.pallas_call(
        functools.partial(finish_kernel, len(token_pieces), len(last), len(near), head_size),
        in_specs=[pl.BlockSpec(memory_space=pltpu.SMEM)]
        + [pl.BlockSpec(memory_space=pltpu.VMEM)] * len(arrays),
        out_shape=jax.ShapeDtypeStruct((length, width), BF16),
        scratch_shapes=scratch,
        compiler_params=pltpu.CompilerParams(vmem_limit_bytes=24 << 20),
        name="finish",
    )(where, *arrays)


def body(tokens, value_weight, queries, key_vectors, level_weight):
    _, width_feat = tokens.shape
    depth, width_local = value_weight.shape
    head_local = level_weight.shape[1]
    head_size = width_local // head_local
    ctx_count = lax.axis_size("ctx")
    dev_bits = ctx_count.bit_length() - 1
    my_index = lax.axis_index("ctx")
    my_head = lax.axis_index("head")
    near = prepare(queries, key_vectors, level_weight)

    running = jnp.einsum("tn,tf->nf", key_vectors, tokens, preferred_element_type=F32)
    level_sums = []
    for section_bit in range(dev_bits):
        partner = from_partner(running.astype(BF16), "ctx", section_bit)
        is_right = my_index // 2**section_bit % 2 == 1
        level_sums.append(jnp.where(is_right, partner, jnp.zeros_like(partner)))
        running = running + partner.astype(F32)
    level_sums = jnp.concatenate(level_sums, axis=0)

    if depth % 256 or width_feat % depth:
        features = lax.all_gather(tokens, "head", axis=1, tiled=True)
        sums = lax.all_gather(level_sums, "head", axis=1, tiled=True)
        weight = lax.all_gather(value_weight, "ctx", axis=0, tiled=True)
        values = jnp.einsum("fc,tf->ct", weight, features, preferred_element_type=F32)
        states = jnp.einsum("fc,nf->cn", weight, sums, preferred_element_type=F32)
        where = jnp.zeros((2,), jnp.int32)
        return finish(values, states, where, [], [], [], queries, level_weight, near, head_size)

    order = list(range(0, ctx_count, 2)) + list(range(1, ctx_count, 2))[::-1]
    ahead = [(order[i], order[(i + 1) % ctx_count]) for i in range(ctx_count)]
    back = [(b, a) for a, b in ahead]
    half_count = ctx_count // 2
    my_pos = jnp.where(my_index % 2 == 0, my_index // 2, ctx_count - 1 - my_index // 2)

    def place(offset):
        pos = (my_pos + offset) % ctx_count
        index = jnp.where(pos < half_count, 2 * pos, 2 * (ctx_count - 1 - pos) + 1)
        start = index * depth
        return start // width_feat ^ my_head, start % width_feat

    token_pieces = gather_pieces(tokens, "head")
    sum_pieces = gather_pieces(level_sums, "head")
    cw = ccw = value_weight.T
    steps = [[(place(0), cw)]]
    for step in range(1, half_count):
        cw = lax.ppermute(cw, "ctx", ahead)
        ccw = lax.ppermute(ccw, "ctx", back)
        steps.append([(place(-step), cw), (place(step), ccw)])
    half = width_local // 2
    cw = lax.ppermute(cw[:half], "ctx", ahead)
    ccw = lax.ppermute(ccw[half:], "ctx", back)
    last = [cw, ccw]
    values = extend(None, token_pieces, steps[0] + steps[1])
    for step in range(2, half_count):
        values = extend(values, token_pieces, steps[step])
    states = extend(None, sum_pieces, [part for parts in steps for part in parts])
    return finish(
        values,
        states,
        jnp.stack(place(half_count)),
        last,
        token_pieces,
        sum_pieces,
        queries,
        level_weight,
        near,
        head_size,
    )


def solution(mesh):
    return jax.shard_map(
        body,
        mesh=mesh,
        in_specs=(
            P("ctx", "head"),
            P("ctx", "head"),
            P("ctx", None),
            P("ctx", None),
            P(None, "head", "ctx"),
        ),
        out_specs=P("ctx", "head"),
        check_vma=False,
    )
```

profile of v0, /device:TPU:0, one launch (start us, length us, event | category | flops | bytes accessed | tf_op | source)
XLA Modules:
  0.0 81.5 jit_solution(350277841911971242)
XLA Ops:
  0.0 1.3 %copy.6 = bf16[256,1024]{0,1:T(8,128)(2,1)S(1)} copy(bf16[256,1024]{1,0:T(8,128)(2,1)} %param.6) | data formatting | bytes 1048576 | tf_op args[1]
  1.3 3.0 %collective-permute-start.13 = (bf16[1024,256]{1,0:T(8,128)(2,1)S(1)}, bf16[1024,256]{1,0:T(8,128)(2,1)S(1)}, u32[]{:S(2)}, u32[]{:S(2)}) collective-permute-start(bf16[1024,256]{1,0:T(8,128)(2,1)S(1)} %bitcast.19), channel_id=1, source_target_pairs={{8,0},{16,8},{24,16},{28,24},{20,28},{12,20},{4,12},{0,4},{9,1},{1... | collective-permute-start | bytes 1572872 | tf_op jit(solution)/shard_map/ppermute | solution.py:319
  4.4 1.4 %fusion.1 = (bf16[128,512]{1,0:T(8,128)(2,1)S(1)}, f32[128,512]{1,0:T(8,128)S(1)}) fusion(bf16[512,128]{1,0:T(8,128)(2,1)} %k_ref.1, bf16[512,512]{1,0:T(8,128)(2,1)} %refs_0_.7), kind=kOutput, calls=%fused_computation.10 | convolution fusion | flops 67174400 | bytes 1048576 | tf_op jit(solution)/shard_map/tn,tf->nf/dot_general | solution.py:283
  5.7 1.6 %collective-permute-start.3 = (bf16[128,512]{1,0:T(8,128)(2,1)S(1)}, bf16[128,512]{1,0:T(8,128)(2,1)S(1)}, u32[]{:S(2)}, u32[]{:S(2)}) collective-permute-start(bf16[128,512]{1,0:T(8,128)(2,1)S(1)} %get-tuple-element.9), channel_id=1, source_target_pairs={{0,4},{4,0},{8,12},{12,8},{16,20},{20,16},{24,28},{28,24},{1,5},{5... | collective-permute-start | bytes 393224 | tf_op jit(solution)/shard_map/ppermute | solution.py:22
  7.4 1.6 %collective-permute-start.9 = (bf16[1024,256]{1,0:T(8,128)(2,1)S(1)}, bf16[1024,256]{1,0:T(8,128)(2,1)}, u32[]{:S(2)}, u32[]{:S(2)}) collective-permute-start(bf16[1024,256]{1,0:T(8,128)(2,1)S(1)} %bitcast.20), channel_id=1, source_target_pairs={{0,8},{8,16},{16,24},{24,28},{28,20},{20,12},{12,4},{4,0},{1,9},{9... | collective-permute-start | bytes 1572872 | tf_op jit(solution)/shard_map/ppermute | solution.py:318
  9.0 1.5 %collective-permute-start.1 = (bf16[512,512]{1,0:T(8,128)(2,1)S(1)}, bf16[512,512]{1,0:T(8,128)(2,1)S(1)}, u32[]{:S(2)}, u32[]{:S(2)}) collective-permute-start(bf16[512,512]{1,0:T(8,128)(2,1)S(1)} %copy-done), channel_id=1, source_target_pairs={{0,2},{2,0},{1,3},{3,1},{4,6},{6,4},{5,7},{7,5},{8,10},{10,8},{9,1... | collective-permute-start | bytes 1572872 | tf_op jit(solution)/shard_map/ppermute | solution.py:22
  10.4 0.0 collective-permute-start
  10.4 7.9 %collective-permute-done.3 = bf16[128,512]{1,0:T(8,128)(2,1)S(1)} collective-permute-done((bf16[128,512]{1,0:T(8,128)(2,1)S(1)}, bf16[128,512]{1,0:T(8,128)(2,1)S(1)}, u32[]{:S(2)}, u32[]{:S(2)}) %collective-permute-start.3) | collective-permute-done | bytes 131104 | tf_op jit(solution)/shard_map/ppermute | solution.py:22
  18.4 0.1 collective-permute-start.4
  18.5 2.5 %collective-permute-start.14 = (bf16[1024,256]{1,0:T(8,128)(2,1)S(1)}, bf16[1024,256]{1,0:T(8,128)(2,1)S(1)}, u32[]{:S(2)}, u32[]{:S(2)}) collective-permute-start(bf16[1024,256]{1,0:T(8,128)(2,1)S(1)} %collective-permute-done.13.refs_6_), channel_id=1, source_target_pairs={{8,0},{16,8},{24,16},{28,24},{20,28},{12,20},{4,12},{0,4},{9,1},{1... | collective-permute-start | bytes 1572872 | tf_op jit(solution)/shard_map/ppermute | solution.py:319
  21.0 1.1 %collective-permute-done.9.refs_5_ = bf16[1024,256]{1,0:T(8,128)(2,1)} collective-permute-done((bf16[1024,256]{1,0:T(8,128)(2,1)S(1)}, bf16[1024,256]{1,0:T(8,128)(2,1)}, u32[]{:S(2)}, u32[]{:S(2)}) %collective-permute-start.9) | collective-permute-done | bytes 524320 | tf_op jit(solution)/shard_map/ppermute | solution.py:318
  22.1 1.5 %collective-permute-start.10 = (bf16[1024,256]{1,0:T(8,128)(2,1)}, bf16[1024,256]{1,0:T(8,128)(2,1)}, u32[]{:S(2)}, u32[]{:S(2)}) collective-permute-start(bf16[1024,256]{1,0:T(8,128)(2,1)} %collective-permute-done.9.refs_5_), channel_id=1, source_target_pairs={{0,8},{8,16},{16,24},{24,28},{28,20},{20,12},{12,4},{4,0},{1,9},{9... | collective-permute-start | bytes 1572872 | tf_op jit(solution)/shard_map/ppermute | solution.py:318
  23.6 1.2 %collective-permute-done.4 = bf16[128,512]{1,0:T(8,128)(2,1)S(1)} collective-permute-done((bf16[128,512]{1,0:T(8,128)(2,1)S(1)}, bf16[128,512]{1,0:T(8,128)(2,1)S(1)}, u32[]{:S(2)}, u32[]{:S(2)}) %collective-permute-start.4) | collective-permute-done | bytes 131104 | tf_op jit(solution)/shard_map/ppermute | solution.py:22
  24.9 3.2 %collective-permute-start.5 = (bf16[128,512]{1,0:T(8,128)(2,1)S(1)}, bf16[128,512]{1,0:T(8,128)(2,1)S(1)}, u32[]{:S(2)}, u32[]{:S(2)}) collective-permute-start(bf16[128,512]{1,0:T(8,128)(2,1)S(1)} %add_convert_fusion), channel_id=1, source_target_pairs={{0,16},{16,0},{4,20},{20,4},{8,24},{24,8},{12,28},{28,12},{1,17},{... | collective-permute-start | bytes 393224 | tf_op jit(solution)/shard_map/ppermute | solution.py:22
  28.1 7.7 %collective-permute-done.14.refs_5_.refs_8_ = bf16[1024,256]{1,0:T(8,128)(2,1)S(1)} collective-permute-done((bf16[1024,256]{1,0:T(8,128)(2,1)S(1)}, bf16[1024,256]{1,0:T(8,128)(2,1)S(1)}, u32[]{:S(2)}, u32[]{:S(2)}) %collective-permute-start.14) | collective-permute-done | bytes 524320 | tf_op jit(solution)/shard_map/ppermute | solution.py:319
  35.8 0.3 collective-permute-start.15
  36.1 4.6 %collective-permute-done.5 = bf16[128,512]{1,0:T(8,128)(2,1)S(1)} collective-permute-done((bf16[128,512]{1,0:T(8,128)(2,1)S(1)}, bf16[128,512]{1,0:T(8,128)(2,1)S(1)}, u32[]{:S(2)}, u32[]{:S(2)}) %collective-permute-start.5) | collective-permute-done | bytes 131104 | tf_op jit(solution)/shard_map/ppermute | solution.py:22
  40.7 1.3 %collective-permute-start.11 = (bf16[1024,256]{1,0:T(8,128)(2,1)}, bf16[1024,256]{1,0:T(8,128)(2,1)}, u32[]{:S(2)}, u32[]{:S(2)}) collective-permute-start(bf16[1024,256]{1,0:T(8,128)(2,1)} %collective-permute-done.10.refs_4_.refs_7_), channel_id=1, source_target_pairs={{0,8},{8,16},{16,24},{24,28},{28,20},{20,12},{12,4},{4,0},{1,9},{9... | collective-permute-start | bytes 1572872 | tf_op jit(solution)/shard_map/ppermute | solution.py:318
  42.1 1.6 %collective-permute-start.7 = (bf16[384,512]{1,0:T(8,128)(2,1)S(1)}, bf16[384,512]{1,0:T(8,128)(2,1)}, u32[]{:S(2)}, u32[]{:S(2)}) collective-permute-start(bf16[384,512]{1,0:T(8,128)(2,1)S(1)} %pad_maximum_fusion.refs_0_.refs_4_), channel_id=1, source_target_pairs={{0,2},{2,0},{1,3},{3,1},{4,6},{6,4},{5,7},{7,5},{8,10},{10,8},{9,1... | collective-permute-start | bytes 1179656 | tf_op jit(solution)/shard_map/ppermute | solution.py:22
  43.6 0.0 collective-permute-done.1.refs_2_
  43.6 0.0 collective-permute-start.2
  43.6 6.4 %collective-permute-done.7.refs_2_.refs_6_ = bf16[384,512]{1,0:T(8,128)(2,1)} collective-permute-done((bf16[384,512]{1,0:T(8,128)(2,1)S(1)}, bf16[384,512]{1,0:T(8,128)(2,1)}, u32[]{:S(2)}, u32[]{:S(2)}) %collective-permute-start.7) | collective-permute-done | bytes 393248 | tf_op jit(solution)/shard_map/ppermute | solution.py:22
  50.0 0.0 collective-permute-start.6
  50.0 0.5 collective-permute-start.8
  50.5 0.7 slice.9
  51.3 1.2 %collective-permute-start.16 = (bf16[512,256]{1,0:T(8,128)(2,1)}, bf16[512,256]{1,0:T(8,128)(2,1)}, u32[]{:S(2)}, u32[]{:S(2)}) collective-permute-start(bf16[512,256]{1,0:T(8,128)(2,1)} %slice.9), channel_id=1, source_target_pairs={{8,0},{16,8},{24,16},{28,24},{20,28},{12,20},{4,12},{0,4},{9,1},{1... | collective-permute-start | bytes 786440 | tf_op jit(solution)/shard_map/ppermute | solution.py:323
  52.4 1.7 %slice.8 = bf16[512,256]{1,0:T(8,128)(2,1)} slice(bf16[1024,256]{1,0:T(8,128)(2,1)} %collective-permute-done.11.refs_4_.refs_9_), slice={[0:512], [0:256]} | slice | bytes 524288 | tf_op jit(solution)/shard_map/slice | solution.py:322
  54.1 0.9 %collective-permute-start.12 = (bf16[512,256]{1,0:T(8,128)(2,1)}, bf16[512,256]{1,0:T(8,128)(2,1)}, u32[]{:S(2)}, u32[]{:S(2)}) collective-permute-start(bf16[512,256]{1,0:T(8,128)(2,1)} %slice.8), channel_id=1, source_target_pairs={{0,8},{8,16},{16,24},{24,28},{28,20},{20,12},{12,4},{4,0},{1,9},{9... | collective-permute-start | bytes 786440 | tf_op jit(solution)/shard_map/ppermute | solution.py:322
  55.0 0.1 pad_add_fusion.1.where_ref
  55.3 0.0 copy-start.10
  55.3 1.0 %copy-done.10 = f32[13,16,512]{2,1,0:T(8,128)S(1)} copy-done((f32[13,16,512]{2,1,0:T(8,128)S(1)}, f32[13,16,512]{2,1,0:T(8,128)}, u32[]{:S(2)}) %copy-start.10) | copy-done | bytes 426008
  56.3 0.9 %copy-done.12 = bf16[512,128]{1,0:T(8,128)(2,1)S(1)} copy-done((bf16[512,128]{1,0:T(8,128)(2,1)S(1)}, bf16[512,128]{1,0:T(8,128)(2,1)}, u32[]{:S(2)}) %copy-start.12) | copy-done | bytes 131096
  57.2 0.9 %copy-done.14 = bf16[512,128]{1,0:T(8,128)(2,1)S(1)} copy-done((bf16[512,128]{1,0:T(8,128)(2,1)S(1)}, bf16[512,128]{1,0:T(8,128)(2,1)}, u32[]{:S(2)}) %copy-start.14) | copy-done | bytes 131096
  58.1 1.9 %prepare.1 = (bf16[16,256,256]{2,1,0:T(8,128)(2,1)S(1)}, bf16[16,512,256]{2,1,0:T(8,128)(2,1)S(1)}) custom-call(bf16[512,128]{1,0:T(8,128)(2,1)S(1)} %copy-done.12, bf16[512,128]{1,0:T(8,128)(2,1)S(1)} %copy-done.14, f32[13,16,512]{2,1,0:T(8,128)S(1)} %copy-done.10), custom_call_target="tpu_custom_call" | custom-call | tf_op jit(solution)/shard_map/prepare/pallas_call | solution.py:127
  60.0 1.9 %copy-done.1 = bf16[16,512,256]{2,1,0:T(8,128)(2,1)} copy-done((bf16[16,512,256]{2,1,0:T(8,128)(2,1)}, bf16[16,512,256]{2,1,0:T(8,128)(2,1)S(1)}, u32[]{:S(2)}) %copy-start.1) | copy-done | bytes 4194328
  62.0 1.4 %copy-done.3 = bf16[16,256,256]{2,1,0:T(8,128)(2,1)} copy-done((bf16[16,256,256]{2,1,0:T(8,128)(2,1)}, bf16[16,256,256]{2,1,0:T(8,128)(2,1)S(1)}, u32[]{:S(2)}) %copy-start.3) | copy-done | bytes 2097176
  63.4 0.1 stack.96.where_ref
  63.5 0.1 stack.97.where_ref
  63.5 0.1 pad_add_fusion.2.where_ref
  63.6 0.1 pad_add_fusion.where_ref
  63.7 1.0 %copy-done.6 = bf16[1024,256]{1,0:T(8,128)(2,1)S(1)} copy-done((bf16[1024,256]{1,0:T(8,128)(2,1)S(1)}, bf16[1024,256]{1,0:T(8,128)(2,1)}, u32[]{:S(2)}) %copy-start.6) | copy-done | bytes 524312
  64.8 2.2 %shard_map.55.refs_6_ = f32[1024,512]{1,0:T(8,128)S(1)} custom-call(s32[6]{0:T(128)S(1)} %stack.96.where_ref, bf16[512,512]{1,0:T(8,128)(2,1)S(1)} %copy-done, bf16[512,512]{1,0:T(8,128)(2,1)S(1)} %collective-permute-done.refs_1_, bf16[512,512]{1,0:T(8,128)(2,1)S(1)} %collective-permute-done.1.refs_2_, bf16[512,512]{1,0:T(8,128)(2,1)S(1)} %collective-permute-done.2.refs_3_, ...), custom_call_target="tpu_custom_call" | custom-call | tf_op jit(solution)/shard_map/pallas_call | solution.py:174
  67.0 1.9 %shard_map.56.refs_6_ = f32[1024,512]{1,0:T(8,128)S(1)} custom-call(s32[4]{0:T(128)S(1)} %pad_add_fusion.2.where_ref, bf16[512,512]{1,0:T(8,128)(2,1)S(1)} %copy-done, bf16[512,512]{1,0:T(8,128)(2,1)S(1)} %collective-permute-done.refs_1_, bf16[512,512]{1,0:T(8,128)(2,1)S(1)} %collective-permute-done.1.refs_2_, ...), custom_call_target="tpu_custom_call" | custom-call | tf_op jit(solution)/shard_map/pallas_call | solution.py:174
  68.9 0.0 copy-start.13
  68.9 1.9 %shard_map.57.refs_10_ = f32[1024,512]{1,0:T(8,128)S(1)} custom-call(s32[4]{0:T(128)S(1)} %pad_add_fusion.1.where_ref, bf16[512,512]{1,0:T(8,128)(2,1)S(1)} %copy-done, bf16[512,512]{1,0:T(8,128)(2,1)S(1)} %collective-permute-done.refs_1_, bf16[512,512]{1,0:T(8,128)(2,1)S(1)} %collective-permute-done.1.refs_2_, ...), custom_call_target="tpu_custom_call" | custom-call | tf_op jit(solution)/shard_map/pallas_call | solution.py:174
  70.9 0.0 copy-start.11
  70.9 4.2 %shard_map.58.refs_11_ = f32[1024,384]{1,0:T(8,128)S(1)} custom-call(s32[14]{0:T(128)S(1)} %stack.97.where_ref, bf16[384,512]{1,0:T(8,128)(2,1)S(1)} %pad_maximum_fusion.refs_0_.refs_4_, bf16[384,512]{1,0:T(8,128)(2,1)} %collective-permute-done.6.refs_1_.refs_5_, bf16[384,512]{1,0:T(8,128)(2,1)} %collective-permute-done.7.refs_2_.refs_6_, ...), custom_call_target="tpu_custom_call" | custom-call | tf_op jit(solution)/shard_map/pallas_call | solution.py:174
  75.2 6.3 %finish.1 = bf16[512,1024]{1,0:T(8,128)(2,1)} custom-call(s32[2]{0:T(128)S(1)} %pad_add_fusion.where_ref, bf16[512,512]{1,0:T(8,128)(2,1)S(1)} %copy-done, bf16[512,512]{1,0:T(8,128)(2,1)S(1)} %collective-permute-done.refs_1_, bf16[512,512]{1,0:T(8,128)(2,1)S(1)} %collective-permute-done.1.refs_2_, bf16[512,512]{1,0:T(8,128)(2,1)S(1)} %collective-permute-done.2.refs_3_, ...), custom_call_target="tpu_custom_call" | custom-call | tf_op jit(solution)/shard_map/finish/pallas_call | solution.py:261
  (37 shorter events, 0.2 us)
Async XLA Ops:
  0.0 8.9 %copy-start = (bf16[512,512]{1,0:T(8,128)(2,1)S(1)}, bf16[512,512]{1,0:T(8,128)(2,1)}, u32[]{:S(2)}) copy-start(bf16[512,512]{1,0:T(8,128)(2,1)} %refs_0_.7) | copy-start | bytes 1572868
  1.3 17.2 %collective-permute-start.13 = (bf16[1024,256]{1,0:T(8,128)(2,1)S(1)}, bf16[1024,256]{1,0:T(8,128)(2,1)S(1)}, u32[]{:S(2)}, u32[]{:S(2)}) collective-permute-start(bf16[1024,256]{1,0:T(8,128)(2,1)S(1)} %bitcast.19), channel_id=1, source_target_pairs={{8,0},{16,8},{24,16},{28,24},{20,28},{12,20},{4,12},{0,4},{9,1},{1... | collective-permute-start | bytes 1572872 | tf_op jit(solution)/shard_map/ppermute | solution.py:319
  5.7 12.6 %collective-permute-start.3 = (bf16[128,512]{1,0:T(8,128)(2,1)S(1)}, bf16[128,512]{1,0:T(8,128)(2,1)S(1)}, u32[]{:S(2)}, u32[]{:S(2)}) collective-permute-start(bf16[128,512]{1,0:T(8,128)(2,1)S(1)} %get-tuple-element.9), channel_id=1, source_target_pairs={{0,4},{4,0},{8,12},{12,8},{16,20},{20,16},{24,28},{28,24},{1,5},{5... | collective-permute-start | bytes 393224 | tf_op jit(solution)/shard_map/ppermute | solution.py:22
  7.4 14.7 %collective-permute-start.9 = (bf16[1024,256]{1,0:T(8,128)(2,1)S(1)}, bf16[1024,256]{1,0:T(8,128)(2,1)}, u32[]{:S(2)}, u32[]{:S(2)}) collective-permute-start(bf16[1024,256]{1,0:T(8,128)(2,1)S(1)} %bitcast.20), channel_id=1, source_target_pairs={{0,8},{8,16},{16,24},{24,28},{28,20},{20,12},{12,4},{4,0},{1,9},{9... | collective-permute-start | bytes 1572872 | tf_op jit(solution)/shard_map/ppermute | solution.py:318
  9.0 34.7 %collective-permute-start.1 = (bf16[512,512]{1,0:T(8,128)(2,1)S(1)}, bf16[512,512]{1,0:T(8,128)(2,1)S(1)}, u32[]{:S(2)}, u32[]{:S(2)}) collective-permute-start(bf16[512,512]{1,0:T(8,128)(2,1)S(1)} %copy-done), channel_id=1, source_target_pairs={{0,2},{2,0},{1,3},{3,1},{4,6},{6,4},{5,7},{7,5},{8,10},{10,8},{9,1... | collective-permute-start | bytes 1572872 | tf_op jit(solution)/shard_map/ppermute | solution.py:22
  10.4 43.7 %collective-permute-start = (bf16[512,512]{1,0:T(8,128)(2,1)S(1)}, bf16[512,512]{1,0:T(8,128)(2,1)S(1)}, u32[]{:S(2)}, u32[]{:S(2)}) collective-permute-start(bf16[512,512]{1,0:T(8,128)(2,1)S(1)} %copy-done), channel_id=1, source_target_pairs={{0,1},{1,0},{2,3},{3,2},{4,5},{5,4},{6,7},{7,6},{8,9},{9,8},{10,11... | collective-permute-start | bytes 1572872 | tf_op jit(solution)/shard_map/ppermute | solution.py:22
  18.4 6.4 %collective-permute-start.4 = (bf16[128,512]{1,0:T(8,128)(2,1)S(1)}, bf16[128,512]{1,0:T(8,128)(2,1)S(1)}, u32[]{:S(2)}, u32[]{:S(2)}) collective-permute-start(bf16[128,512]{1,0:T(8,128)(2,1)S(1)} %fusion), channel_id=1, source_target_pairs={{0,8},{8,0},{4,12},{12,4},{16,24},{24,16},{20,28},{28,20},{1,9},{9... | collective-permute-start | bytes 393224 | tf_op jit(solution)/shard_map/ppermute | solution.py:22
  18.5 25.2 %copy-start.5 = (bf16[1024,256]{1,0:T(8,128)(2,1)}, bf16[1024,256]{1,0:T(8,128)(2,1)S(1)}, u32[]{:S(2)}) copy-start(bf16[1024,256]{1,0:T(8,128)(2,1)S(1)} %collective-permute-done.13.refs_6_) | copy-start | bytes 1572868
  18.5 17.3 %collective-permute-start.14 = (bf16[1024,256]{1,0:T(8,128)(2,1)S(1)}, bf16[1024,256]{1,0:T(8,128)(2,1)S(1)}, u32[]{:S(2)}, u32[]{:S(2)}) collective-permute-start(bf16[1024,256]{1,0:T(8,128)(2,1)S(1)} %collective-permute-done.13.refs_6_), channel_id=1, source_target_pairs={{8,0},{16,8},{24,16},{28,24},{20,28},{12,20},{4,12},{0,4},{9,1},{1... | collective-permute-start | bytes 1572872 | tf_op jit(solution)/shard_map/ppermute | solution.py:319
  22.1 18.6 %collective-permute-start.10 = (bf16[1024,256]{1,0:T(8,128)(2,1)}, bf16[1024,256]{1,0:T(8,128)(2,1)}, u32[]{:S(2)}, u32[]{:S(2)}) collective-permute-start(bf16[1024,256]{1,0:T(8,128)(2,1)} %collective-permute-done.9.refs_5_), channel_id=1, source_target_pairs={{0,8},{8,16},{16,24},{24,28},{28,20},{20,12},{12,4},{4,0},{1,9},{9... | collective-permute-start | bytes 1572872 | tf_op jit(solution)/shard_map/ppermute | solution.py:318
  24.9 15.8 %collective-permute-start.5 = (bf16[128,512]{1,0:T(8,128)(2,1)S(1)}, bf16[128,512]{1,0:T(8,128)(2,1)S(1)}, u32[]{:S(2)}, u32[]{:S(2)}) collective-permute-start(bf16[128,512]{1,0:T(8,128)(2,1)S(1)} %add_convert_fusion), channel_id=1, source_target_pairs={{0,16},{16,0},{4,20},{20,4},{8,24},{24,8},{12,28},{28,12},{1,17},{... | collective-permute-start | bytes 393224 | tf_op jit(solution)/shard_map/ppermute | solution.py:22
  35.8 14.2 %copy-start.8 = (bf16[1024,256]{1,0:T(8,128)(2,1)}, bf16[1024,256]{1,0:T(8,128)(2,1)S(1)}, u32[]{:S(2)}) copy-start(bf16[1024,256]{1,0:T(8,128)(2,1)S(1)} %collective-permute-done.14.refs_5_.refs_8_) | copy-start | bytes 1572868
  35.8 14.2 %collective-permute-start.15 = (bf16[1024,256]{1,0:T(8,128)(2,1)S(1)}, bf16[1024,256]{1,0:T(8,128)(2,1)S(1)}, u32[]{:S(2)}, u32[]{:S(2)}) collective-permute-start(bf16[1024,256]{1,0:T(8,128)(2,1)S(1)} %collective-permute-done.14.refs_5_.refs_8_), channel_id=1, source_target_pairs={{8,0},{16,8},{24,16},{28,24},{20,28},{12,20},{4,12},{0,4},{9,1},{1... | collective-permute-start | bytes 1572872 | tf_op jit(solution)/shard_map/ppermute | solution.py:319
  40.7 10.6 %collective-permute-start.11 = (bf16[1024,256]{1,0:T(8,128)(2,1)}, bf16[1024,256]{1,0:T(8,128)(2,1)}, u32[]{:S(2)}, u32[]{:S(2)}) collective-permute-start(bf16[1024,256]{1,0:T(8,128)(2,1)} %collective-permute-done.10.refs_4_.refs_7_), channel_id=1, source_target_pairs={{0,8},{8,16},{16,24},{24,28},{28,20},{20,12},{12,4},{4,0},{1,9},{9... | collective-permute-start | bytes 1572872 | tf_op jit(solution)/shard_map/ppermute | solution.py:318
  42.1 7.9 %collective-permute-start.7 = (bf16[384,512]{1,0:T(8,128)(2,1)S(1)}, bf16[384,512]{1,0:T(8,128)(2,1)}, u32[]{:S(2)}, u32[]{:S(2)}) collective-permute-start(bf16[384,512]{1,0:T(8,128)(2,1)S(1)} %pad_maximum_fusion.refs_0_.refs_4_), channel_id=1, source_target_pairs={{0,2},{2,0},{1,3},{3,1},{4,6},{6,4},{5,7},{7,5},{8,10},{10,8},{9,1... | collective-permute-start | bytes 1179656 | tf_op jit(solution)/shard_map/ppermute | solution.py:22
  43.6 20.1 %collective-permute-start.2 = (bf16[512,512]{1,0:T(8,128)(2,1)S(1)}, bf16[512,512]{1,0:T(8,128)(2,1)S(1)}, u32[]{:S(2)}, u32[]{:S(2)}) collective-permute-start(bf16[512,512]{1,0:T(8,128)(2,1)S(1)} %collective-permute-done.1.refs_2_), channel_id=1, source_target_pairs={{0,1},{1,0},{2,3},{3,2},{4,5},{5,4},{6,7},{7,6},{8,9},{9,8},{10,11... | collective-permute-start | bytes 1572872 | tf_op jit(solution)/shard_map/ppermute | solution.py:22
  50.0 20.9 %collective-permute-start.6 = (bf16[384,512]{1,0:T(8,128)(2,1)S(1)}, bf16[384,512]{1,0:T(8,128)(2,1)}, u32[]{:S(2)}, u32[]{:S(2)}) collective-permute-start(bf16[384,512]{1,0:T(8,128)(2,1)S(1)} %pad_maximum_fusion.refs_0_.refs_4_), channel_id=1, source_target_pairs={{0,1},{1,0},{2,3},{3,2},{4,5},{5,4},{6,7},{7,6},{8,9},{9,8},{10,11... | collective-permute-start | bytes 1179656 | tf_op jit(solution)/shard_map/ppermute | solution.py:22
  50.0 20.9 %collective-permute-start.8 = (bf16[384,512]{1,0:T(8,128)(2,1)}, bf16[384,512]{1,0:T(8,128)(2,1)}, u32[]{:S(2)}, u32[]{:S(2)}) collective-permute-start(bf16[384,512]{1,0:T(8,128)(2,1)} %collective-permute-done.7.refs_2_.refs_6_), channel_id=1, source_target_pairs={{0,1},{1,0},{2,3},{3,2},{4,5},{5,4},{6,7},{7,6},{8,9},{9,8},{10,11... | collective-permute-start | bytes 1179656 | tf_op jit(solution)/shard_map/ppermute | solution.py:22
  51.3 23.8 %collective-permute-start.16 = (bf16[512,256]{1,0:T(8,128)(2,1)}, bf16[512,256]{1,0:T(8,128)(2,1)}, u32[]{:S(2)}, u32[]{:S(2)}) collective-permute-start(bf16[512,256]{1,0:T(8,128)(2,1)} %slice.9), channel_id=1, source_target_pairs={{8,0},{16,8},{24,16},{28,24},{20,28},{12,20},{4,12},{0,4},{9,1},{1... | collective-permute-start | bytes 786440 | tf_op jit(solution)/shard_map/ppermute | solution.py:323
  54.1 21.0 %collective-permute-start.12 = (bf16[512,256]{1,0:T(8,128)(2,1)}, bf16[512,256]{1,0:T(8,128)(2,1)}, u32[]{:S(2)}, u32[]{:S(2)}) collective-permute-start(bf16[512,256]{1,0:T(8,128)(2,1)} %slice.8), channel_id=1, source_target_pairs={{0,8},{8,16},{16,24},{24,28},{28,20},{20,12},{12,4},{4,0},{1,9},{9... | collective-permute-start | bytes 786440 | tf_op jit(solution)/shard_map/ppermute | solution.py:322
  55.3 1.0 %copy-start.10 = (f32[13,16,512]{2,1,0:T(8,128)S(1)}, f32[13,16,512]{2,1,0:T(8,128)}, u32[]{:S(2)}) copy-start(f32[13,16,512]{2,1,0:T(8,128)} %refs_13_.1) | copy-start | bytes 1277956
  56.3 0.9 %copy-start.12 = (bf16[512,128]{1,0:T(8,128)(2,1)S(1)}, bf16[512,128]{1,0:T(8,128)(2,1)}, u32[]{:S(2)}) copy-start(bf16[512,128]{1,0:T(8,128)(2,1)} %refs_12_.1) | copy-start | bytes 393220
  57.2 0.9 %copy-start.14 = (bf16[512,128]{1,0:T(8,128)(2,1)S(1)}, bf16[512,128]{1,0:T(8,128)(2,1)}, u32[]{:S(2)}) copy-start(bf16[512,128]{1,0:T(8,128)(2,1)} %k_ref.1) | copy-start | bytes 393220
  60.0 2.0 %copy-start.1 = (bf16[16,512,256]{2,1,0:T(8,128)(2,1)}, bf16[16,512,256]{2,1,0:T(8,128)(2,1)S(1)}, u32[]{:S(2)}) copy-start(bf16[16,512,256]{2,1,0:T(8,128)(2,1)S(1)} %get-tuple-element.8.refs_15_) | copy-start | bytes 12582916
  62.0 1.4 %copy-start.3 = (bf16[16,256,256]{2,1,0:T(8,128)(2,1)}, bf16[16,256,256]{2,1,0:T(8,128)(2,1)S(1)}, u32[]{:S(2)}) copy-start(bf16[16,256,256]{2,1,0:T(8,128)(2,1)S(1)} %get-tuple-element.7.refs_14_) | copy-start | bytes 6291460
  63.7 1.0 %copy-start.6 = (bf16[1024,256]{1,0:T(8,128)(2,1)S(1)}, bf16[1024,256]{1,0:T(8,128)(2,1)}, u32[]{:S(2)}) copy-start(bf16[1024,256]{1,0:T(8,128)(2,1)} %copy-done.5) | copy-start | bytes 1572868
  64.8 2.2 %copy-start.9 = (bf16[1024,256]{1,0:T(8,128)(2,1)S(1)}, bf16[1024,256]{1,0:T(8,128)(2,1)}, u32[]{:S(2)}) copy-start(bf16[1024,256]{1,0:T(8,128)(2,1)} %copy-done.8) | copy-start | bytes 1572868
  68.9 2.0 %copy-start.7 = (bf16[1024,256]{1,0:T(8,128)(2,1)S(1)}, bf16[1024,256]{1,0:T(8,128)(2,1)}, u32[]{:S(2)}) copy-start(bf16[1024,256]{1,0:T(8,128)(2,1)} %copy-done.5) | copy-start | bytes 1572868
  68.9 6.2 %copy-start.13 = (bf16[512,128]{1,0:T(8,128)(2,1)S(1)}, bf16[512,128]{1,0:T(8,128)(2,1)}, u32[]{:S(2)}) copy-start(bf16[512,128]{1,0:T(8,128)(2,1)} %refs_12_.1) | copy-start | bytes 393220
  70.9 4.3 %copy-start.2 = (bf16[16,512,256]{2,1,0:T(8,128)(2,1)S(1)}, bf16[16,512,256]{2,1,0:T(8,128)(2,1)}, u32[]{:S(2)}) copy-start(bf16[16,512,256]{2,1,0:T(8,128)(2,1)} %copy-done.1) | copy-start | bytes 12582916
  70.9 4.3 %copy-start.4 = (bf16[16,256,256]{2,1,0:T(8,128)(2,1)S(1)}, bf16[16,256,256]{2,1,0:T(8,128)(2,1)}, u32[]{:S(2)}) copy-start(bf16[16,256,256]{2,1,0:T(8,128)(2,1)} %copy-done.3) | copy-start | bytes 6291460
  70.9 4.3 %copy-start.11 = (f32[13,16,512]{2,1,0:T(8,128)S(1)}, f32[13,16,512]{2,1,0:T(8,128)}, u32[]{:S(2)}) copy-start(f32[13,16,512]{2,1,0:T(8,128)} %refs_13_.1) | copy-start | bytes 1277956
where the time goes:
time: 81.9 us; the launch traced here: 81.5 us
  waiting for transfers between devices  29 us (35%)
  starting transfers between devices  20.7 us (25%)
  Pallas kernels  18.4 us (22%)
  local copies, waits for them, and re-layouts  11.1 us (14%)
  matrix products  1.37 us (2%)
    ppermute x9, waiting for transfers between devices, from_partner(): return lax.ppermute(block, axis, route)  20.2 us
    pallas_call x4, Pallas kernels, extend(): pl.pallas_call(functools.partial(extend_kernel, len(pieces), len(blocks),...  10.2 us
    unnamed x31, local copies, waits for them, and re-layouts  8.53 us
    ppermute x9, starting transfers between devices, from_partner(): return lax.ppermute(block, axis, route)  8.45 us
    ppermute x3, waiting for transfers between devices, body(): ccw = lax.ppermute(ccw, 'ctx', back)  7.74 us
    pallas_call x1, Pallas kernels, finish(): pl.pallas_call(functools.partial(finish_kernel, len(token_pieces), len(la...  6.29 us
    ppermute x3, starting transfers between devices, body(): ccw = lax.ppermute(ccw, 'ctx', back)  5.84 us
    ppermute x3, starting transfers between devices, body(): cw = lax.ppermute(cw, 'ctx', ahead)  4.39 us
  transfers between devices with their start and end apart: 17, of which 6 were waited for; matrix products, arithmetic and copies ran while one was open for 5% of the time, Pallas kernels for 15%

commit v1 on v0

--- a/solution.py
+++ b/solution.py
@@ -149,34 +149,38 @@
                 chosen_ref[:, num * depth : (num + 1) * depth] = ref[:, pl.ds(start, depth)]
 
 
-def extend_kernel(piece_count, count, started, where_ref, *refs):
+def extend_kernel(piece_count, count, split, started, where_ref, *refs):
     pieces = refs[:piece_count]
-    blocks = refs[piece_count : piece_count + count]
+    blocks = [refs[piece_count + num * split :][:split] for num in range(count)]
     out_ref, chosen_ref = refs[-2], refs[-1]
-    depth = blocks[0].shape[1]
+    share, depth = blocks[0][0].shape
     choose(where_ref, pieces, depth, chosen_ref, 0, count)
     width = out_ref.shape[0]
-    step = min(256, width)
+    step = min(256, share)
     for c0 in range(0, width, step):
-        left = jnp.concatenate([block[c0 : c0 + step, :] for block in blocks], axis=1)
+        at = c0 % share
+        left = jnp.concatenate(
+            [block[c0 // share][at : at + step, :] for block in blocks], axis=1
+        )
         total = dot_last(left, chosen_ref[...])
         if started:
-            total = total + refs[piece_count + count][c0 : c0 + step, :]
+            total = total + refs[piece_count + count * split][c0 : c0 + step, :]
         out_ref[c0 : c0 + step, :] = total
 
 
 def extend(total, pieces, parts):
     where = jnp.stack([num for pair, _ in parts for num in pair])
-    blocks = [block for _, block in parts]
+    blocks = [half for _, block in parts for half in block]
+    split = len(parts[0][1])
     rows = pieces[0].shape[0]
-    width, depth = blocks[0].shape
-    arrays = on_chip(*pieces, *blocks, *([] if total is None else [total]))
+    share, depth = blocks[0].shape
+    arrays = [*pieces, *blocks, *([] if total is None else [total])]
     return pl.pallas_call(
-        functools.partial(extend_kernel, len(pieces), len(blocks), total is not None),
+        functools.partial(extend_kernel, len(pieces), len(parts), split, total is not None),
         in_specs=[pl.BlockSpec(memory_space=pltpu.SMEM)]
         + [pl.BlockSpec(memory_space=pltpu.VMEM)] * len(arrays),
-        out_shape=pltpu.VMEM((width, rows), F32),
-        scratch_shapes=[pltpu.VMEM((rows, depth * len(blocks)), BF16)],
+        out_shape=pltpu.VMEM((share * split, rows), F32),
+        scratch_shapes=[pltpu.VMEM((rows, depth * len(parts)), BF16)],
         compiler_params=pltpu.CompilerParams(vmem_limit_bytes=12 << 20),
     )(where, *arrays)
 
@@ -253,7 +257,7 @@
 
 def finish(values, states, where, last, token_pieces, sum_pieces, queries, level_weight, near, head_size):
     width, length = values.shape
-    arrays = on_chip(*token_pieces, *sum_pieces, *last, values, states, queries, level_weight, *near)
+    arrays = [*token_pieces, *sum_pieces, *last, values, states, queries, level_weight, *near]
     scratch = []
     if last:
         depth = last[0].shape[1]
@@ -310,18 +314,21 @@
         start = index * depth
         return start // width_feat ^ my_head, start % width_feat
 
-    token_pieces = gather_pieces(tokens, "head")
-    sum_pieces = gather_pieces(level_sums, "head")
-    cw = ccw = value_weight.T
-    steps = [[(place(0), cw)]]
+    token_pieces = on_chip(*gather_pieces(tokens, "head"))
+    sum_pieces = on_chip(*gather_pieces(level_sums, "head"))
+    half = width_local // 2
+    first = value_weight.T
+    cw = ccw = (first[:half], first[half:])
+    steps = [[(place(0), on_chip(*cw))]]
+
+    def move(part, route):
+        return lax.ppermute(part, "ctx", route)
+
     for step in range(1, half_count):
-        cw = lax.ppermute(cw, "ctx", ahead)
-        ccw = lax.ppermute(ccw, "ctx", back)
-        steps.append([(place(-step), cw), (place(step), ccw)])
-    half = width_local // 2
-    cw = lax.ppermute(cw[:half], "ctx", ahead)
-    ccw = lax.ppermute(ccw[half:], "ctx", back)
-    last = [cw, ccw]
+        cw = tuple(move(part, ahead) for part in cw)
+        ccw = tuple(move(part, back) for part in ccw)
+        steps.append([(place(-step), on_chip(*cw)), (place(step), on_chip(*ccw))])
+    last = on_chip(move(cw[0], ahead), move(ccw[1], back))
     values = extend(None, token_pieces, steps[0] + steps[1])
     for step in range(2, half_count):
         values = extend(values, token_pieces, steps[step])

time: 81.9 us -> 85.5 us (1.044)
  starting transfers between devices: 20.7 us -> 24.9 us
  local copies, waits for them, and re-layouts: 11.1 us -> 8.32 us
  waiting for transfers between devices: 29 us -> 30.9 us
    ppermute x8 -> x14, waiting for transfers between devices: 8.81 us -> 12.9 us  [move(): return lax.ppermute(part, 'ctx', route)]
    ppermute x8 -> x14, starting transfers between devices: 12.3 us -> 15.5 us  [move(): return lax.ppermute(part, 'ctx', route)]
    slice x2 -> x1, local copies, waits for them, and re-layouts: 2.4 us -> 0.04 us  [body(): cw = ccw = (first[:half], first[half:])]
    ppermute x9, waiting for transfers between devices: 20.2 us -> 18 us  [from_partner(): return lax.ppermute(block, axis, route)]
    ppermute x9, starting transfers between devices: 8.45 us -> 9.47 us  [from_partner(): return lax.ppermute(block, axis, route)]
    unnamed x31 -> x37, local copies, waits for them, and re-layouts: 8.53 us -> 8.11 us
  transfers between devices with their start and end apart: 17 -> 23, of which waited for: 6 -> 8; matrix products, arithmetic and copies ran while one was open for 5% -> 2% of each run, Pallas kernels for 15% -> 15%
where the time goes in v1:
time: 85.5 us; the launch traced here: 85.2 us
  waiting for transfers between devices  30.9 us (36%)
  starting transfers between devices  24.9 us (29%)
  Pallas kernels  18.7 us (22%)
  local copies, waits for them, and re-layouts  8.32 us (10%)
  matrix products  1.41 us (2%)
    ppermute x9, waiting for transfers between devices, from_partner(): return lax.ppermute(block, axis, route)  18 us
    ppermute x14, starting transfers between devices, move(): return lax.ppermute(part, 'ctx', route)  15.5 us
    ppermute x14, waiting for transfers between devices, move(): return lax.ppermute(part, 'ctx', route)  12.9 us
    pallas_call x4, Pallas kernels, extend(): pl.pallas_call(functools.partial(extend_kernel, len(pieces), len(parts),...  10.5 us
    ppermute x9, starting transfers between devices, from_partner(): return lax.ppermute(block, axis, route)  9.47 us
    unnamed x37, local copies, waits for them, and re-layouts  8.11 us
    pallas_call x1, Pallas kernels, finish(): pl.pallas_call(functools.partial(finish_kernel, len(token_pieces), len(la...  6.29 us
    pallas_call x1, Pallas kernels, prepare(): pl.pallas_call(prepare_kernel, out_shape=[pltpu.VMEM((heads, (block + 1)...  1.87 us
  transfers between devices with their start and end apart: 23, of which 8 were waited for; matrix products, arithmetic and copies ran while one was open for 2% of the time, Pallas kernels for 15%

profile of v1, /device:TPU:0, one launch (start us, length us, event | category | flops | bytes accessed | tf_op | source)
XLA Modules:
  0.0 85.2 jit_solution(11093031025795030093)
XLA Ops:
  0.0 1.4 %fusion.2 = (bf16[128,512]{1,0:T(8,128)(2,1)S(1)}, f32[128,512]{1,0:T(8,128)S(1)}) fusion(bf16[512,128]{1,0:T(8,128)(2,1)} %k_ref.1, bf16[512,512]{1,0:T(8,128)(2,1)} %refs_0_.7), kind=kOutput, calls=%fused_computation.11 | convolution fusion | flops 67174400 | bytes 1048576 | tf_op jit(solution)/shard_map/tn,tf->nf/dot_general | solution.py:287
  1.4 3.1 %collective-permute-start.3 = (bf16[128,512]{1,0:T(8,128)(2,1)S(1)}, bf16[128,512]{1,0:T(8,128)(2,1)S(1)}, u32[]{:S(2)}, u32[]{:S(2)}) collective-permute-start(bf16[128,512]{1,0:T(8,128)(2,1)S(1)} %get-tuple-element.11), channel_id=1, source_target_pairs={{0,4},{4,0},{8,12},{12,8},{16,20},{20,16},{24,28},{28,24},{1,5},{5... | collective-permute-start | bytes 393224 | tf_op jit(solution)/shard_map/ppermute | solution.py:22
  4.5 1.2 %copy.6 = bf16[256,1024]{0,1:T(8,128)(2,1)S(1)} copy(bf16[256,1024]{1,0:T(8,128)(2,1)} %param.6) | data formatting | bytes 1048576 | tf_op args[1]
  5.8 1.6 %collective-permute-start.17 = (bf16[512,256]{1,0:T(8,128)(2,1)S(1)}, bf16[512,256]{1,0:T(8,128)(2,1)S(1)}, u32[]{:S(2)}, u32[]{:S(2)}) collective-permute-start(bf16[512,256]{1,0:T(8,128)(2,1)S(1)} %get-tuple-element.9.refs_5_), channel_id=1, source_target_pairs={{0,8},{8,16},{16,24},{24,28},{28,20},{20,12},{12,4},{4,0},{1,9},{9... | collective-permute-start | bytes 786440 | tf_op jit(solution)/shard_map/ppermute | solution.py:325
  7.4 0.4 collective-permute-start.13
  7.9 0.1 collective-permute-start.20
  8.0 1.9 %collective-permute-start.9 = (bf16[512,256]{1,0:T(8,128)(2,1)S(1)}, bf16[512,256]{1,0:T(8,128)(2,1)}, u32[]{:S(2)}, u32[]{:S(2)}) collective-permute-start(bf16[512,256]{1,0:T(8,128)(2,1)S(1)} %get-tuple-element.10.refs_4_), channel_id=1, source_target_pairs={{0,8},{8,16},{16,24},{24,28},{28,20},{20,12},{12,4},{4,0},{1,9},{9... | collective-permute-start | bytes 786440 | tf_op jit(solution)/shard_map/ppermute | solution.py:325
  9.9 1.6 %collective-permute-start.4 = (bf16[128,512]{1,0:T(8,128)(2,1)S(1)}, bf16[128,512]{1,0:T(8,128)(2,1)S(1)}, u32[]{:S(2)}, u32[]{:S(2)}) collective-permute-start(bf16[128,512]{1,0:T(8,128)(2,1)S(1)} %fusion), channel_id=1, source_target_pairs={{0,8},{8,0},{4,12},{12,4},{16,24},{24,16},{20,28},{28,20},{1,9},{9... | collective-permute-start | bytes 393224 | tf_op jit(solution)/shard_map/ppermute | solution.py:22
  11.6 11.7 %collective-permute-done.4 = bf16[128,512]{1,0:T(8,128)(2,1)S(1)} collective-permute-done((bf16[128,512]{1,0:T(8,128)(2,1)S(1)}, bf16[128,512]{1,0:T(8,128)(2,1)S(1)}, u32[]{:S(2)}, u32[]{:S(2)}) %collective-permute-start.4) | collective-permute-done | bytes 131104 | tf_op jit(solution)/shard_map/ppermute | solution.py:22
  23.3 1.5 %collective-permute-start.1 = (bf16[512,512]{1,0:T(8,128)(2,1)S(1)}, bf16[512,512]{1,0:T(8,128)(2,1)S(1)}, u32[]{:S(2)}, u32[]{:S(2)}) collective-permute-start(bf16[512,512]{1,0:T(8,128)(2,1)S(1)} %copy-done), channel_id=1, source_target_pairs={{0,2},{2,0},{1,3},{3,1},{4,6},{6,4},{5,7},{7,5},{8,10},{10,8},{9,1... | collective-permute-start | bytes 1572872 | tf_op jit(solution)/shard_map/ppermute | solution.py:22
  24.9 2.7 %collective-permute-start.5 = (bf16[128,512]{1,0:T(8,128)(2,1)S(1)}, bf16[128,512]{1,0:T(8,128)(2,1)S(1)}, u32[]{:S(2)}, u32[]{:S(2)}) collective-permute-start(bf16[128,512]{1,0:T(8,128)(2,1)S(1)} %add_convert_fusion), channel_id=1, source_target_pairs={{0,16},{16,0},{4,20},{20,4},{8,24},{24,8},{12,28},{28,12},{1,17},{... | collective-permute-start | bytes 393224 | tf_op jit(solution)/shard_map/ppermute | solution.py:22
  27.6 0.3 collective-permute-start.18
  27.9 0.1 collective-permute-start
  27.9 1.8 %collective-permute-start.14 = (bf16[512,256]{1,0:T(8,128)(2,1)}, bf16[512,256]{1,0:T(8,128)(2,1)}, u32[]{:S(2)}, u32[]{:S(2)}) collective-permute-start(bf16[512,256]{1,0:T(8,128)(2,1)} %collective-permute-done.13.refs_9_), channel_id=1, source_target_pairs={{8,0},{16,8},{24,16},{28,24},{20,28},{12,20},{4,12},{0,4},{9,1},{1... | collective-permute-start | bytes 786440 | tf_op jit(solution)/shard_map/ppermute | solution.py:325
  29.7 3.6 %collective-permute-done.5 = bf16[128,512]{1,0:T(8,128)(2,1)S(1)} collective-permute-done((bf16[128,512]{1,0:T(8,128)(2,1)S(1)}, bf16[128,512]{1,0:T(8,128)(2,1)S(1)}, u32[]{:S(2)}, u32[]{:S(2)}) %collective-permute-start.5) | collective-permute-done | bytes 131104 | tf_op jit(solution)/shard_map/ppermute | solution.py:22
  33.3 1.0 %collective-permute-done.18.refs_5_.refs_11_ = bf16[512,256]{1,0:T(8,128)(2,1)S(1)} collective-permute-done((bf16[512,256]{1,0:T(8,128)(2,1)S(1)}, bf16[512,256]{1,0:T(8,128)(2,1)S(1)}, u32[]{:S(2)}, u32[]{:S(2)}) %collective-permute-start.18) | collective-permute-done | bytes 262176 | tf_op jit(solution)/shard_map/ppermute | solution.py:325
  34.4 3.3 %collective-permute-start.10 = (bf16[512,256]{1,0:T(8,128)(2,1)}, bf16[512,256]{1,0:T(8,128)(2,1)}, u32[]{:S(2)}, u32[]{:S(2)}) collective-permute-start(bf16[512,256]{1,0:T(8,128)(2,1)} %collective-permute-done.9.refs_6_), channel_id=1, source_target_pairs={{0,8},{8,16},{16,24},{24,28},{28,20},{20,12},{12,4},{4,0},{1,9},{9... | collective-permute-start | bytes 786440 | tf_op jit(solution)/shard_map/ppermute | solution.py:325
  37.8 0.5 collective-permute-done.14.refs_7_.refs_13_
  38.3 0.5 collective-permute-start.7
  38.8 4.7 %collective-permute-done.21.refs_6_.refs_12_ = bf16[512,256]{1,0:T(8,128)(2,1)S(1)} collective-permute-done((bf16[512,256]{1,0:T(8,128)(2,1)}, bf16[512,256]{1,0:T(8,128)(2,1)S(1)}, u32[]{:S(2)}, u32[]{:S(2)}) %collective-permute-start.21) | collective-permute-done | bytes 262176 | tf_op jit(solution)/shard_map/ppermute | solution.py:325
  43.5 0.6 collective-permute-start.19
  44.1 1.5 %collective-permute-start.15 = (bf16[512,256]{1,0:T(8,128)(2,1)}, bf16[512,256]{1,0:T(8,128)(2,1)}, u32[]{:S(2)}, u32[]{:S(2)}) collective-permute-start(bf16[512,256]{1,0:T(8,128)(2,1)} %collective-permute-done.14.refs_7_.refs_13_), channel_id=1, source_target_pairs={{8,0},{16,8},{24,16},{28,24},{20,28},{12,20},{4,12},{0,4},{9,1},{1... | collective-permute-start | bytes 786440 | tf_op jit(solution)/shard_map/ppermute | solution.py:325
  45.6 1.2 %collective-permute-start.11 = (bf16[512,256]{1,0:T(8,128)(2,1)}, bf16[512,256]{1,0:T(8,128)(2,1)}, u32[]{:S(2)}, u32[]{:S(2)}) collective-permute-start(bf16[512,256]{1,0:T(8,128)(2,1)} %collective-permute-done.10.refs_4_.refs_10_), channel_id=1, source_target_pairs={{0,8},{8,16},{16,24},{24,28},{28,20},{20,12},{12,4},{4,0},{1,9},{9... | collective-permute-start | bytes 786440 | tf_op jit(solution)/shard_map/ppermute | solution.py:325
  46.8 2.7 %collective-permute-done.7.refs_2_.refs_6_ = bf16[384,512]{1,0:T(8,128)(2,1)} collective-permute-done((bf16[384,512]{1,0:T(8,128)(2,1)S(1)}, bf16[384,512]{1,0:T(8,128)(2,1)}, u32[]{:S(2)}, u32[]{:S(2)}) %collective-permute-start.7) | collective-permute-done | bytes 393248 | tf_op jit(solution)/shard_map/ppermute | solution.py:22
  49.5 3.3 %collective-permute-done.19.refs_5_.refs_15_ = bf16[512,256]{1,0:T(8,128)(2,1)S(1)} collective-permute-done((bf16[512,256]{1,0:T(8,128)(2,1)S(1)}, bf16[512,256]{1,0:T(8,128)(2,1)S(1)}, u32[]{:S(2)}, u32[]{:S(2)}) %collective-permute-start.19) | collective-permute-done | bytes 262176 | tf_op jit(solution)/shard_map/ppermute | solution.py:325
  52.7 0.7 copy-done.13
  53.4 0.7 collective-permute-start.22
  54.1 3.3 %collective-permute-done.11.refs_4_.refs_14_ = bf16[512,256]{1,0:T(8,128)(2,1)} collective-permute-done((bf16[512,256]{1,0:T(8,128)(2,1)}, bf16[512,256]{1,0:T(8,128)(2,1)}, u32[]{:S(2)}, u32[]{:S(2)}) %collective-permute-start.11) | collective-permute-done | bytes 262176 | tf_op jit(solution)/shard_map/ppermute | solution.py:325
  57.5 0.4 collective-permute-start.16
  57.9 1.6 %collective-permute-start.12 = (bf16[512,256]{1,0:T(8,128)(2,1)}, bf16[512,256]{1,0:T(8,128)(2,1)}, u32[]{:S(2)}, u32[]{:S(2)}) collective-permute-start(bf16[512,256]{1,0:T(8,128)(2,1)} %collective-permute-done.11.refs_4_.refs_14_), channel_id=1, source_target_pairs={{0,8},{8,16},{16,24},{24,28},{28,20},{20,12},{12,4},{4,0},{1,9},{9... | collective-permute-start | bytes 786440 | tf_op jit(solution)/shard_map/ppermute | solution.py:325
  59.5 0.1 pad_add_fusion.1.where_ref
  59.9 0.9 %copy-done.15 = bf16[512,128]{1,0:T(8,128)(2,1)S(1)} copy-done((bf16[512,128]{1,0:T(8,128)(2,1)S(1)}, bf16[512,128]{1,0:T(8,128)(2,1)}, u32[]{:S(2)}) %copy-start.15) | copy-done | bytes 131096
  60.8 0.9 %copy-done.17 = bf16[512,128]{1,0:T(8,128)(2,1)S(1)} copy-done((bf16[512,128]{1,0:T(8,128)(2,1)S(1)}, bf16[512,128]{1,0:T(8,128)(2,1)}, u32[]{:S(2)}) %copy-start.17) | copy-done | bytes 131096
  61.7 1.9 %prepare.1 = (bf16[16,256,256]{2,1,0:T(8,128)(2,1)S(1)}, bf16[16,512,256]{2,1,0:T(8,128)(2,1)S(1)}) custom-call(bf16[512,128]{1,0:T(8,128)(2,1)S(1)} %copy-done.15, bf16[512,128]{1,0:T(8,128)(2,1)S(1)} %copy-done.17, f32[13,16,512]{2,1,0:T(8,128)S(1)} %copy-done.5), custom_call_target="tpu_custom_call" | custom-call | tf_op jit(solution)/shard_map/prepare/pallas_call | solution.py:127
  63.6 2.0 %copy-done.1 = bf16[16,512,256]{2,1,0:T(8,128)(2,1)} copy-done((bf16[16,512,256]{2,1,0:T(8,128)(2,1)}, bf16[16,512,256]{2,1,0:T(8,128)(2,1)S(1)}, u32[]{:S(2)}) %copy-start.1) | copy-done | bytes 4194328
  65.5 1.4 %copy-done.3 = bf16[16,256,256]{2,1,0:T(8,128)(2,1)} copy-done((bf16[16,256,256]{2,1,0:T(8,128)(2,1)}, bf16[16,256,256]{2,1,0:T(8,128)(2,1)S(1)}, u32[]{:S(2)}) %copy-start.3) | copy-done | bytes 2097176
  66.9 0.1 stack.96.where_ref
  67.0 0.1 stack.97.where_ref
  67.1 0.1 pad_add_fusion.2.where_ref
  67.2 0.1 pad_add_fusion.where_ref
  67.2 1.0 %copy-done.7 = bf16[512,256]{1,0:T(8,128)(2,1)S(1)} copy-done((bf16[512,256]{1,0:T(8,128)(2,1)S(1)}, bf16[512,256]{1,0:T(8,128)(2,1)}, u32[]{:S(2)}) %copy-start.7) | copy-done | bytes 262168
  68.2 2.3 %shard_map.55.refs_8_ = f32[1024,512]{1,0:T(8,128)S(1)} custom-call(s32[6]{0:T(128)S(1)} %stack.96.where_ref, bf16[512,512]{1,0:T(8,128)(2,1)S(1)} %copy-done, bf16[512,512]{1,0:T(8,128)(2,1)S(1)} %collective-permute-done.refs_1_, bf16[512,512]{1,0:T(8,128)(2,1)S(1)} %collective-permute-done.1.refs_2_, bf16[512,512]{1,0:T(8,128)(2,1)S(1)} %collective-permute-done.2.refs_3_, ...), custom_call_target="tpu_custom_call" | custom-call | tf_op jit(solution)/shard_map/pallas_call | solution.py:178
  70.5 0.0 copy-start.14
  70.5 1.9 %shard_map.56.refs_8_ = f32[1024,512]{1,0:T(8,128)S(1)} custom-call(s32[4]{0:T(128)S(1)} %pad_add_fusion.2.where_ref, bf16[512,512]{1,0:T(8,128)(2,1)S(1)} %copy-done, bf16[512,512]{1,0:T(8,128)(2,1)S(1)} %collective-permute-done.refs_1_, bf16[512,512]{1,0:T(8,128)(2,1)S(1)} %collective-permute-done.1.refs_2_, ...), custom_call_target="tpu_custom_call" | custom-call | tf_op jit(solution)/shard_map/pallas_call | solution.py:178
  72.5 2.0 %shard_map.57.refs_10_ = f32[1024,512]{1,0:T(8,128)S(1)} custom-call(s32[4]{0:T(128)S(1)} %pad_add_fusion.1.where_ref, bf16[512,512]{1,0:T(8,128)(2,1)S(1)} %copy-done, bf16[512,512]{1,0:T(8,128)(2,1)S(1)} %collective-permute-done.refs_1_, bf16[512,512]{1,0:T(8,128)(2,1)S(1)} %collective-permute-done.1.refs_2_, ...), custom_call_target="tpu_custom_call" | custom-call | tf_op jit(solution)/shard_map/pallas_call | solution.py:178
  74.5 0.0 copy-start.16
  74.5 4.3 %shard_map.58.refs_11_ = f32[1024,384]{1,0:T(8,128)S(1)} custom-call(s32[14]{0:T(128)S(1)} %stack.97.where_ref, bf16[384,512]{1,0:T(8,128)(2,1)S(1)} %pad_maximum_fusion.refs_0_.refs_4_, bf16[384,512]{1,0:T(8,128)(2,1)} %collective-permute-done.6.refs_1_.refs_5_, bf16[384,512]{1,0:T(8,128)(2,1)} %collective-permute-done.7.refs_2_.refs_6_, ...), custom_call_target="tpu_custom_call" | custom-call | tf_op jit(solution)/shard_map/pallas_call | solution.py:178
  78.9 6.3 %finish.1 = bf16[512,1024]{1,0:T(8,128)(2,1)} custom-call(s32[2]{0:T(128)S(1)} %pad_add_fusion.where_ref, bf16[512,512]{1,0:T(8,128)(2,1)S(1)} %copy-done, bf16[512,512]{1,0:T(8,128)(2,1)S(1)} %collective-permute-done.refs_1_, bf16[512,512]{1,0:T(8,128)(2,1)S(1)} %collective-permute-done.1.refs_2_, bf16[512,512]{1,0:T(8,128)(2,1)S(1)} %collective-permute-done.2.refs_3_, ...), custom_call_target="tpu_custom_call" | custom-call | tf_op jit(solution)/shard_map/finish/pallas_call | solution.py:265
  (54 shorter events, 0.3 us)
Async XLA Ops:
  0.0 23.3 %copy-start = (bf16[512,512]{1,0:T(8,128)(2,1)S(1)}, bf16[512,512]{1,0:T(8,128)(2,1)}, u32[]{:S(2)}) copy-start(bf16[512,512]{1,0:T(8,128)(2,1)} %refs_0_.7) | copy-start | bytes 1572868
  1.4 8.5 %collective-permute-start.3 = (bf16[128,512]{1,0:T(8,128)(2,1)S(1)}, bf16[128,512]{1,0:T(8,128)(2,1)S(1)}, u32[]{:S(2)}, u32[]{:S(2)}) collective-permute-start(bf16[128,512]{1,0:T(8,128)(2,1)S(1)} %get-tuple-element.11), channel_id=1, source_target_pairs={{0,4},{4,0},{8,12},{12,8},{16,20},{20,16},{24,28},{28,24},{1,5},{5... | collective-permute-start | bytes 393224 | tf_op jit(solution)/shard_map/ppermute | solution.py:22
  5.7 54.1 %copy-start.5 = (f32[13,16,512]{2,1,0:T(8,128)S(1)}, f32[13,16,512]{2,1,0:T(8,128)}, u32[]{:S(2)}) copy-start(f32[13,16,512]{2,1,0:T(8,128)} %refs_13_.1) | copy-start | bytes 1277956
  5.8 19.1 %collective-permute-start.17 = (bf16[512,256]{1,0:T(8,128)(2,1)S(1)}, bf16[512,256]{1,0:T(8,128)(2,1)S(1)}, u32[]{:S(2)}, u32[]{:S(2)}) collective-permute-start(bf16[512,256]{1,0:T(8,128)(2,1)S(1)} %get-tuple-element.9.refs_5_), channel_id=1, source_target_pairs={{0,8},{8,16},{16,24},{24,28},{28,20},{20,12},{12,4},{4,0},{1,9},{9... | collective-permute-start | bytes 786440 | tf_op jit(solution)/shard_map/ppermute | solution.py:325
  7.4 20.1 %collective-permute-start.13 = (bf16[512,256]{1,0:T(8,128)(2,1)S(1)}, bf16[512,256]{1,0:T(8,128)(2,1)}, u32[]{:S(2)}, u32[]{:S(2)}) collective-permute-start(bf16[512,256]{1,0:T(8,128)(2,1)S(1)} %get-tuple-element.9.refs_5_), channel_id=1, source_target_pairs={{8,0},{16,8},{24,16},{28,24},{20,28},{12,20},{4,12},{0,4},{9,1},{1... | collective-permute-start | bytes 786440 | tf_op jit(solution)/shard_map/ppermute | solution.py:325
  7.9 20.0 %collective-permute-start.20 = (bf16[512,256]{1,0:T(8,128)(2,1)S(1)}, bf16[512,256]{1,0:T(8,128)(2,1)}, u32[]{:S(2)}, u32[]{:S(2)}) collective-permute-start(bf16[512,256]{1,0:T(8,128)(2,1)S(1)} %get-tuple-element.10.refs_4_), channel_id=1, source_target_pairs={{8,0},{16,8},{24,16},{28,24},{20,28},{12,20},{4,12},{0,4},{9,1},{1... | collective-permute-start | bytes 786440 | tf_op jit(solution)/shard_map/ppermute | solution.py:325
  8.0 20.0 %collective-permute-start.9 = (bf16[512,256]{1,0:T(8,128)(2,1)S(1)}, bf16[512,256]{1,0:T(8,128)(2,1)}, u32[]{:S(2)}, u32[]{:S(2)}) collective-permute-start(bf16[512,256]{1,0:T(8,128)(2,1)S(1)} %get-tuple-element.10.refs_4_), channel_id=1, source_target_pairs={{0,8},{8,16},{16,24},{24,28},{28,20},{20,12},{12,4},{4,0},{1,9},{9... | collective-permute-start | bytes 786440 | tf_op jit(solution)/shard_map/ppermute | solution.py:325
  9.9 13.4 %collective-permute-start.4 = (bf16[128,512]{1,0:T(8,128)(2,1)S(1)}, bf16[128,512]{1,0:T(8,128)(2,1)S(1)}, u32[]{:S(2)}, u32[]{:S(2)}) collective-permute-start(bf16[128,512]{1,0:T(8,128)(2,1)S(1)} %fusion), channel_id=1, source_target_pairs={{0,8},{8,0},{4,12},{12,4},{16,24},{24,16},{20,28},{28,20},{1,9},{9... | collective-permute-start | bytes 393224 | tf_op jit(solution)/shard_map/ppermute | solution.py:22
  23.3 14.4 %collective-permute-start.1 = (bf16[512,512]{1,0:T(8,128)(2,1)S(1)}, bf16[512,512]{1,0:T(8,128)(2,1)S(1)}, u32[]{:S(2)}, u32[]{:S(2)}) collective-permute-start(bf16[512,512]{1,0:T(8,128)(2,1)S(1)} %copy-done), channel_id=1, source_target_pairs={{0,2},{2,0},{1,3},{3,1},{4,6},{6,4},{5,7},{7,5},{8,10},{10,8},{9,1... | collective-permute-start | bytes 1572872 | tf_op jit(solution)/shard_map/ppermute | solution.py:22
  24.9 12.8 %copy-start.6 = (bf16[512,256]{1,0:T(8,128)(2,1)}, bf16[512,256]{1,0:T(8,128)(2,1)S(1)}, u32[]{:S(2)}) copy-start(bf16[512,256]{1,0:T(8,128)(2,1)S(1)} %collective-permute-done.17.refs_7_) | copy-start | bytes 786436
  24.9 8.4 %collective-permute-start.5 = (bf16[128,512]{1,0:T(8,128)(2,1)S(1)}, bf16[128,512]{1,0:T(8,128)(2,1)S(1)}, u32[]{:S(2)}, u32[]{:S(2)}) collective-permute-start(bf16[128,512]{1,0:T(8,128)(2,1)S(1)} %add_convert_fusion), channel_id=1, source_target_pairs={{0,16},{16,0},{4,20},{20,4},{8,24},{24,8},{12,28},{28,12},{1,17},{... | collective-permute-start | bytes 393224 | tf_op jit(solution)/shard_map/ppermute | solution.py:22
  27.6 6.8 %collective-permute-start.18 = (bf16[512,256]{1,0:T(8,128)(2,1)S(1)}, bf16[512,256]{1,0:T(8,128)(2,1)S(1)}, u32[]{:S(2)}, u32[]{:S(2)}) collective-permute-start(bf16[512,256]{1,0:T(8,128)(2,1)S(1)} %collective-permute-done.17.refs_7_), channel_id=1, source_target_pairs={{0,8},{8,16},{16,24},{24,28},{28,20},{20,12},{12,4},{4,0},{1,9},{9... | collective-permute-start | bytes 786440 | tf_op jit(solution)/shard_map/ppermute | solution.py:325
  27.9 17.7 %collective-permute-start = (bf16[512,512]{1,0:T(8,128)(2,1)S(1)}, bf16[512,512]{1,0:T(8,128)(2,1)S(1)}, u32[]{:S(2)}, u32[]{:S(2)}) collective-permute-start(bf16[512,512]{1,0:T(8,128)(2,1)S(1)} %copy-done), channel_id=1, source_target_pairs={{0,1},{1,0},{2,3},{3,2},{4,5},{5,4},{6,7},{7,6},{8,9},{9,8},{10,11... | collective-permute-start | bytes 1572872 | tf_op jit(solution)/shard_map/ppermute | solution.py:22
  27.9 10.3 %collective-permute-start.14 = (bf16[512,256]{1,0:T(8,128)(2,1)}, bf16[512,256]{1,0:T(8,128)(2,1)}, u32[]{:S(2)}, u32[]{:S(2)}) collective-permute-start(bf16[512,256]{1,0:T(8,128)(2,1)} %collective-permute-done.13.refs_9_), channel_id=1, source_target_pairs={{8,0},{16,8},{24,16},{28,24},{20,28},{12,20},{4,12},{0,4},{9,1},{1... | collective-permute-start | bytes 786440 | tf_op jit(solution)/shard_map/ppermute | solution.py:325
  33.3 10.2 %collective-permute-start.21 = (bf16[512,256]{1,0:T(8,128)(2,1)}, bf16[512,256]{1,0:T(8,128)(2,1)S(1)}, u32[]{:S(2)}, u32[]{:S(2)}) collective-permute-start(bf16[512,256]{1,0:T(8,128)(2,1)} %collective-permute-done.20.refs_8_), channel_id=1, source_target_pairs={{8,0},{16,8},{24,16},{28,24},{20,28},{12,20},{4,12},{0,4},{9,1},{1... | collective-permute-start | bytes 786440 | tf_op jit(solution)/shard_map/ppermute | solution.py:325
  34.4 15.1 %copy-start.9 = (bf16[512,256]{1,0:T(8,128)(2,1)}, bf16[512,256]{1,0:T(8,128)(2,1)S(1)}, u32[]{:S(2)}) copy-start(bf16[512,256]{1,0:T(8,128)(2,1)S(1)} %collective-permute-done.18.refs_5_.refs_11_) | copy-start | bytes 786436
  34.4 9.7 %collective-permute-start.10 = (bf16[512,256]{1,0:T(8,128)(2,1)}, bf16[512,256]{1,0:T(8,128)(2,1)}, u32[]{:S(2)}, u32[]{:S(2)}) collective-permute-start(bf16[512,256]{1,0:T(8,128)(2,1)} %collective-permute-done.9.refs_6_), channel_id=1, source_target_pairs={{0,8},{8,16},{16,24},{24,28},{28,20},{20,12},{12,4},{4,0},{1,9},{9... | collective-permute-start | bytes 786440 | tf_op jit(solution)/shard_map/ppermute | solution.py:325
  37.7 20.1 %collective-permute-start.2 = (bf16[512,512]{1,0:T(8,128)(2,1)S(1)}, bf16[512,512]{1,0:T(8,128)(2,1)S(1)}, u32[]{:S(2)}, u32[]{:S(2)}) collective-permute-start(bf16[512,512]{1,0:T(8,128)(2,1)S(1)} %collective-permute-done.1.refs_2_), channel_id=1, source_target_pairs={{0,1},{1,0},{2,3},{3,2},{4,5},{5,4},{6,7},{7,6},{8,9},{9,8},{10,11... | collective-permute-start | bytes 1572872 | tf_op jit(solution)/shard_map/ppermute | solution.py:22
  38.3 11.2 %collective-permute-start.7 = (bf16[384,512]{1,0:T(8,128)(2,1)S(1)}, bf16[384,512]{1,0:T(8,128)(2,1)}, u32[]{:S(2)}, u32[]{:S(2)}) collective-permute-start(bf16[384,512]{1,0:T(8,128)(2,1)S(1)} %pad_maximum_fusion.refs_0_.refs_4_), channel_id=1, source_target_pairs={{0,2},{2,0},{1,3},{3,1},{4,6},{6,4},{5,7},{7,5},{8,10},{10,8},{9,1... | collective-permute-start | bytes 1179656 | tf_op jit(solution)/shard_map/ppermute | solution.py:22
  43.5 9.2 %copy-start.11 = (bf16[512,256]{1,0:T(8,128)(2,1)}, bf16[512,256]{1,0:T(8,128)(2,1)S(1)}, u32[]{:S(2)}) copy-start(bf16[512,256]{1,0:T(8,128)(2,1)S(1)} %collective-permute-done.21.refs_6_.refs_12_) | copy-start | bytes 786436
  43.5 9.2 %collective-permute-start.19 = (bf16[512,256]{1,0:T(8,128)(2,1)S(1)}, bf16[512,256]{1,0:T(8,128)(2,1)S(1)}, u32[]{:S(2)}, u32[]{:S(2)}) collective-permute-start(bf16[512,256]{1,0:T(8,128)(2,1)S(1)} %collective-permute-done.18.refs_5_.refs_11_), channel_id=1, source_target_pairs={{0,8},{8,16},{16,24},{24,28},{28,20},{20,12},{12,4},{4,0},{1,9},{9... | collective-permute-start | bytes 786440 | tf_op jit(solution)/shard_map/ppermute | solution.py:325
  44.1 9.3 %collective-permute-start.15 = (bf16[512,256]{1,0:T(8,128)(2,1)}, bf16[512,256]{1,0:T(8,128)(2,1)}, u32[]{:S(2)}, u32[]{:S(2)}) collective-permute-start(bf16[512,256]{1,0:T(8,128)(2,1)} %collective-permute-done.14.refs_7_.refs_13_), channel_id=1, source_target_pairs={{8,0},{16,8},{24,16},{28,24},{20,28},{12,20},{4,12},{0,4},{9,1},{1... | collective-permute-start | bytes 786440 | tf_op jit(solution)/shard_map/ppermute | solution.py:325
  45.6 11.9 %collective-permute-start.11 = (bf16[512,256]{1,0:T(8,128)(2,1)}, bf16[512,256]{1,0:T(8,128)(2,1)}, u32[]{:S(2)}, u32[]{:S(2)}) collective-permute-start(bf16[512,256]{1,0:T(8,128)(2,1)} %collective-permute-done.10.refs_4_.refs_10_), channel_id=1, source_target_pairs={{0,8},{8,16},{16,24},{24,28},{28,20},{20,12},{12,4},{4,0},{1,9},{9... | collective-permute-start | bytes 786440 | tf_op jit(solution)/shard_map/ppermute | solution.py:325
  49.5 25.0 %collective-permute-start.6 = (bf16[384,512]{1,0:T(8,128)(2,1)S(1)}, bf16[384,512]{1,0:T(8,128)(2,1)}, u32[]{:S(2)}, u32[]{:S(2)}) collective-permute-start(bf16[384,512]{1,0:T(8,128)(2,1)S(1)} %pad_maximum_fusion.refs_0_.refs_4_), channel_id=1, source_target_pairs={{0,1},{1,0},{2,3},{3,2},{4,5},{5,4},{6,7},{7,6},{8,9},{9,8},{10,11... | collective-permute-start | bytes 1179656 | tf_op jit(solution)/shard_map/ppermute | solution.py:22
  52.7 0.7 copy-start.13
  53.4 21.1 %collective-permute-start.8 = (bf16[384,512]{1,0:T(8,128)(2,1)}, bf16[384,512]{1,0:T(8,128)(2,1)}, u32[]{:S(2)}, u32[]{:S(2)}) collective-permute-start(bf16[384,512]{1,0:T(8,128)(2,1)} %collective-permute-done.7.refs_2_.refs_6_), channel_id=1, source_target_pairs={{0,1},{1,0},{2,3},{3,2},{4,5},{5,4},{6,7},{7,6},{8,9},{9,8},{10,11... | collective-permute-start | bytes 1179656 | tf_op jit(solution)/shard_map/ppermute | solution.py:22
  53.4 19.0 %collective-permute-start.22 = (bf16[512,256]{1,0:T(8,128)(2,1)}, bf16[512,256]{1,0:T(8,128)(2,1)}, u32[]{:S(2)}, u32[]{:S(2)}) collective-permute-start(bf16[512,256]{1,0:T(8,128)(2,1)} %copy-done.11), channel_id=1, source_target_pairs={{8,0},{16,8},{24,16},{28,24},{20,28},{12,20},{4,12},{0,4},{9,1},{1... | collective-permute-start | bytes 786440 | tf_op jit(solution)/shard_map/ppermute | solution.py:325
  57.5 21.4 %collective-permute-start.16 = (bf16[512,256]{1,0:T(8,128)(2,1)}, bf16[512,256]{1,0:T(8,128)(2,1)}, u32[]{:S(2)}, u32[]{:S(2)}) collective-permute-start(bf16[512,256]{1,0:T(8,128)(2,1)} %collective-permute-done.15.refs_7_.refs_17_), channel_id=1, source_target_pairs={{8,0},{16,8},{24,16},{28,24},{20,28},{12,20},{4,12},{0,4},{9,1},{1... | collective-permute-start | bytes 786440 | tf_op jit(solution)/shard_map/ppermute | solution.py:325
  57.9 21.0 %collective-permute-start.12 = (bf16[512,256]{1,0:T(8,128)(2,1)}, bf16[512,256]{1,0:T(8,128)(2,1)}, u32[]{:S(2)}, u32[]{:S(2)}) collective-permute-start(bf16[512,256]{1,0:T(8,128)(2,1)} %collective-permute-done.11.refs_4_.refs_14_), channel_id=1, source_target_pairs={{0,8},{8,16},{16,24},{24,28},{28,20},{20,12},{12,4},{4,0},{1,9},{9... | collective-permute-start | bytes 786440 | tf_op jit(solution)/shard_map/ppermute | solution.py:325
  59.8 0.9 %copy-start.15 = (bf16[512,128]{1,0:T(8,128)(2,1)S(1)}, bf16[512,128]{1,0:T(8,128)(2,1)}, u32[]{:S(2)}) copy-start(bf16[512,128]{1,0:T(8,128)(2,1)} %refs_12_.1) | copy-start | bytes 393220
  60.8 0.9 %copy-start.17 = (bf16[512,128]{1,0:T(8,128)(2,1)S(1)}, bf16[512,128]{1,0:T(8,128)(2,1)}, u32[]{:S(2)}) copy-start(bf16[512,128]{1,0:T(8,128)(2,1)} %k_ref.1) | copy-start | bytes 393220
  63.5 2.0 %copy-start.1 = (bf16[16,512,256]{2,1,0:T(8,128)(2,1)}, bf16[16,512,256]{2,1,0:T(8,128)(2,1)S(1)}, u32[]{:S(2)}) copy-start(bf16[16,512,256]{2,1,0:T(8,128)(2,1)S(1)} %get-tuple-element.8.refs_15_) | copy-start | bytes 12582916
  65.5 1.4 %copy-start.3 = (bf16[16,256,256]{2,1,0:T(8,128)(2,1)}, bf16[16,256,256]{2,1,0:T(8,128)(2,1)S(1)}, u32[]{:S(2)}) copy-start(bf16[16,256,256]{2,1,0:T(8,128)(2,1)S(1)} %get-tuple-element.7.refs_14_) | copy-start | bytes 6291460
  67.2 1.0 %copy-start.7 = (bf16[512,256]{1,0:T(8,128)(2,1)S(1)}, bf16[512,256]{1,0:T(8,128)(2,1)}, u32[]{:S(2)}) copy-start(bf16[512,256]{1,0:T(8,128)(2,1)} %copy-done.6) | copy-start | bytes 786436
  68.2 2.3 %copy-start.10 = (bf16[512,256]{1,0:T(8,128)(2,1)S(1)}, bf16[512,256]{1,0:T(8,128)(2,1)}, u32[]{:S(2)}) copy-start(bf16[512,256]{1,0:T(8,128)(2,1)} %copy-done.9) | copy-start | bytes 786436
  68.2 2.3 %copy-start.12 = (bf16[512,256]{1,0:T(8,128)(2,1)S(1)}, bf16[512,256]{1,0:T(8,128)(2,1)}, u32[]{:S(2)}) copy-start(bf16[512,256]{1,0:T(8,128)(2,1)} %copy-done.11) | copy-start | bytes 786436
  70.5 1.9 %copy-start.14 = (bf16[512,256]{1,0:T(8,128)(2,1)S(1)}, bf16[512,256]{1,0:T(8,128)(2,1)}, u32[]{:S(2)}) copy-start(bf16[512,256]{1,0:T(8,128)(2,1)} %copy-done.13) | copy-start | bytes 786436
  72.4 2.1 %copy-start.8 = (bf16[512,256]{1,0:T(8,128)(2,1)S(1)}, bf16[512,256]{1,0:T(8,128)(2,1)}, u32[]{:S(2)}) copy-start(bf16[512,256]{1,0:T(8,128)(2,1)} %copy-done.6) | copy-start | bytes 786436
  74.5 4.4 %copy-start.2 = (bf16[16,512,256]{2,1,0:T(8,128)(2,1)S(1)}, bf16[16,512,256]{2,1,0:T(8,128)(2,1)}, u32[]{:S(2)}) copy-start(bf16[16,512,256]{2,1,0:T(8,128)(2,1)} %copy-done.1) | copy-start | bytes 12582916
  74.5 4.4 %copy-start.4 = (bf16[16,256,256]{2,1,0:T(8,128)(2,1)S(1)}, bf16[16,256,256]{2,1,0:T(8,128)(2,1)}, u32[]{:S(2)}) copy-start(bf16[16,256,256]{2,1,0:T(8,128)(2,1)} %copy-done.3) | copy-start | bytes 6291460
  74.5 4.4 %copy-start.16 = (bf16[512,128]{1,0:T(8,128)(2,1)S(1)}, bf16[512,128]{1,0:T(8,128)(2,1)}, u32[]{:S(2)}) copy-start(bf16[512,128]{1,0:T(8,128)(2,1)} %refs_12_.1) | copy-start | bytes 393220

commit v2 on v1

--- a/solution.py
+++ b/solution.py
@@ -138,10 +138,40 @@
     )(queries, key_vectors, level_weight)
 
 
-def choose(where_ref, pieces, depth, chosen_ref, first, count):
-    for num in range(count):
-        piece = where_ref[2 * (first + num)]
-        start = pl.multiple_of(where_ref[2 * (first + num) + 1], 128)
+def turn_kernel(weight_ref, *half_refs):
+    share = half_refs[0].shape[0]
+    for num, half_ref in enumerate(half_refs):
+        half_ref[...] = weight_ref[:, num * share : (num + 1) * share].T
+
+
+def turn(weight, split):
+    depth, width = weight.shape
+    return pl.pallas_call(
+        turn_kernel,
+        out_shape=[pltpu.VMEM((width // split, depth), weight.dtype)] * split,
+        compiler_params=pltpu.CompilerParams(vmem_limit_bytes=8 << 20),
+        name="turn",
+    )(weight)
+
+
+def ring_order(count):
+    return list(range(0, count, 2)) + list(range(1, count, 2))[::-1]
+
+
+def place(offset, depth, piece_width):
+    count = lax.axis_size("ctx")
+    mine = lax.axis_index("ctx")
+    pos = jnp.where(mine % 2 == 0, mine // 2, count - 1 - mine // 2)
+    pos = (pos + offset + count) % count
+    index = jnp.where(pos < count // 2, 2 * pos, 2 * (count - 1 - pos) + 1)
+    per_piece = piece_width // depth
+    return jnp.bitwise_xor(index // per_piece, lax.axis_index("head")), index % per_piece * depth
+
+
+def choose(offsets, pieces, depth, chosen_ref):
+    for num, offset in enumerate(offsets):
+        piece, start = place(offset, depth, pieces[0].shape[1])
+        start = pl.multiple_of(start, 128)
         for index, ref in enumerate(pieces):
 
             @pl.when(piece == index)
@@ -149,12 +179,13 @@
                 chosen_ref[:, num * depth : (num + 1) * depth] = ref[:, pl.ds(start, depth)]
 
 
-def extend_kernel(piece_count, count, split, started, where_ref, *refs):
+def extend_kernel(piece_count, offsets, split, started, *refs):
+    count = len(offsets)
     pieces = refs[:piece_count]
     blocks = [refs[piece_count + num * split :][:split] for num in range(count)]
     out_ref, chosen_ref = refs[-2], refs[-1]
     share, depth = blocks[0][0].shape
-    choose(where_ref, pieces, depth, chosen_ref, 0, count)
+    choose(offsets, pieces, depth, chosen_ref)
     width = out_ref.shape[0]
     step = min(256, share)
     for c0 in range(0, width, step):
@@ -169,23 +200,22 @@
 
 
 def extend(total, pieces, parts):
-    where = jnp.stack([num for pair, _ in parts for num in pair])
+    offsets = tuple(offset for offset, _ in parts)
     blocks = [half for _, block in parts for half in block]
     split = len(parts[0][1])
     rows = pieces[0].shape[0]
     share, depth = blocks[0].shape
     arrays = [*pieces, *blocks, *([] if total is None else [total])]
     return pl.pallas_call(
-        functools.partial(extend_kernel, len(pieces), len(parts), split, total is not None),
-        in_specs=[pl.BlockSpec(memory_space=pltpu.SMEM)]
-        + [pl.BlockSpec(memory_space=pltpu.VMEM)] * len(arrays),
+        functools.partial(extend_kernel, len(pieces), offsets, split, total is not None),
+        in_specs=[pl.BlockSpec(memory_space=pltpu.VMEM)] * len(arrays),
         out_shape=pltpu.VMEM((share * split, rows), F32),
         scratch_shapes=[pltpu.VMEM((rows, depth * len(parts)), BF16)],
         compiler_params=pltpu.CompilerParams(vmem_limit_bytes=12 << 20),
-    )(where, *arrays)
-
-
-def finish_kernel(piece_count, last_count, near_count, head_size, where_ref, *refs):
+    )(*arrays)
+
+
+def finish_kernel(piece_count, offset, last_count, near_count, head_size, *refs):
     refs = list(refs)
     take = lambda count: [refs.pop(0) for _ in range(count)]
     token_refs, sum_refs = take(piece_count), take(piece_count)
@@ -201,8 +231,9 @@
     if last_count:
         token_chosen, sum_chosen = refs
         depth = token_chosen.shape[1]
-        choose(where_ref, token_refs, depth, token_chosen, 0, 1)
-        choose(where_ref, sum_refs, depth, sum_chosen, 0, 1)
+        choose([offset], token_refs, depth, token_chosen)
+        choose([offset], sum_refs, depth, sum_chosen)
+    mine = lax.axis_index("ctx")
     queries = q_ref[...]
     twice = jnp.concatenate([queries, queries], axis=1)
     step = min(256, width)
@@ -222,6 +253,7 @@
         far = None
         for num in range(far_levels):
             state = states[:, num * state_rows : (num + 1) * state_rows]
+            state = jnp.where(jnp.right_shift(mine, num) % 2 == 1, state, jnp.zeros_like(state))
             high = state.astype(BF16)
             low = (state - high.astype(F32)).astype(BF16)
             reading = dot_last(jnp.concatenate([high, low], axis=1), twice)
@@ -255,7 +287,7 @@
             ).astype(BF16)
 
 
-def finish(values, states, where, last, token_pieces, sum_pieces, queries, level_weight, near, head_size):
+def finish(values, states, offset, last, token_pieces, sum_pieces, queries, level_weight, near, head_size):
     width, length = values.shape
     arrays = [*token_pieces, *sum_pieces, *last, values, states, queries, level_weight, *near]
     scratch = []
@@ -263,14 +295,13 @@
         depth = last[0].shape[1]
         scratch = [pltpu.VMEM((length, depth), BF16), pltpu.VMEM((states.shape[1], depth), BF16)]
     return pl.pallas_call(
-        functools.partial(finish_kernel, len(token_pieces), len(last), len(near), head_size),
-        in_specs=[pl.BlockSpec(memory_space=pltpu.SMEM)]
-        + [pl.BlockSpec(memory_space=pltpu.VMEM)] * len(arrays),
+        functools.partial(finish_kernel, len(token_pieces), offset, len(last), len(near), head_size),
+        in_specs=[pl.BlockSpec(memory_space=pltpu.VMEM)] * len(arrays),
         out_shape=jax.ShapeDtypeStruct((length, width), BF16),
         scratch_shapes=scratch,
         compiler_params=pltpu.CompilerParams(vmem_limit_bytes=24 << 20),
         name="finish",
-    )(where, *arrays)
+    )(*arrays)
 
 
 def body(tokens, value_weight, queries, key_vectors, level_weight):
@@ -280,16 +311,13 @@
     head_size = width_local // head_local
     ctx_count = lax.axis_size("ctx")
     dev_bits = ctx_count.bit_length() - 1
-    my_index = lax.axis_index("ctx")
-    my_head = lax.axis_index("head")
     near = prepare(queries, key_vectors, level_weight)
 
     running = jnp.einsum("tn,tf->nf", key_vectors, tokens, preferred_element_type=F32)
     level_sums = []
     for section_bit in range(dev_bits):
         partner = from_partner(running.astype(BF16), "ctx", section_bit)
-        is_right = my_index // 2**section_bit % 2 == 1
-        level_sums.append(jnp.where(is_right, partner, jnp.zeros_like(partner)))
+        level_sums.append(partner)
         running = running + partner.astype(F32)
     level_sums = jnp.concatenate(level_sums, axis=0)
 
@@ -299,27 +327,16 @@
         weight = lax.all_gather(value_weight, "ctx", axis=0, tiled=True)
         values = jnp.einsum("fc,tf->ct", weight, features, preferred_element_type=F32)
         states = jnp.einsum("fc,nf->cn", weight, sums, preferred_element_type=F32)
-        where = jnp.zeros((2,), jnp.int32)
-        return finish(values, states, where, [], [], [], queries, level_weight, near, head_size)
-
-    order = list(range(0, ctx_count, 2)) + list(range(1, ctx_count, 2))[::-1]
+        return finish(values, states, 0, [], [], [], queries, level_weight, near, head_size)
+
+    order = ring_order(ctx_count)
     ahead = [(order[i], order[(i + 1) % ctx_count]) for i in range(ctx_count)]
     back = [(b, a) for a, b in ahead]
     half_count = ctx_count // 2
-    my_pos = jnp.where(my_index % 2 == 0, my_index // 2, ctx_count - 1 - my_index // 2)
-
-    def place(offset):
-        pos = (my_pos + offset) % ctx_count
-        index = jnp.where(pos < half_count, 2 * pos, 2 * (ctx_count - 1 - pos) + 1)
-        start = index * depth
-        return start // width_feat ^ my_head, start % width_feat
-
     token_pieces = on_chip(*gather_pieces(tokens, "head"))
     sum_pieces = on_chip(*gather_pieces(level_sums, "head"))
-    half = width_local // 2
-    first = value_weight.T
-    cw = ccw = (first[:half], first[half:])
-    steps = [[(place(0), on_chip(*cw))]]
+    cw = ccw = tuple(turn(value_weight, 2))
+    steps = [[(0, cw)]]
 
     def move(part, route):
         return lax.ppermute(part, "ctx", route)
@@ -327,7 +344,7 @@
     for step in range(1, half_count):
         cw = tuple(move(part, ahead) for part in cw)
         ccw = tuple(move(part, back) for part in ccw)
-        steps.append([(place(-step), on_chip(*cw)), (place(step), on_chip(*ccw))])
+        steps.append([(-step, on_chip(*cw)), (step, on_chip(*ccw))])
     last = on_chip(move(cw[0], ahead), move(ccw[1], back))
     values = extend(None, token_pieces, steps[0] + steps[1])
     for step in range(2, half_count):
@@ -336,7 +353,7 @@
     return finish(
         values,
         states,
-        jnp.stack(place(half_count)),
+        half_count,
         last,
         token_pieces,
         sum_pieces,

time: 85.5 us -> 71.9 us (0.84)
  starting transfers between devices: 24.9 us -> 34.6 us
  waiting for transfers between devices: 30.9 us -> 21.6 us
  local copies, waits for them, and re-layouts: 8.32 us -> 1.09 us
  Pallas kernels: 18.7 us -> 12.2 us
    ppermute x9, waiting for transfers between devices: 18 us -> 5.99 us  [from_partner(): return lax.ppermute(block, axis, route)]
    ppermute x14, starting transfers between devices: 15.5 us -> 24.1 us  [move(): return lax.ppermute(part, 'ctx', route)]
    unnamed x37 -> x12, local copies, waits for them, and re-layouts: 8.11 us -> 1.07 us
    pallas_call x5 -> x6, Pallas kernels: 16.8 us -> 10.3 us  [the longest x4 5.3 us: extend(): pl.pallas_call(functools.partial(extend_kernel, len(pieces), offsets, spl...]
    ppermute x14, waiting for transfers between devices: 12.9 us -> 15.6 us  [move(): return lax.ppermute(part, 'ctx', route)]
    ppermute x9, starting transfers between devices: 9.47 us -> 10.5 us  [from_partner(): return lax.ppermute(block, axis, route)]
  transfers between devices with their start and end apart: 23 -> 23, of which waited for: 8 -> 9; matrix products, arithmetic and copies ran while one was open for 2% -> 0% of each run, Pallas kernels for 15% -> 10%
where the time goes in v2:
time: 71.9 us; the launch traced here: 71.1 us
  starting transfers between devices  34.6 us (48%)
  waiting for transfers between devices  21.6 us (30%)
  Pallas kernels  12.2 us (17%)
  matrix products  1.45 us (2%)
  local copies, waits for them, and re-layouts  1.09 us (2%)
    ppermute x14, starting transfers between devices, move(): return lax.ppermute(part, 'ctx', route)  24.1 us
    ppermute x14, waiting for transfers between devices, move(): return lax.ppermute(part, 'ctx', route)  15.6 us
    ppermute x9, starting transfers between devices, from_partner(): return lax.ppermute(block, axis, route)  10.5 us
    ppermute x9, waiting for transfers between devices, from_partner(): return lax.ppermute(block, axis, route)  5.99 us
    pallas_call x4, Pallas kernels, extend(): pl.pallas_call(functools.partial(extend_kernel, len(pieces), offsets, spl...  5.3 us
    pallas_call x1, Pallas kernels, finish(): pl.pallas_call(functools.partial(finish_kernel, len(token_pieces), offset...  4.86 us
    pallas_call x1, Pallas kernels, prepare(): pl.pallas_call(prepare_kernel, out_shape=[pltpu.VMEM((heads, (block + 1)...  1.88 us
    dot_general x1, matrix products, body(): jnp.einsum('tn,tf->nf', key_vectors, tokens, preferred_element_type=F32)  1.45 us
  transfers between devices with their start and end apart: 23, of which 9 were waited for; matrix products, arithmetic and copies ran while one was open for 0% of the time, Pallas kernels for 10%

profile of v2, /device:TPU:0, one launch (start us, length us, event | category | flops | bytes accessed | tf_op | source)
XLA Modules:
  0.0 71.1 jit_solution(3605102919961229659)
XLA Ops:
  0.0 1.5 %fusion.1 = (bf16[128,512]{1,0:T(8,128)(2,1)S(1)}, f32[128,512]{1,0:T(8,128)S(1)}) fusion(bf16[512,128]{1,0:T(8,128)(2,1)} %k_ref.1, bf16[512,512]{1,0:T(8,128)(2,1)} %refs_0_.7), kind=kOutput, calls=%fused_computation.6 | convolution fusion | flops 67174400 | bytes 1048576 | tf_op jit(solution)/shard_map/tn,tf->nf/dot_general | solution.py:316
  1.5 3.1 %collective-permute-start.3 = (bf16[128,512]{1,0:T(8,128)(2,1)S(1)}, bf16[128,512]{1,0:T(8,128)(2,1)S(1)}, u32[]{:S(2)}, u32[]{:S(2)}) collective-permute-start(bf16[128,512]{1,0:T(8,128)(2,1)S(1)} %get-tuple-element.13), channel_id=1, source_target_pairs={{0,4},{4,0},{8,12},{12,8},{16,20},{20,16},{24,28},{28,24},{1,5},{5... | collective-permute-start | bytes 393224 | tf_op jit(solution)/shard_map/ppermute | solution.py:22
  4.5 3.5 %collective-permute-done.3 = bf16[128,512]{1,0:T(8,128)(2,1)S(1)} collective-permute-done((bf16[128,512]{1,0:T(8,128)(2,1)S(1)}, bf16[128,512]{1,0:T(8,128)(2,1)S(1)}, u32[]{:S(2)}, u32[]{:S(2)}) %collective-permute-start.3) | collective-permute-done | bytes 131104 | tf_op jit(solution)/shard_map/ppermute | solution.py:22
  8.1 1.9 %collective-permute-start.4 = (bf16[128,512]{1,0:T(8,128)(2,1)S(1)}, bf16[128,512]{1,0:T(8,128)(2,1)S(1)}, u32[]{:S(2)}, u32[]{:S(2)}) collective-permute-start(bf16[128,512]{1,0:T(8,128)(2,1)S(1)} %fusion), channel_id=1, source_target_pairs={{0,8},{8,0},{4,12},{12,4},{16,24},{24,16},{20,28},{28,20},{1,9},{9... | collective-permute-start | bytes 393224 | tf_op jit(solution)/shard_map/ppermute | solution.py:22
  9.9 1.0 %copy-done.3 = bf16[256,1024]{1,0:T(8,128)(2,1)S(1)} copy-done((bf16[256,1024]{1,0:T(8,128)(2,1)S(1)}, bf16[256,1024]{1,0:T(8,128)(2,1)}, u32[]{:S(2)}) %copy-start.3) | copy-done | bytes 524312
  11.0 0.2 turn.1
  11.2 1.6 %collective-permute-start.20 = (bf16[512,256]{1,0:T(8,128)(2,1)S(1)}, bf16[512,256]{1,0:T(8,128)(2,1)S(1)}, u32[]{:S(2)}, u32[]{:S(2)}) collective-permute-start(bf16[512,256]{1,0:T(8,128)(2,1)S(1)} %get-tuple-element.9.refs_4_), channel_id=1, source_target_pairs={{8,0},{16,8},{24,16},{28,24},{20,28},{12,20},{4,12},{0,4},{9,1},{1... | collective-permute-start | bytes 786440 | tf_op jit(solution)/shard_map/ppermute | solution.py:342
  12.7 0.5 collective-permute-start.9
  13.2 1.2 %collective-permute-start.17 = (bf16[512,256]{1,0:T(8,128)(2,1)S(1)}, bf16[512,256]{1,0:T(8,128)(2,1)S(1)}, u32[]{:S(2)}, u32[]{:S(2)}) collective-permute-start(bf16[512,256]{1,0:T(8,128)(2,1)S(1)} %get-tuple-element.10.refs_5_), channel_id=1, source_target_pairs={{0,8},{8,16},{16,24},{24,28},{28,20},{20,12},{12,4},{4,0},{1,9},{9... | collective-permute-start | bytes 786440 | tf_op jit(solution)/shard_map/ppermute | solution.py:342
  14.4 0.8 %collective-permute-start.13 = (bf16[512,256]{1,0:T(8,128)(2,1)S(1)}, bf16[512,256]{1,0:T(8,128)(2,1)S(1)}, u32[]{:S(2)}, u32[]{:S(2)}) collective-permute-start(bf16[512,256]{1,0:T(8,128)(2,1)S(1)} %get-tuple-element.10.refs_5_), channel_id=1, source_target_pairs={{8,0},{16,8},{24,16},{28,24},{20,28},{12,20},{4,12},{0,4},{9,1},{1... | collective-permute-start | bytes 786440 | tf_op jit(solution)/shard_map/ppermute | solution.py:342
  15.3 0.0 collective-permute-done.4
  15.3 1.5 %collective-permute-start.1 = (bf16[512,512]{1,0:T(8,128)(2,1)S(1)}, bf16[512,512]{1,0:T(8,128)(2,1)S(1)}, u32[]{:S(2)}, u32[]{:S(2)}) collective-permute-start(bf16[512,512]{1,0:T(8,128)(2,1)S(1)} %copy-done), channel_id=1, source_target_pairs={{0,2},{2,0},{1,3},{3,1},{4,6},{6,4},{5,7},{7,5},{8,10},{10,8},{9,1... | collective-permute-start | bytes 1572872 | tf_op jit(solution)/shard_map/ppermute | solution.py:22
  16.8 3.6 %collective-permute-done.20.refs_8_ = bf16[512,256]{1,0:T(8,128)(2,1)S(1)} collective-permute-done((bf16[512,256]{1,0:T(8,128)(2,1)S(1)}, bf16[512,256]{1,0:T(8,128)(2,1)S(1)}, u32[]{:S(2)}, u32[]{:S(2)}) %collective-permute-start.20) | collective-permute-done | bytes 262176 | tf_op jit(solution)/shard_map/ppermute | solution.py:342
  20.4 2.6 %collective-permute-start.5 = (bf16[128,512]{1,0:T(8,128)(2,1)S(1)}, bf16[128,512]{1,0:T(8,128)(2,1)S(1)}, u32[]{:S(2)}, u32[]{:S(2)}) collective-permute-start(bf16[128,512]{1,0:T(8,128)(2,1)S(1)} %add_convert_fusion), channel_id=1, source_target_pairs={{0,16},{16,0},{4,20},{20,4},{8,24},{24,8},{12,28},{28,12},{1,17},{... | collective-permute-start | bytes 393224 | tf_op jit(solution)/shard_map/ppermute | solution.py:22
  23.0 0.0 collective-permute-done.9.refs_6_
  23.0 2.1 %collective-permute-done.17.refs_7_ = bf16[512,256]{1,0:T(8,128)(2,1)S(1)} collective-permute-done((bf16[512,256]{1,0:T(8,128)(2,1)S(1)}, bf16[512,256]{1,0:T(8,128)(2,1)S(1)}, u32[]{:S(2)}, u32[]{:S(2)}) %collective-permute-start.17) | collective-permute-done | bytes 262176 | tf_op jit(solution)/shard_map/ppermute | solution.py:342
  25.1 2.2 %collective-permute-start.21 = (bf16[512,256]{1,0:T(8,128)(2,1)S(1)}, bf16[512,256]{1,0:T(8,128)(2,1)S(1)}, u32[]{:S(2)}, u32[]{:S(2)}) collective-permute-start(bf16[512,256]{1,0:T(8,128)(2,1)S(1)} %collective-permute-done.20.refs_8_), channel_id=1, source_target_pairs={{8,0},{16,8},{24,16},{28,24},{20,28},{12,20},{4,12},{0,4},{9,1},{1... | collective-permute-start | bytes 786440 | tf_op jit(solution)/shard_map/ppermute | solution.py:342
  27.2 0.0 collective-permute-done.13.refs_9_
  27.2 2.1 %collective-permute-start.10 = (bf16[512,256]{1,0:T(8,128)(2,1)S(1)}, bf16[512,256]{1,0:T(8,128)(2,1)S(1)}, u32[]{:S(2)}, u32[]{:S(2)}) collective-permute-start(bf16[512,256]{1,0:T(8,128)(2,1)S(1)} %collective-permute-done.9.refs_6_), channel_id=1, source_target_pairs={{0,8},{8,16},{16,24},{24,28},{28,20},{20,12},{12,4},{4,0},{1,9},{9... | collective-permute-start | bytes 786440 | tf_op jit(solution)/shard_map/ppermute | solution.py:342
  29.4 2.5 %collective-permute-done.5 = bf16[128,512]{1,0:T(8,128)(2,1)S(1)} collective-permute-done((bf16[128,512]{1,0:T(8,128)(2,1)S(1)}, bf16[128,512]{1,0:T(8,128)(2,1)S(1)}, u32[]{:S(2)}, u32[]{:S(2)}) %collective-permute-start.5) | collective-permute-done | bytes 131104 | tf_op jit(solution)/shard_map/ppermute | solution.py:22
  31.9 0.5 collective-permute-start.18
  32.4 1.8 %collective-permute-done.21.refs_6_.refs_12_ = bf16[512,256]{1,0:T(8,128)(2,1)S(1)} collective-permute-done((bf16[512,256]{1,0:T(8,128)(2,1)S(1)}, bf16[512,256]{1,0:T(8,128)(2,1)S(1)}, u32[]{:S(2)}, u32[]{:S(2)}) %collective-permute-start.21) | collective-permute-done | bytes 262176 | tf_op jit(solution)/shard_map/ppermute | solution.py:342
  34.2 6.0 %collective-permute-start.14 = (bf16[512,256]{1,0:T(8,128)(2,1)S(1)}, bf16[512,256]{1,0:T(8,128)(2,1)S(1)}, u32[]{:S(2)}, u32[]{:S(2)}) collective-permute-start(bf16[512,256]{1,0:T(8,128)(2,1)S(1)} %collective-permute-done.13.refs_9_), channel_id=1, source_target_pairs={{8,0},{16,8},{24,16},{28,24},{20,28},{12,20},{4,12},{0,4},{9,1},{1... | collective-permute-start | bytes 786440 | tf_op jit(solution)/shard_map/ppermute | solution.py:342
  40.2 0.0 collective-permute-done.10.refs_4_.refs_10_
  40.2 1.5 %collective-permute-start.7 = (bf16[384,512]{1,0:T(8,128)(2,1)S(1)}, bf16[384,512]{1,0:T(8,128)(2,1)S(1)}, u32[]{:S(2)}, u32[]{:S(2)}) collective-permute-start(bf16[384,512]{1,0:T(8,128)(2,1)S(1)} %constant_dynamic-update-slice_fusion.refs_0_.refs_4_), channel_id=1, source_target_pairs={{0,2},{2,0},{1,3},{3,1},{4,6},{6,4},{5,7},{7,5},{8,10},{10,8},{9,1... | collective-permute-start | bytes 1179656 | tf_op jit(solution)/shard_map/ppermute | solution.py:22
  41.7 0.0 collective-permute-done.1.refs_2_
  41.7 0.0 collective-permute-start.2
  41.7 0.0 collective-permute-done.18.refs_5_.refs_11_
  41.7 2.5 %collective-permute-start.22 = (bf16[512,256]{1,0:T(8,128)(2,1)S(1)}, bf16[512,256]{1,0:T(8,128)(2,1)S(1)}, u32[]{:S(2)}, u32[]{:S(2)}) collective-permute-start(bf16[512,256]{1,0:T(8,128)(2,1)S(1)} %collective-permute-done.21.refs_6_.refs_12_), channel_id=1, source_target_pairs={{8,0},{16,8},{24,16},{28,24},{20,28},{12,20},{4,12},{0,4},{9,1},{1... | collective-permute-start | bytes 786440 | tf_op jit(solution)/shard_map/ppermute | solution.py:342
  44.2 2.4 %collective-permute-start.11 = (bf16[512,256]{1,0:T(8,128)(2,1)S(1)}, bf16[512,256]{1,0:T(8,128)(2,1)S(1)}, u32[]{:S(2)}, u32[]{:S(2)}) collective-permute-start(bf16[512,256]{1,0:T(8,128)(2,1)S(1)} %collective-permute-done.10.refs_4_.refs_10_), channel_id=1, source_target_pairs={{0,8},{8,16},{16,24},{24,28},{28,20},{20,12},{12,4},{4,0},{1,9},{9... | collective-permute-start | bytes 786440 | tf_op jit(solution)/shard_map/ppermute | solution.py:342
  46.6 1.4 %collective-permute-start.15 = (bf16[512,256]{1,0:T(8,128)(2,1)S(1)}, bf16[512,256]{1,0:T(8,128)(2,1)S(1)}, u32[]{:S(2)}, u32[]{:S(2)}) collective-permute-start(bf16[512,256]{1,0:T(8,128)(2,1)S(1)} %collective-permute-done.14.refs_7_.refs_13_), channel_id=1, source_target_pairs={{8,0},{16,8},{24,16},{28,24},{20,28},{12,20},{4,12},{0,4},{9,1},{1... | collective-permute-start | bytes 786440 | tf_op jit(solution)/shard_map/ppermute | solution.py:342
  48.0 0.0 collective-permute-done.7.refs_2_.refs_6_
  48.0 0.0 collective-permute-start.6
  48.0 2.9 %collective-permute-done.22.refs_6_.refs_16_ = bf16[512,256]{1,0:T(8,128)(2,1)S(1)} collective-permute-done((bf16[512,256]{1,0:T(8,128)(2,1)S(1)}, bf16[512,256]{1,0:T(8,128)(2,1)S(1)}, u32[]{:S(2)}, u32[]{:S(2)}) %collective-permute-start.22) | collective-permute-done | bytes 262176 | tf_op jit(solution)/shard_map/ppermute | solution.py:342
  50.9 0.0 collective-permute-start.8
  50.9 1.7 %collective-permute-done.11.refs_4_.refs_14_ = bf16[512,256]{1,0:T(8,128)(2,1)S(1)} collective-permute-done((bf16[512,256]{1,0:T(8,128)(2,1)S(1)}, bf16[512,256]{1,0:T(8,128)(2,1)S(1)}, u32[]{:S(2)}, u32[]{:S(2)}) %collective-permute-start.11) | collective-permute-done | bytes 262176 | tf_op jit(solution)/shard_map/ppermute | solution.py:342
  52.6 0.4 collective-permute-start.19
  53.0 3.0 %collective-permute-done.15.refs_7_.refs_17_ = bf16[512,256]{1,0:T(8,128)(2,1)S(1)} collective-permute-done((bf16[512,256]{1,0:T(8,128)(2,1)S(1)}, bf16[512,256]{1,0:T(8,128)(2,1)S(1)}, u32[]{:S(2)}, u32[]{:S(2)}) %collective-permute-start.15) | collective-permute-done | bytes 262176 | tf_op jit(solution)/shard_map/ppermute | solution.py:342
  56.0 0.5 collective-permute-start.12
  56.5 2.0 %collective-permute-start.16 = (bf16[512,256]{1,0:T(8,128)(2,1)S(1)}, bf16[512,256]{1,0:T(8,128)(2,1)S(1)}, u32[]{:S(2)}, u32[]{:S(2)}) collective-permute-start(bf16[512,256]{1,0:T(8,128)(2,1)S(1)} %collective-permute-done.15.refs_7_.refs_17_), channel_id=1, source_target_pairs={{8,0},{16,8},{24,16},{28,24},{20,28},{12,20},{4,12},{0,4},{9,1},{1... | collective-permute-start | bytes 786440 | tf_op jit(solution)/shard_map/ppermute | solution.py:342
  58.5 1.9 %prepare.1 = (bf16[16,256,256]{2,1,0:T(8,128)(2,1)S(1)}, bf16[16,512,256]{2,1,0:T(8,128)(2,1)S(1)}) custom-call(bf16[512,128]{1,0:T(8,128)(2,1)S(1)} %copy-done.2, bf16[512,128]{1,0:T(8,128)(2,1)S(1)} %copy-done.4, f32[13,16,512]{2,1,0:T(8,128)S(1)} %copy-done.1), custom_call_target="tpu_custom_call" | custom-call | tf_op jit(solution)/shard_map/prepare/pallas_call | solution.py:127
  60.4 1.2 %shard_map.55.refs_8_ = f32[1024,512]{1,0:T(8,128)S(1)} custom-call(bf16[512,512]{1,0:T(8,128)(2,1)S(1)} %copy-done, bf16[512,512]{1,0:T(8,128)(2,1)S(1)} %collective-permute-done.refs_1_, bf16[512,512]{1,0:T(8,128)(2,1)S(1)} %collective-permute-done.1.refs_2_, bf16[512,512]{1,0:T(8,128)(2,1)S(1)} %collective-permute-done.2.refs_3_, ...), custom_call_target="tpu_custom_call" | custom-call | tf_op jit(solution)/shard_map/pallas_call | solution.py:209
  61.6 0.9 %shard_map.56.refs_8_ = f32[1024,512]{1,0:T(8,128)S(1)} custom-call(bf16[512,512]{1,0:T(8,128)(2,1)S(1)} %copy-done, bf16[512,512]{1,0:T(8,128)(2,1)S(1)} %collective-permute-done.refs_1_, bf16[512,512]{1,0:T(8,128)(2,1)S(1)} %collective-permute-done.1.refs_2_, bf16[512,512]{1,0:T(8,128)(2,1)S(1)} %collective-permute-done.2.refs_3_, ...), custom_call_target="tpu_custom_call" | custom-call | tf_op jit(solution)/shard_map/pallas_call | solution.py:209
  62.4 0.0 collective-permute-done.19.refs_5_.refs_15_
  62.5 0.9 %shard_map.57.refs_10_ = f32[1024,512]{1,0:T(8,128)S(1)} custom-call(bf16[512,512]{1,0:T(8,128)(2,1)S(1)} %copy-done, bf16[512,512]{1,0:T(8,128)(2,1)S(1)} %collective-permute-done.refs_1_, bf16[512,512]{1,0:T(8,128)(2,1)S(1)} %collective-permute-done.1.refs_2_, bf16[512,512]{1,0:T(8,128)(2,1)S(1)} %collective-permute-done.2.refs_3_, ...), custom_call_target="tpu_custom_call" | custom-call | tf_op jit(solution)/shard_map/pallas_call | solution.py:209
  63.3 2.4 %shard_map.58.refs_11_ = f32[1024,384]{1,0:T(8,128)S(1)} custom-call(bf16[384,512]{1,0:T(8,128)(2,1)S(1)} %constant_dynamic-update-slice_fusion.refs_0_.refs_4_, bf16[384,512]{1,0:T(8,128)(2,1)S(1)} %collective-permute-done.6.refs_1_.refs_5_, bf16[384,512]{1,0:T(8,128)(2,1)S(1)} %collective-permute-done.7.refs_2_.refs_6_, ...), custom_call_target="tpu_custom_call" | custom-call | tf_op jit(solution)/shard_map/pallas_call | solution.py:209
  65.8 0.5 collective-permute-done.12.refs_8_
  66.2 4.9 %finish.1 = bf16[512,1024]{1,0:T(8,128)(2,1)} custom-call(bf16[512,512]{1,0:T(8,128)(2,1)S(1)} %copy-done, bf16[512,512]{1,0:T(8,128)(2,1)S(1)} %collective-permute-done.refs_1_, bf16[512,512]{1,0:T(8,128)(2,1)S(1)} %collective-permute-done.1.refs_2_, bf16[512,512]{1,0:T(8,128)(2,1)S(1)} %collective-permute-done.2.refs_3_, ...), custom_call_target="tpu_custom_call" | custom-call | tf_op jit(solution)/shard_map/finish/pallas_call | solution.py:297
  (21 shorter events, 0.1 us)
Async XLA Ops:
  0.0 15.3 %copy-start = (bf16[512,512]{1,0:T(8,128)(2,1)S(1)}, bf16[512,512]{1,0:T(8,128)(2,1)}, u32[]{:S(2)}) copy-start(bf16[512,512]{1,0:T(8,128)(2,1)} %refs_0_.7) | copy-start | bytes 1572868
  0.0 58.5 %copy-start.4 = (bf16[512,128]{1,0:T(8,128)(2,1)S(1)}, bf16[512,128]{1,0:T(8,128)(2,1)}, u32[]{:S(2)}) copy-start(bf16[512,128]{1,0:T(8,128)(2,1)} %k_ref.1) | copy-start | bytes 393220
  0.0 58.5 %copy-start.1 = (f32[13,16,512]{2,1,0:T(8,128)S(1)}, f32[13,16,512]{2,1,0:T(8,128)}, u32[]{:S(2)}) copy-start(f32[13,16,512]{2,1,0:T(8,128)} %refs_13_.1) | copy-start | bytes 1277956
  0.0 58.5 %copy-start.2 = (bf16[512,128]{1,0:T(8,128)(2,1)S(1)}, bf16[512,128]{1,0:T(8,128)(2,1)}, u32[]{:S(2)}) copy-start(bf16[512,128]{1,0:T(8,128)(2,1)} %refs_12_.1) | copy-start | bytes 393220
  1.5 6.6 %collective-permute-start.3 = (bf16[128,512]{1,0:T(8,128)(2,1)S(1)}, bf16[128,512]{1,0:T(8,128)(2,1)S(1)}, u32[]{:S(2)}, u32[]{:S(2)}) collective-permute-start(bf16[128,512]{1,0:T(8,128)(2,1)S(1)} %get-tuple-element.13), channel_id=1, source_target_pairs={{0,4},{4,0},{8,12},{12,8},{16,20},{20,16},{24,28},{28,24},{1,5},{5... | collective-permute-start | bytes 393224 | tf_op jit(solution)/shard_map/ppermute | solution.py:22
  8.1 7.2 %collective-permute-start.4 = (bf16[128,512]{1,0:T(8,128)(2,1)S(1)}, bf16[128,512]{1,0:T(8,128)(2,1)S(1)}, u32[]{:S(2)}, u32[]{:S(2)}) collective-permute-start(bf16[128,512]{1,0:T(8,128)(2,1)S(1)} %fusion), channel_id=1, source_target_pairs={{0,8},{8,0},{4,12},{12,4},{16,24},{24,16},{20,28},{28,20},{1,9},{9... | collective-permute-start | bytes 393224 | tf_op jit(solution)/shard_map/ppermute | solution.py:22
  9.9 1.0 %copy-start.3 = (bf16[256,1024]{1,0:T(8,128)(2,1)S(1)}, bf16[256,1024]{1,0:T(8,128)(2,1)}, u32[]{:S(2)}) copy-start(bf16[256,1024]{1,0:T(8,128)(2,1)} %weight_ref.1) | copy-start | bytes 1572868
  11.2 9.2 %collective-permute-start.20 = (bf16[512,256]{1,0:T(8,128)(2,1)S(1)}, bf16[512,256]{1,0:T(8,128)(2,1)S(1)}, u32[]{:S(2)}, u32[]{:S(2)}) collective-permute-start(bf16[512,256]{1,0:T(8,128)(2,1)S(1)} %get-tuple-element.9.refs_4_), channel_id=1, source_target_pairs={{8,0},{16,8},{24,16},{28,24},{20,28},{12,20},{4,12},{0,4},{9,1},{1... | collective-permute-start | bytes 786440 | tf_op jit(solution)/shard_map/ppermute | solution.py:342
  12.7 10.3 %collective-permute-start.9 = (bf16[512,256]{1,0:T(8,128)(2,1)S(1)}, bf16[512,256]{1,0:T(8,128)(2,1)S(1)}, u32[]{:S(2)}, u32[]{:S(2)}) collective-permute-start(bf16[512,256]{1,0:T(8,128)(2,1)S(1)} %get-tuple-element.9.refs_4_), channel_id=1, source_target_pairs={{0,8},{8,16},{16,24},{24,28},{28,20},{20,12},{12,4},{4,0},{1,9},{9... | collective-permute-start | bytes 786440 | tf_op jit(solution)/shard_map/ppermute | solution.py:342
  13.2 11.8 %collective-permute-start.17 = (bf16[512,256]{1,0:T(8,128)(2,1)S(1)}, bf16[512,256]{1,0:T(8,128)(2,1)S(1)}, u32[]{:S(2)}, u32[]{:S(2)}) collective-permute-start(bf16[512,256]{1,0:T(8,128)(2,1)S(1)} %get-tuple-element.10.refs_5_), channel_id=1, source_target_pairs={{0,8},{8,16},{16,24},{24,28},{28,20},{20,12},{12,4},{4,0},{1,9},{9... | collective-permute-start | bytes 786440 | tf_op jit(solution)/shard_map/ppermute | solution.py:342
  14.4 12.8 %collective-permute-start.13 = (bf16[512,256]{1,0:T(8,128)(2,1)S(1)}, bf16[512,256]{1,0:T(8,128)(2,1)S(1)}, u32[]{:S(2)}, u32[]{:S(2)}) collective-permute-start(bf16[512,256]{1,0:T(8,128)(2,1)S(1)} %get-tuple-element.10.refs_5_), channel_id=1, source_target_pairs={{8,0},{16,8},{24,16},{28,24},{20,28},{12,20},{4,12},{0,4},{9,1},{1... | collective-permute-start | bytes 786440 | tf_op jit(solution)/shard_map/ppermute | solution.py:342
  15.3 26.4 %collective-permute-start.1 = (bf16[512,512]{1,0:T(8,128)(2,1)S(1)}, bf16[512,512]{1,0:T(8,128)(2,1)S(1)}, u32[]{:S(2)}, u32[]{:S(2)}) collective-permute-start(bf16[512,512]{1,0:T(8,128)(2,1)S(1)} %copy-done), channel_id=1, source_target_pairs={{0,2},{2,0},{1,3},{3,1},{4,6},{6,4},{5,7},{7,5},{8,10},{10,8},{9,1... | collective-permute-start | bytes 1572872 | tf_op jit(solution)/shard_map/ppermute | solution.py:22
  20.4 11.5 %collective-permute-start.5 = (bf16[128,512]{1,0:T(8,128)(2,1)S(1)}, bf16[128,512]{1,0:T(8,128)(2,1)S(1)}, u32[]{:S(2)}, u32[]{:S(2)}) collective-permute-start(bf16[128,512]{1,0:T(8,128)(2,1)S(1)} %add_convert_fusion), channel_id=1, source_target_pairs={{0,16},{16,0},{4,20},{20,4},{8,24},{24,8},{12,28},{28,12},{1,17},{... | collective-permute-start | bytes 393224 | tf_op jit(solution)/shard_map/ppermute | solution.py:22
  23.0 23.6 %collective-permute-start = (bf16[512,512]{1,0:T(8,128)(2,1)S(1)}, bf16[512,512]{1,0:T(8,128)(2,1)S(1)}, u32[]{:S(2)}, u32[]{:S(2)}) collective-permute-start(bf16[512,512]{1,0:T(8,128)(2,1)S(1)} %copy-done), channel_id=1, source_target_pairs={{0,1},{1,0},{2,3},{3,2},{4,5},{5,4},{6,7},{7,6},{8,9},{9,8},{10,11... | collective-permute-start | bytes 1572872 | tf_op jit(solution)/shard_map/ppermute | solution.py:22
  25.1 9.1 %collective-permute-start.21 = (bf16[512,256]{1,0:T(8,128)(2,1)S(1)}, bf16[512,256]{1,0:T(8,128)(2,1)S(1)}, u32[]{:S(2)}, u32[]{:S(2)}) collective-permute-start(bf16[512,256]{1,0:T(8,128)(2,1)S(1)} %collective-permute-done.20.refs_8_), channel_id=1, source_target_pairs={{8,0},{16,8},{24,16},{28,24},{20,28},{12,20},{4,12},{0,4},{9,1},{1... | collective-permute-start | bytes 786440 | tf_op jit(solution)/shard_map/ppermute | solution.py:342
  27.2 12.9 %collective-permute-start.10 = (bf16[512,256]{1,0:T(8,128)(2,1)S(1)}, bf16[512,256]{1,0:T(8,128)(2,1)S(1)}, u32[]{:S(2)}, u32[]{:S(2)}) collective-permute-start(bf16[512,256]{1,0:T(8,128)(2,1)S(1)} %collective-permute-done.9.refs_6_), channel_id=1, source_target_pairs={{0,8},{8,16},{16,24},{24,28},{28,20},{20,12},{12,4},{4,0},{1,9},{9... | collective-permute-start | bytes 786440 | tf_op jit(solution)/shard_map/ppermute | solution.py:342
  31.9 9.8 %collective-permute-start.18 = (bf16[512,256]{1,0:T(8,128)(2,1)S(1)}, bf16[512,256]{1,0:T(8,128)(2,1)S(1)}, u32[]{:S(2)}, u32[]{:S(2)}) collective-permute-start(bf16[512,256]{1,0:T(8,128)(2,1)S(1)} %collective-permute-done.17.refs_7_), channel_id=1, source_target_pairs={{0,8},{8,16},{16,24},{24,28},{28,20},{20,12},{12,4},{4,0},{1,9},{9... | collective-permute-start | bytes 786440 | tf_op jit(solution)/shard_map/ppermute | solution.py:342
  34.2 10.0 %collective-permute-start.14 = (bf16[512,256]{1,0:T(8,128)(2,1)S(1)}, bf16[512,256]{1,0:T(8,128)(2,1)S(1)}, u32[]{:S(2)}, u32[]{:S(2)}) collective-permute-start(bf16[512,256]{1,0:T(8,128)(2,1)S(1)} %collective-permute-done.13.refs_9_), channel_id=1, source_target_pairs={{8,0},{16,8},{24,16},{28,24},{20,28},{12,20},{4,12},{0,4},{9,1},{1... | collective-permute-start | bytes 786440 | tf_op jit(solution)/shard_map/ppermute | solution.py:342
  40.2 7.9 %collective-permute-start.7 = (bf16[384,512]{1,0:T(8,128)(2,1)S(1)}, bf16[384,512]{1,0:T(8,128)(2,1)S(1)}, u32[]{:S(2)}, u32[]{:S(2)}) collective-permute-start(bf16[384,512]{1,0:T(8,128)(2,1)S(1)} %constant_dynamic-update-slice_fusion.refs_0_.refs_4_), channel_id=1, source_target_pairs={{0,2},{2,0},{1,3},{3,1},{4,6},{6,4},{5,7},{7,5},{8,10},{10,8},{9,1... | collective-permute-start | bytes 1179656 | tf_op jit(solution)/shard_map/ppermute | solution.py:22
  41.7 14.8 %collective-permute-start.2 = (bf16[512,512]{1,0:T(8,128)(2,1)S(1)}, bf16[512,512]{1,0:T(8,128)(2,1)S(1)}, u32[]{:S(2)}, u32[]{:S(2)}) collective-permute-start(bf16[512,512]{1,0:T(8,128)(2,1)S(1)} %collective-permute-done.1.refs_2_), channel_id=1, source_target_pairs={{0,1},{1,0},{2,3},{3,2},{4,5},{5,4},{6,7},{7,6},{8,9},{9,8},{10,11... | collective-permute-start | bytes 1572872 | tf_op jit(solution)/shard_map/ppermute | solution.py:22
  41.7 9.2 %collective-permute-start.22 = (bf16[512,256]{1,0:T(8,128)(2,1)S(1)}, bf16[512,256]{1,0:T(8,128)(2,1)S(1)}, u32[]{:S(2)}, u32[]{:S(2)}) collective-permute-start(bf16[512,256]{1,0:T(8,128)(2,1)S(1)} %collective-permute-done.21.refs_6_.refs_12_), channel_id=1, source_target_pairs={{8,0},{16,8},{24,16},{28,24},{20,28},{12,20},{4,12},{0,4},{9,1},{1... | collective-permute-start | bytes 786440 | tf_op jit(solution)/shard_map/ppermute | solution.py:342
  44.2 8.4 %collective-permute-start.11 = (bf16[512,256]{1,0:T(8,128)(2,1)S(1)}, bf16[512,256]{1,0:T(8,128)(2,1)S(1)}, u32[]{:S(2)}, u32[]{:S(2)}) collective-permute-start(bf16[512,256]{1,0:T(8,128)(2,1)S(1)} %collective-permute-done.10.refs_4_.refs_10_), channel_id=1, source_target_pairs={{0,8},{8,16},{16,24},{24,28},{28,20},{20,12},{12,4},{4,0},{1,9},{9... | collective-permute-start | bytes 786440 | tf_op jit(solution)/shard_map/ppermute | solution.py:342
  46.6 9.4 %collective-permute-start.15 = (bf16[512,256]{1,0:T(8,128)(2,1)S(1)}, bf16[512,256]{1,0:T(8,128)(2,1)S(1)}, u32[]{:S(2)}, u32[]{:S(2)}) collective-permute-start(bf16[512,256]{1,0:T(8,128)(2,1)S(1)} %collective-permute-done.14.refs_7_.refs_13_), channel_id=1, source_target_pairs={{8,0},{16,8},{24,16},{28,24},{20,28},{12,20},{4,12},{0,4},{9,1},{1... | collective-permute-start | bytes 786440 | tf_op jit(solution)/shard_map/ppermute | solution.py:342
  48.0 15.3 %collective-permute-start.6 = (bf16[384,512]{1,0:T(8,128)(2,1)S(1)}, bf16[384,512]{1,0:T(8,128)(2,1)S(1)}, u32[]{:S(2)}, u32[]{:S(2)}) collective-permute-start(bf16[384,512]{1,0:T(8,128)(2,1)S(1)} %constant_dynamic-update-slice_fusion.refs_0_.refs_4_), channel_id=1, source_target_pairs={{0,1},{1,0},{2,3},{3,2},{4,5},{5,4},{6,7},{7,6},{8,9},{9,8},{10,11... | collective-permute-start | bytes 1179656 | tf_op jit(solution)/shard_map/ppermute | solution.py:22
  50.9 12.4 %collective-permute-start.8 = (bf16[384,512]{1,0:T(8,128)(2,1)S(1)}, bf16[384,512]{1,0:T(8,128)(2,1)S(1)}, u32[]{:S(2)}, u32[]{:S(2)}) collective-permute-start(bf16[384,512]{1,0:T(8,128)(2,1)S(1)} %collective-permute-done.7.refs_2_.refs_6_), channel_id=1, source_target_pairs={{0,1},{1,0},{2,3},{3,2},{4,5},{5,4},{6,7},{7,6},{8,9},{9,8},{10,11... | collective-permute-start | bytes 1179656 | tf_op jit(solution)/shard_map/ppermute | solution.py:22
  52.6 9.8 %collective-permute-start.19 = (bf16[512,256]{1,0:T(8,128)(2,1)S(1)}, bf16[512,256]{1,0:T(8,128)(2,1)S(1)}, u32[]{:S(2)}, u32[]{:S(2)}) collective-permute-start(bf16[512,256]{1,0:T(8,128)(2,1)S(1)} %collective-permute-done.18.refs_5_.refs_11_), channel_id=1, source_target_pairs={{0,8},{8,16},{16,24},{24,28},{28,20},{20,12},{12,4},{4,0},{1,9},{9... | collective-permute-start | bytes 786440 | tf_op jit(solution)/shard_map/ppermute | solution.py:342
  56.0 10.2 %collective-permute-start.12 = (bf16[512,256]{1,0:T(8,128)(2,1)S(1)}, bf16[512,256]{1,0:T(8,128)(2,1)S(1)}, u32[]{:S(2)}, u32[]{:S(2)}) collective-permute-start(bf16[512,256]{1,0:T(8,128)(2,1)S(1)} %collective-permute-done.11.refs_4_.refs_14_), channel_id=1, source_target_pairs={{0,8},{8,16},{16,24},{24,28},{28,20},{20,12},{12,4},{4,0},{1,9},{9... | collective-permute-start | bytes 786440 | tf_op jit(solution)/shard_map/ppermute | solution.py:342
  56.5 9.8 %collective-permute-start.16 = (bf16[512,256]{1,0:T(8,128)(2,1)S(1)}, bf16[512,256]{1,0:T(8,128)(2,1)S(1)}, u32[]{:S(2)}, u32[]{:S(2)}) collective-permute-start(bf16[512,256]{1,0:T(8,128)(2,1)S(1)} %collective-permute-done.15.refs_7_.refs_17_), channel_id=1, source_target_pairs={{8,0},{16,8},{24,16},{28,24},{20,28},{12,20},{4,12},{0,4},{9,1},{1... | collective-permute-start | bytes 786440 | tf_op jit(solution)/shard_map/ppermute | solution.py:342

commit v3 on v2

--- a/solution.py
+++ b/solution.py
@@ -48,18 +48,15 @@
     return jnp.broadcast_to(row, (count, row.shape[1]))
 
 
-def prepare_kernel(q_ref, k_ref, w_ref, *rest):
-    near_refs, (score_ref, row_ref) = rest[:-2], rest[-2:]
+def prepare_kernel(q_ref, k_ref, w_ref, near_ref, score_ref, row_ref):
     length = q_ref.shape[0]
-    heads = w_ref.shape[1]
-    rows = near_refs[0].shape[2]
+    heads, _, rows = near_ref.shape
     tile = min(128, length)
     sub = 8
     tile_levels = tile.bit_length() - 1
     sub_levels = sub.bit_length() - 1
-    score_ref[...] = dot_last(k_ref[...], q_ref[...]).astype(BF16).astype(F32)
-
-    for num in range(length.bit_length()):
+    score_ref[...] = dot_last(k_ref[...], q_ref[...]).astype(BF16)
+    for num in range(rows.bit_length()):
         for head in range(heads):
             row_ref[head, num : num + 1, :] = w_ref[num, head : head + 1, :] * level_scale(num)
 
@@ -81,21 +78,17 @@
     )
 
     def one_head(head, carry):
-        for t_tile in range(length // tile):
-            t0 = t_tile * tile
-            block = t0 // rows
-            near_ref = near_refs[block]
-            c0 = t0 - block * rows
+        for t0 in range(0, length, tile):
+            base = t0 // rows * rows
             weight_rows = [
-                row_ref[head, num : num + 1, t0 : t0 + tile]
-                for num in range(length.bit_length())
+                row_ref[head, num : num + 1, t0 : t0 + tile] for num in range(rows.bit_length())
             ]
-            for s_tile in range((block + 1) * rows // tile):
-                s0 = s_tile * tile
-                if s_tile > t_tile:
-                    near_ref[head, s0 : s0 + tile, c0 : c0 + tile] = jnp.zeros((tile, tile), BF16)
+            for s0 in range(base, base + rows, tile):
+                place_at = (head, pl.ds(s0, tile), pl.ds(t0 - base, tile))
+                if s0 > t0:
+                    near_ref[place_at] = jnp.zeros((tile, tile), BF16)
                     continue
-                if s_tile == t_tile:
+                if s0 == t0:
                     small = jnp.zeros((sub, tile), F32)
                     for num in range(sub_levels + 1):
                         small = jnp.where(fine == num, spread_rows(weight_rows[num], sub), small)
@@ -111,10 +104,10 @@
                     )
                     weight = jnp.where(near_diag, jnp.concatenate([small] * (tile // sub), 0), big)
                 else:
-                    num = tile_levels + (s_tile ^ t_tile).bit_length()
+                    num = tile_levels + (s0 // tile ^ t0 // tile).bit_length()
                     weight = spread_rows(weight_rows[num], tile)
-                score = score_ref[s0 : s0 + tile, t0 : t0 + tile]
-                near_ref[head, s0 : s0 + tile, c0 : c0 + tile] = (weight * score).astype(BF16)
+                score = score_ref[s0 : s0 + tile, t0 : t0 + tile].astype(F32)
+                near_ref[place_at] = (weight * score).astype(BF16)
         return carry
 
     lax.fori_loop(0, heads, one_head, 0)
@@ -127,31 +120,36 @@
     return pl.pallas_call(
         prepare_kernel,
         out_shape=[
-            pltpu.VMEM((heads, (block + 1) * rows, rows), BF16) for block in range(length // rows)
+            pltpu.VMEM((heads, length, rows), BF16),
+            pltpu.VMEM((length, length), BF16),
         ],
-        scratch_shapes=[
-            pltpu.VMEM((length, length), F32),
-            pltpu.VMEM((heads, length.bit_length(), length), F32),
-        ],
+        scratch_shapes=[pltpu.VMEM((heads, rows.bit_length(), length), F32)],
         compiler_params=pltpu.CompilerParams(vmem_limit_bytes=16 << 20),
         name="prepare",
     )(queries, key_vectors, level_weight)
 
 
-def turn_kernel(weight_ref, *half_refs):
-    share = half_refs[0].shape[0]
-    for num, half_ref in enumerate(half_refs):
-        half_ref[...] = weight_ref[:, num * share : (num + 1) * share].T
-
-
-def turn(weight, split):
+def begin_kernel(k_ref, token_ref, weight_ref, sum_ref, sent_ref, *part_refs):
+    total = lax.dot_general(
+        k_ref[...], token_ref[...], (((0,), (0,)), ((), ())), preferred_element_type=F32
+    )
+    sum_ref[...] = total
+    sent_ref[...] = total.astype(BF16)
+    share = part_refs[0].shape[0]
+    for num, part_ref in enumerate(part_refs):
+        part_ref[...] = weight_ref[:, num * share : (num + 1) * share].T
+
+
+def begin(key_vectors, tokens, weight, split):
     depth, width = weight.shape
+    shape = (key_vectors.shape[1], tokens.shape[1])
     return pl.pallas_call(
-        turn_kernel,
-        out_shape=[pltpu.VMEM((width // split, depth), weight.dtype)] * split,
+        begin_kernel,
+        out_shape=[pltpu.VMEM(shape, F32), pltpu.VMEM(shape, BF16)]
+        + [pltpu.VMEM((width // split, depth), weight.dtype)] * split,
         compiler_params=pltpu.CompilerParams(vmem_limit_bytes=8 << 20),
-        name="turn",
-    )(weight)
+        name="begin",
+    )(key_vectors, tokens, weight)
 
 
 def ring_order(count):
@@ -170,18 +168,28 @@
 
 def choose(offsets, pieces, depth, chosen_ref):
     for num, offset in enumerate(offsets):
-        piece, start = place(offset, depth, pieces[0].shape[1])
+        piece, start = place(offset, depth, pieces[0][0].shape[1])
         start = pl.multiple_of(start, 128)
-        for index, ref in enumerate(pieces):
+        for index, parts in enumerate(pieces):
 
             @pl.when(piece == index)
             def _():
-                chosen_ref[:, num * depth : (num + 1) * depth] = ref[:, pl.ds(start, depth)]
-
-
-def extend_kernel(piece_count, offsets, split, started, *refs):
+                row = 0
+                for ref in parts:
+                    rows = ref.shape[0]
+                    chosen_ref[row : row + rows, num * depth : (num + 1) * depth] = ref[
+                        :, pl.ds(start, depth)
+                    ]
+                    row += rows
+
+
+def in_parts(refs, count):
+    return [refs[num : num + count] for num in range(0, len(refs), count)]
+
+
+def extend_kernel(piece_count, parts, offsets, split, started, *refs):
     count = len(offsets)
-    pieces = refs[:piece_count]
+    pieces = in_parts(refs[:piece_count], parts)
     blocks = [refs[piece_count + num * split :][:split] for num in range(count)]
     out_ref, chosen_ref = refs[-2], refs[-1]
     share, depth = blocks[0][0].shape
@@ -203,11 +211,14 @@
     offsets = tuple(offset for offset, _ in parts)
     blocks = [half for _, block in parts for half in block]
     split = len(parts[0][1])
-    rows = pieces[0].shape[0]
+    rows = sum(part.shape[0] for part in pieces[0])
     share, depth = blocks[0].shape
-    arrays = [*pieces, *blocks, *([] if total is None else [total])]
+    flat = [part for piece in pieces for part in piece]
+    arrays = [*flat, *blocks, *([] if total is None else [total])]
     return pl.pallas_call(
-        functools.partial(extend_kernel, len(pieces), offsets, split, total is not None),
+        functools.partial(
+            extend_kernel, len(flat), len(pieces[0]), offsets, split, total is not None
+        ),
         in_specs=[pl.BlockSpec(memory_space=pltpu.VMEM)] * len(arrays),
         out_shape=pltpu.VMEM((share * split, rows), F32),
         scratch_shapes=[pltpu.VMEM((rows, depth * len(parts)), BF16)],
@@ -215,24 +226,22 @@
     )(*arrays)
 
 
-def finish_kernel(piece_count, offset, last_count, near_count, head_size, *refs):
+def finish_kernel(piece_count, sum_parts, offset, last_count, head_size, *refs):
     refs = list(refs)
     take = lambda count: [refs.pop(0) for _ in range(count)]
-    token_refs, sum_refs = take(piece_count), take(piece_count)
+    token_refs, sum_refs = take(piece_count), take(piece_count * sum_parts)
     last_refs = take(last_count)
-    value_ref, state_ref, q_ref, w_ref = take(4)
-    near_refs = take(near_count)
-    out_ref = refs.pop(0)
+    value_ref, state_ref, q_ref, w_ref, near_ref, score_ref, out_ref = take(7)
     length, state_rows = q_ref.shape
     width = value_ref.shape[0]
     near_levels = length.bit_length()
     far_levels = w_ref.shape[0] - near_levels
-    rows = length // near_count
+    rows = near_ref.shape[2]
     if last_count:
         token_chosen, sum_chosen = refs
         depth = token_chosen.shape[1]
-        choose([offset], token_refs, depth, token_chosen)
-        choose([offset], sum_refs, depth, sum_chosen)
+        choose([offset], in_parts(token_refs, 1), depth, token_chosen)
+        choose([offset], in_parts(sum_refs, sum_parts), depth, sum_chosen)
     mine = lax.axis_index("ctx")
     queries = q_ref[...]
     twice = jnp.concatenate([queries, queries], axis=1)
@@ -250,6 +259,18 @@
             states = states + dot_last(left, sum_chosen[...])
         values = values.astype(BF16)
         heads = range(c0 // head_size, (c0 + step) // head_size)
+
+        def weight(level, low, high):
+            return jnp.concatenate(
+                [
+                    spread_rows(
+                        w_ref[level, head : head + 1, low:high] * level_scale(level), head_size
+                    )
+                    for head in heads
+                ],
+                axis=0,
+            )
+
         far = None
         for num in range(far_levels):
             state = states[:, num * state_rows : (num + 1) * state_rows]
@@ -257,45 +278,49 @@
             high = state.astype(BF16)
             low = (state - high.astype(F32)).astype(BF16)
             reading = dot_last(jnp.concatenate([high, low], axis=1), twice)
-            level = near_levels + num
-            weight = jnp.concatenate(
-                [
-                    spread_rows(w_ref[level, head : head + 1, :] * level_scale(level), head_size)
-                    for head in heads
-                ],
-                axis=0,
-            )
-            far = weight * reading if far is None else far + weight * reading
-        for block, near_ref in enumerate(near_refs):
-            near = jnp.concatenate(
+            reading = weight(near_levels + num, 0, length) * reading
+            far = reading if far is None else far + reading
+        for t0 in range(0, length, rows):
+            total = far[:, t0 : t0 + rows] + jnp.concatenate(
                 [
                     jnp.dot(
-                        values[
-                            head * head_size - c0 : (head + 1) * head_size - c0,
-                            : (block + 1) * rows,
-                        ],
-                        near_ref[head],
+                        values[head * head_size - c0 : (head + 1) * head_size - c0, t0 : t0 + rows],
+                        near_ref[head, t0 : t0 + rows, :],
                         preferred_element_type=F32,
                     )
                     for head in heads
                 ],
                 axis=0,
             )
-            total = (near + far[:, block * rows : (block + 1) * rows]).astype(BF16)
-            out_ref[block * rows : (block + 1) * rows, c0 : c0 + step] = dot_last(
-                unit, total
-            ).astype(BF16)
+            for level in range(rows.bit_length(), near_levels):
+                span = 1 << level - 1
+                if t0 & span:
+                    s0 = t0 // span * span - span
+                    mixed = jnp.dot(
+                        values[:, s0 : s0 + span],
+                        score_ref[s0 : s0 + span, t0 : t0 + rows],
+                        preferred_element_type=F32,
+                    )
+                    total = total + weight(level, t0, t0 + rows) * mixed
+            out_ref[t0 : t0 + rows, c0 : c0 + step] = dot_last(unit, total.astype(BF16)).astype(
+                BF16
+            )
 
 
 def finish(values, states, offset, last, token_pieces, sum_pieces, queries, level_weight, near, head_size):
     width, length = values.shape
-    arrays = [*token_pieces, *sum_pieces, *last, values, states, queries, level_weight, *near]
+    sum_parts = len(sum_pieces[0]) if sum_pieces else 1
+    flat_sums = [part for piece in sum_pieces for part in piece]
+    flat_tokens = [piece[0] for piece in token_pieces]
+    arrays = [*flat_tokens, *flat_sums, *last, values, states, queries, level_weight, *near]
     scratch = []
     if last:
         depth = last[0].shape[1]
         scratch = [pltpu.VMEM((length, depth), BF16), pltpu.VMEM((states.shape[1], depth), BF16)]
     return pl.pallas_call(
-        functools.partial(finish_kernel, len(token_pieces), offset, len(last), len(near), head_size),
+        functools.partial(
+            finish_kernel, len(flat_tokens), sum_parts, offset, len(last), head_size
+        ),
         in_specs=[pl.BlockSpec(memory_space=pltpu.VMEM)] * len(arrays),
         out_shape=jax.ShapeDtypeStruct((length, width), BF16),
         scratch_shapes=scratch,
@@ -313,16 +338,29 @@
     dev_bits = ctx_count.bit_length() - 1
     near = prepare(queries, key_vectors, level_weight)
 
-    running = jnp.einsum("tn,tf->nf", key_vectors, tokens, preferred_element_type=F32)
+    running, sent, *turned = begin(key_vectors, tokens, value_weight, 2)
     level_sums = []
     for section_bit in range(dev_bits):
-        partner = from_partner(running.astype(BF16), "ctx", section_bit)
+        if section_bit > 0:
+            sent = running.astype(BF16)
+        if section_bit == dev_bits - 1 and dev_bits > 1:
+            break
+        partner = from_partner(sent, "ctx", section_bit)
         level_sums.append(partner)
         running = running + partner.astype(F32)
-    level_sums = jnp.concatenate(level_sums, axis=0)
+    if dev_bits > 1:
+        unit = ctx_count // 4
+        for hop in range(2):
+            route = [((1 + hop) * unit + num, (2 + hop) * unit + num) for num in range(unit)]
+            sent = lax.ppermute(sent, "ctx", route)
+            top = sent if hop == 0 else top + sent
+        level_sums.append(top)
+    low_sums = jnp.concatenate(level_sums[:-1] or level_sums, axis=0)
+    top_sums = level_sums[-1:] if dev_bits > 1 else []
 
     if depth % 256 or width_feat % depth:
         features = lax.all_gather(tokens, "head", axis=1, tiled=True)
+        level_sums = jnp.concatenate([low_sums, *top_sums], axis=0)
         sums = lax.all_gather(level_sums, "head", axis=1, tiled=True)
         weight = lax.all_gather(value_weight, "ctx", axis=0, tiled=True)
         values = jnp.einsum("fc,tf->ct", weight, features, preferred_element_type=F32)
@@ -333,9 +371,11 @@
     ahead = [(order[i], order[(i + 1) % ctx_count]) for i in range(ctx_count)]
     back = [(b, a) for a, b in ahead]
     half_count = ctx_count // 2
-    token_pieces = on_chip(*gather_pieces(tokens, "head"))
-    sum_pieces = on_chip(*gather_pieces(level_sums, "head"))
-    cw = ccw = tuple(turn(value_weight, 2))
+    token_pieces = [[piece] for piece in on_chip(*gather_pieces(tokens, "head"))]
+    low_pieces = on_chip(*gather_pieces(low_sums, "head"))
+    top_pieces = [on_chip(*gather_pieces(sums, "head")) for sums in top_sums]
+    sum_pieces = list(zip(low_pieces, *top_pieces))
+    cw = ccw = tuple(turned)
     steps = [[(0, cw)]]
 
     def move(part, route):

time: 71.9 us -> 72.4 us (level)
  waiting for transfers between devices: 21.6 us -> 27.5 us
  starting transfers between devices: 34.6 us -> 29.6 us
  local copies, waits for them, and re-layouts: 1.09 us -> 3.02 us
  matrix products: 1.45 us -> 0 us
    ppermute x14, waiting for transfers between devices: 15.6 us -> 23.1 us  [move(): return lax.ppermute(part, 'ctx', route)]
    ppermute x14, starting transfers between devices: 24.1 us -> 19.2 us  [move(): return lax.ppermute(part, 'ctx', route)]
    unnamed x12 -> x15, local copies, waits for them, and re-layouts: 1.07 us -> 3.01 us
    ppermute x9 -> x11, waiting for transfers between devices: 5.99 us -> 4.4 us  [from_partner(): return lax.ppermute(block, axis, route)]
    dot_general x1 -> x0, matrix products: 1.45 us -> none  [body(): jnp.einsum('tn,tf->nf', key_vectors, tokens, preferred_element_type=F32)]
    ppermute x9 -> x11, starting transfers between devices: 10.5 us -> 9.09 us  [from_partner(): return lax.ppermute(block, axis, route)]
    ppermute x0 -> x2, starting transfers between devices: none -> 1.32 us  [body(): sent = lax.ppermute(sent, 'ctx', route)]
  transfers between devices with their start and end apart: 23 -> 27, of which waited for: 9 -> 12; matrix products, arithmetic and copies ran while one was open for 0% -> 0% of each run, Pallas kernels for 10% -> 10%
where the time goes in v3:
time: 72.4 us; the launch traced here: 72.2 us
  starting transfers between devices  29.6 us (41%)
  waiting for transfers between devices  27.5 us (38%)
  Pallas kernels  11.8 us (16%)
  local copies, waits for them, and re-layouts  3.02 us (4%)
    ppermute x14, waiting for transfers between devices, move(): return lax.ppermute(part, 'ctx', route)  23.1 us
    ppermute x14, starting transfers between devices, move(): return lax.ppermute(part, 'ctx', route)  19.2 us
    ppermute x11, starting transfers between devices, from_partner(): return lax.ppermute(block, axis, route)  9.09 us
    pallas_call x4, Pallas kernels, extend(): pl.pallas_call(functools.partial(extend_kernel, len(flat), len(pieces[0])...  5.31 us
    pallas_call x1, Pallas kernels, finish(): pl.pallas_call(functools.partial(finish_kernel, len(flat_tokens), sum_par...  4.64 us
    ppermute x11, waiting for transfers between devices, from_partner(): return lax.ppermute(block, axis, route)  4.4 us
    unnamed x15, local copies, waits for them, and re-layouts  3.01 us
    pallas_call x1, Pallas kernels, prepare(): pl.pallas_call(prepare_kernel, out_shape=[pltpu.VMEM((heads, length, rows...  1.59 us
  transfers between devices with their start and end apart: 27, of which 12 were waited for; matrix products, arithmetic and copies ran while one was open for 0% of the time, Pallas kernels for 10%

profile of v3, /device:TPU:0, one launch (start us, length us, event | category | flops | bytes accessed | tf_op | source)
XLA Modules:
  0.0 72.2 jit_solution(9633114676822722022)
XLA Ops:
  0.0 1.0 %copy-done = bf16[512,512]{1,0:T(8,128)(2,1)S(1)} copy-done((bf16[512,512]{1,0:T(8,128)(2,1)S(1)}, bf16[512,512]{1,0:T(8,128)(2,1)}, u32[]{:S(2)}) %copy-start) | copy-done | bytes 524312
  1.0 1.0 %copy-done.4 = bf16[256,1024]{1,0:T(8,128)(2,1)S(1)} copy-done((bf16[256,1024]{1,0:T(8,128)(2,1)S(1)}, bf16[256,1024]{1,0:T(8,128)(2,1)}, u32[]{:S(2)}) %copy-start.4) | copy-done | bytes 524312
  2.1 0.9 %copy-done.5 = bf16[512,128]{1,0:T(8,128)(2,1)S(1)} copy-done((bf16[512,128]{1,0:T(8,128)(2,1)S(1)}, bf16[512,128]{1,0:T(8,128)(2,1)}, u32[]{:S(2)}) %copy-start.5) | copy-done | bytes 131096
  3.0 0.3 begin.1
  3.3 3.1 %collective-permute-start.3 = (bf16[128,512]{1,0:T(8,128)(2,1)S(1)}, bf16[128,512]{1,0:T(8,128)(2,1)S(1)}, u32[]{:S(2)}, u32[]{:S(2)}) collective-permute-start(bf16[128,512]{1,0:T(8,128)(2,1)S(1)} %get-tuple-element.11), channel_id=1, source_target_pairs={{0,4},{4,0},{8,12},{12,8},{16,20},{20,16},{24,28},{28,24},{1,5},{5... | collective-permute-start | bytes 393224 | tf_op jit(solution)/shard_map/ppermute | solution.py:22
  6.3 3.5 %collective-permute-done.3 = bf16[128,512]{1,0:T(8,128)(2,1)S(1)} collective-permute-done((bf16[128,512]{1,0:T(8,128)(2,1)S(1)}, bf16[128,512]{1,0:T(8,128)(2,1)S(1)}, u32[]{:S(2)}, u32[]{:S(2)}) %collective-permute-start.3) | collective-permute-done | bytes 131104 | tf_op jit(solution)/shard_map/ppermute | solution.py:22
  9.9 1.9 %collective-permute-start.4 = (bf16[128,512]{1,0:T(8,128)(2,1)S(1)}, bf16[128,512]{1,0:T(8,128)(2,1)S(1)}, u32[]{:S(2)}, u32[]{:S(2)}) collective-permute-start(bf16[128,512]{1,0:T(8,128)(2,1)S(1)} %fusion), channel_id=1, source_target_pairs={{0,8},{8,0},{4,12},{12,4},{16,24},{24,16},{20,28},{28,20},{1,9},{9... | collective-permute-start | bytes 393224 | tf_op jit(solution)/shard_map/ppermute | solution.py:22
  11.7 1.5 %collective-permute-start.24 = (bf16[512,256]{1,0:T(8,128)(2,1)S(1)}, bf16[512,256]{1,0:T(8,128)(2,1)S(1)}, u32[]{:S(2)}, u32[]{:S(2)}) collective-permute-start(bf16[512,256]{1,0:T(8,128)(2,1)S(1)} %get-tuple-element.13.refs_4_.refs_8_), channel_id=1, source_target_pairs={{8,0},{16,8},{24,16},{28,24},{20,28},{12,20},{4,12},{0,4},{9,1},{1... | collective-permute-start | bytes 786440 | tf_op jit(solution)/shard_map/ppermute | solution.py:382
  13.2 1.5 %collective-permute-start.1 = (bf16[512,512]{1,0:T(8,128)(2,1)}, bf16[512,512]{1,0:T(8,128)(2,1)S(1)}, u32[]{:S(2)}, u32[]{:S(2)}) collective-permute-start(bf16[512,512]{1,0:T(8,128)(2,1)} %refs_0_.7), channel_id=1, source_target_pairs={{0,2},{2,0},{1,3},{3,1},{4,6},{6,4},{5,7},{7,5},{8,10},{10,8},{9,1... | collective-permute-start | bytes 1572872 | tf_op jit(solution)/shard_map/ppermute | solution.py:22
  14.7 0.5 collective-permute-start.13
  15.2 1.1 %collective-permute-start.21 = (bf16[512,256]{1,0:T(8,128)(2,1)S(1)}, bf16[512,256]{1,0:T(8,128)(2,1)S(1)}, u32[]{:S(2)}, u32[]{:S(2)}) collective-permute-start(bf16[512,256]{1,0:T(8,128)(2,1)S(1)} %get-tuple-element.14.refs_5_.refs_9_), channel_id=1, source_target_pairs={{0,8},{8,16},{16,24},{24,28},{28,20},{20,12},{12,4},{4,0},{1,9},{9... | collective-permute-start | bytes 786440 | tf_op jit(solution)/shard_map/ppermute | solution.py:382
  16.4 0.0 collective-permute-done.4
  16.4 0.9 %collective-permute-start.17 = (bf16[512,256]{1,0:T(8,128)(2,1)S(1)}, bf16[512,256]{1,0:T(8,128)(2,1)S(1)}, u32[]{:S(2)}, u32[]{:S(2)}) collective-permute-start(bf16[512,256]{1,0:T(8,128)(2,1)S(1)} %get-tuple-element.14.refs_5_.refs_9_), channel_id=1, source_target_pairs={{8,0},{16,8},{24,16},{28,24},{20,28},{12,20},{4,12},{0,4},{9,1},{1... | collective-permute-start | bytes 786440 | tf_op jit(solution)/shard_map/ppermute | solution.py:382
  17.3 4.6 %collective-permute-done.24.refs_8_.refs_12_ = bf16[512,256]{1,0:T(8,128)(2,1)S(1)} collective-permute-done((bf16[512,256]{1,0:T(8,128)(2,1)S(1)}, bf16[512,256]{1,0:T(8,128)(2,1)S(1)}, u32[]{:S(2)}, u32[]{:S(2)}) %collective-permute-start.24) | collective-permute-done | bytes 262176 | tf_op jit(solution)/shard_map/ppermute | solution.py:382
  21.9 0.7 collective-permute-start.5
  22.6 1.3 %collective-permute-done.13.refs_6_.refs_10_ = bf16[512,256]{1,0:T(8,128)(2,1)S(1)} collective-permute-done((bf16[512,256]{1,0:T(8,128)(2,1)S(1)}, bf16[512,256]{1,0:T(8,128)(2,1)S(1)}, u32[]{:S(2)}, u32[]{:S(2)}) %collective-permute-start.13) | collective-permute-done | bytes 262176 | tf_op jit(solution)/shard_map/ppermute | solution.py:382
  23.9 0.5 collective-permute-start.9
  24.4 0.7 collective-permute-start.6
  25.1 1.6 %collective-permute-done.21.refs_7_.refs_11_ = bf16[512,256]{1,0:T(8,128)(2,1)S(1)} collective-permute-done((bf16[512,256]{1,0:T(8,128)(2,1)S(1)}, bf16[512,256]{1,0:T(8,128)(2,1)S(1)}, u32[]{:S(2)}, u32[]{:S(2)}) %collective-permute-start.21) | collective-permute-done | bytes 262176 | tf_op jit(solution)/shard_map/ppermute | solution.py:382
  26.7 1.4 %collective-permute-start.25 = (bf16[512,256]{1,0:T(8,128)(2,1)S(1)}, bf16[512,256]{1,0:T(8,128)(2,1)S(1)}, u32[]{:S(2)}, u32[]{:S(2)}) collective-permute-start(bf16[512,256]{1,0:T(8,128)(2,1)S(1)} %collective-permute-done.24.refs_8_.refs_12_), channel_id=1, source_target_pairs={{8,0},{16,8},{24,16},{28,24},{20,28},{12,20},{4,12},{0,4},{9,1},{1... | collective-permute-start | bytes 786440 | tf_op jit(solution)/shard_map/ppermute | solution.py:382
  28.1 0.1 collective-permute-done.1.refs_2_
  28.2 2.3 %collective-permute-start.14 = (bf16[512,256]{1,0:T(8,128)(2,1)S(1)}, bf16[512,256]{1,0:T(8,128)(2,1)S(1)}, u32[]{:S(2)}, u32[]{:S(2)}) collective-permute-start(bf16[512,256]{1,0:T(8,128)(2,1)S(1)} %collective-permute-done.13.refs_6_.refs_10_), channel_id=1, source_target_pairs={{0,8},{8,16},{16,24},{24,28},{28,20},{20,12},{12,4},{4,0},{1,9},{9... | collective-permute-start | bytes 786440 | tf_op jit(solution)/shard_map/ppermute | solution.py:382
  30.6 0.0 collective-permute-done.6
  30.6 3.1 %collective-permute-start.22 = (bf16[512,256]{1,0:T(8,128)(2,1)S(1)}, bf16[512,256]{1,0:T(8,128)(2,1)S(1)}, u32[]{:S(2)}, u32[]{:S(2)}) collective-permute-start(bf16[512,256]{1,0:T(8,128)(2,1)S(1)} %collective-permute-done.21.refs_7_.refs_11_), channel_id=1, source_target_pairs={{0,8},{8,16},{16,24},{24,28},{28,20},{20,12},{12,4},{4,0},{1,9},{9... | collective-permute-start | bytes 786440 | tf_op jit(solution)/shard_map/ppermute | solution.py:382
  33.7 0.0 collective-permute-done.9.refs_4_.refs_8_
  33.7 0.1 collective-permute-start.11
  33.8 3.9 %collective-permute-done.25.refs_6_.refs_16_ = bf16[512,256]{1,0:T(8,128)(2,1)S(1)} collective-permute-done((bf16[512,256]{1,0:T(8,128)(2,1)S(1)}, bf16[512,256]{1,0:T(8,128)(2,1)S(1)}, u32[]{:S(2)}, u32[]{:S(2)}) %collective-permute-start.25) | collective-permute-done | bytes 262176 | tf_op jit(solution)/shard_map/ppermute | solution.py:382
  37.7 0.1 collective-permute-start.26
  37.9 0.4 collective-permute-done.14.refs_4_.refs_14_
  38.3 1.5 %collective-permute-start.10 = (bf16[128,512]{1,0:T(8,128)(2,1)S(1)}, bf16[128,512]{1,0:T(8,128)(2,1)S(1)}, u32[]{:S(2)}, u32[]{:S(2)}) collective-permute-start(bf16[128,512]{1,0:T(8,128)(2,1)S(1)} %add.11.refs_1_.refs_5_), channel_id=1, source_target_pairs={{0,2},{2,0},{1,3},{3,1},{4,6},{6,4},{5,7},{7,5},{8,10},{10,8},{9,1... | collective-permute-start | bytes 393224 | tf_op jit(solution)/shard_map/ppermute | solution.py:22
  39.8 3.6 %collective-permute-done.22.refs_5_.refs_15_ = bf16[512,256]{1,0:T(8,128)(2,1)S(1)} collective-permute-done((bf16[512,256]{1,0:T(8,128)(2,1)S(1)}, bf16[512,256]{1,0:T(8,128)(2,1)S(1)}, u32[]{:S(2)}, u32[]{:S(2)}) %collective-permute-start.22) | collective-permute-done | bytes 262176 | tf_op jit(solution)/shard_map/ppermute | solution.py:382
  43.4 0.5 collective-permute-start
  43.9 0.1 collective-permute-start.2
  44.0 0.8 %collective-permute-done.8.refs_3_.refs_7_ = bf16[128,512]{1,0:T(8,128)(2,1)S(1)} collective-permute-done((bf16[128,512]{1,0:T(8,128)(2,1)S(1)}, bf16[128,512]{1,0:T(8,128)(2,1)S(1)}, u32[]{:S(2)}, u32[]{:S(2)}) %collective-permute-start.8) | collective-permute-done | bytes 131104 | tf_op jit(solution)/shard_map/ppermute | solution.py:22
  44.7 2.2 %collective-permute-start.15 = (bf16[512,256]{1,0:T(8,128)(2,1)S(1)}, bf16[512,256]{1,0:T(8,128)(2,1)S(1)}, u32[]{:S(2)}, u32[]{:S(2)}) collective-permute-start(bf16[512,256]{1,0:T(8,128)(2,1)S(1)} %collective-permute-done.14.refs_4_.refs_14_), channel_id=1, source_target_pairs={{0,8},{8,16},{16,24},{24,28},{28,20},{20,12},{12,4},{4,0},{1,9},{9... | collective-permute-start | bytes 786440 | tf_op jit(solution)/shard_map/ppermute | solution.py:382
  46.9 0.9 %collective-permute-start.19 = (bf16[512,256]{1,0:T(8,128)(2,1)S(1)}, bf16[512,256]{1,0:T(8,128)(2,1)S(1)}, u32[]{:S(2)}, u32[]{:S(2)}) collective-permute-start(bf16[512,256]{1,0:T(8,128)(2,1)S(1)} %collective-permute-done.18.refs_7_.refs_17_), channel_id=1, source_target_pairs={{8,0},{16,8},{24,16},{28,24},{20,28},{12,20},{4,12},{0,4},{9,1},{1... | collective-permute-start | bytes 786440 | tf_op jit(solution)/shard_map/ppermute | solution.py:382
  47.8 0.8 %collective-permute-done.26.refs_6_.refs_20_ = bf16[512,256]{1,0:T(8,128)(2,1)S(1)} collective-permute-done((bf16[512,256]{1,0:T(8,128)(2,1)S(1)}, bf16[512,256]{1,0:T(8,128)(2,1)S(1)}, u32[]{:S(2)}, u32[]{:S(2)}) %collective-permute-start.26) | collective-permute-done | bytes 262176 | tf_op jit(solution)/shard_map/ppermute | solution.py:382
  48.6 3.1 %collective-permute-start.23 = (bf16[512,256]{1,0:T(8,128)(2,1)S(1)}, bf16[512,256]{1,0:T(8,128)(2,1)S(1)}, u32[]{:S(2)}, u32[]{:S(2)}) collective-permute-start(bf16[512,256]{1,0:T(8,128)(2,1)S(1)} %collective-permute-done.22.refs_5_.refs_15_), channel_id=1, source_target_pairs={{0,8},{8,16},{16,24},{24,28},{28,20},{20,12},{12,4},{4,0},{1,9},{9... | collective-permute-start | bytes 786440 | tf_op jit(solution)/shard_map/ppermute | solution.py:382
  51.7 3.2 %collective-permute-done.15.refs_4_.refs_18_ = bf16[512,256]{1,0:T(8,128)(2,1)S(1)} collective-permute-done((bf16[512,256]{1,0:T(8,128)(2,1)S(1)}, bf16[512,256]{1,0:T(8,128)(2,1)S(1)}, u32[]{:S(2)}, u32[]{:S(2)}) %collective-permute-start.15) | collective-permute-done | bytes 262176 | tf_op jit(solution)/shard_map/ppermute | solution.py:382
  54.9 1.1 %collective-permute-start.16 = (bf16[512,256]{1,0:T(8,128)(2,1)S(1)}, bf16[512,256]{1,0:T(8,128)(2,1)S(1)}, u32[]{:S(2)}, u32[]{:S(2)}) collective-permute-start(bf16[512,256]{1,0:T(8,128)(2,1)S(1)} %collective-permute-done.15.refs_4_.refs_18_), channel_id=1, source_target_pairs={{0,8},{8,16},{16,24},{24,28},{28,20},{20,12},{12,4},{4,0},{1,9},{9... | collective-permute-start | bytes 786440 | tf_op jit(solution)/shard_map/ppermute | solution.py:382
  56.1 0.9 %collective-permute-start.20 = (bf16[512,256]{1,0:T(8,128)(2,1)S(1)}, bf16[512,256]{1,0:T(8,128)(2,1)S(1)}, u32[]{:S(2)}, u32[]{:S(2)}) collective-permute-start(bf16[512,256]{1,0:T(8,128)(2,1)S(1)} %collective-permute-done.19.refs_7_.refs_21_), channel_id=1, source_target_pairs={{8,0},{16,8},{24,16},{28,24},{20,28},{12,20},{4,12},{0,4},{9,1},{1... | collective-permute-start | bytes 786440 | tf_op jit(solution)/shard_map/ppermute | solution.py:382
  57.0 3.6 %collective-permute-done.23.refs_5_.refs_19_ = bf16[512,256]{1,0:T(8,128)(2,1)S(1)} collective-permute-done((bf16[512,256]{1,0:T(8,128)(2,1)S(1)}, bf16[512,256]{1,0:T(8,128)(2,1)S(1)}, u32[]{:S(2)}, u32[]{:S(2)}) %collective-permute-start.23) | collective-permute-done | bytes 262176 | tf_op jit(solution)/shard_map/ppermute | solution.py:382
  60.6 1.6 %prepare.1 = (bf16[16,512,256]{2,1,0:T(8,128)(2,1)S(1)}, bf16[512,512]{1,0:T(8,128)(2,1)S(1)}) custom-call(bf16[512,128]{1,0:T(8,128)(2,1)S(1)} %copy-done.3, bf16[512,128]{1,0:T(8,128)(2,1)S(1)} %copy-done.6, f32[13,16,512]{2,1,0:T(8,128)S(1)} %copy-done.2), custom_call_target="tpu_custom_call" | custom-call | tf_op jit(solution)/shard_map/prepare/pallas_call | solution.py:120
  62.2 2.4 %shard_map.58.refs_15_ = f32[1024,384]{1,0:T(8,128)S(1)} custom-call(bf16[256,512]{1,0:T(8,128)(2,1)S(1)} %constant_dynamic-update-slice_fusion.refs_0_.refs_4_, bf16[128,512]{1,0:T(8,128)(2,1)S(1)} %add.11.refs_1_.refs_5_, bf16[256,512]{1,0:T(8,128)(2,1)S(1)} %collective-permute-done.7.refs_2_.refs_6_, ...), custom_call_target="tpu_custom_call" | custom-call | tf_op jit(solution)/shard_map/pallas_call | solution.py:218
  64.6 1.2 %shard_map.55.refs_8_ = f32[1024,512]{1,0:T(8,128)S(1)} custom-call(bf16[512,512]{1,0:T(8,128)(2,1)S(1)} %copy-done.1, bf16[512,512]{1,0:T(8,128)(2,1)S(1)} %collective-permute-done.refs_1_, bf16[512,512]{1,0:T(8,128)(2,1)S(1)} %collective-permute-done.1.refs_2_, bf16[512,512]{1,0:T(8,128)(2,1)S(1)} %collective-permute-done.2.refs_3_, ...), custom_call_target="tpu_custom_call" | custom-call | tf_op jit(solution)/shard_map/pallas_call | solution.py:218
  65.8 0.9 %shard_map.56.refs_8_ = f32[1024,512]{1,0:T(8,128)S(1)} custom-call(bf16[512,512]{1,0:T(8,128)(2,1)S(1)} %copy-done.1, bf16[512,512]{1,0:T(8,128)(2,1)S(1)} %collective-permute-done.refs_1_, bf16[512,512]{1,0:T(8,128)(2,1)S(1)} %collective-permute-done.1.refs_2_, bf16[512,512]{1,0:T(8,128)(2,1)S(1)} %collective-permute-done.2.refs_3_, ...), custom_call_target="tpu_custom_call" | custom-call | tf_op jit(solution)/shard_map/pallas_call | solution.py:218
  66.7 0.9 %shard_map.57.refs_14_ = f32[1024,512]{1,0:T(8,128)S(1)} custom-call(bf16[512,512]{1,0:T(8,128)(2,1)S(1)} %copy-done.1, bf16[512,512]{1,0:T(8,128)(2,1)S(1)} %collective-permute-done.refs_1_, bf16[512,512]{1,0:T(8,128)(2,1)S(1)} %collective-permute-done.1.refs_2_, bf16[512,512]{1,0:T(8,128)(2,1)S(1)} %collective-permute-done.2.refs_3_, ...), custom_call_target="tpu_custom_call" | custom-call | tf_op jit(solution)/shard_map/pallas_call | solution.py:218
  67.6 4.6 %finish.1 = bf16[512,1024]{1,0:T(8,128)(2,1)} custom-call(bf16[512,512]{1,0:T(8,128)(2,1)S(1)} %copy-done.1, bf16[512,512]{1,0:T(8,128)(2,1)S(1)} %collective-permute-done.refs_1_, bf16[512,512]{1,0:T(8,128)(2,1)S(1)} %collective-permute-done.1.refs_2_, bf16[512,512]{1,0:T(8,128)(2,1)S(1)} %collective-permute-done.2.refs_3_, ...), custom_call_target="tpu_custom_call" | custom-call | tf_op jit(solution)/shard_map/finish/pallas_call | solution.py:320
  (32 shorter events, 0.2 us)
Async XLA Ops:
  0.0 1.0 %copy-start = (bf16[512,512]{1,0:T(8,128)(2,1)S(1)}, bf16[512,512]{1,0:T(8,128)(2,1)}, u32[]{:S(2)}) copy-start(bf16[512,512]{1,0:T(8,128)(2,1)} %refs_0_.7) | copy-start | bytes 1572868
  1.0 1.0 %copy-start.4 = (bf16[256,1024]{1,0:T(8,128)(2,1)S(1)}, bf16[256,1024]{1,0:T(8,128)(2,1)}, u32[]{:S(2)}) copy-start(bf16[256,1024]{1,0:T(8,128)(2,1)} %weight_ref.1) | copy-start | bytes 1572868
  2.1 0.9 %copy-start.5 = (bf16[512,128]{1,0:T(8,128)(2,1)S(1)}, bf16[512,128]{1,0:T(8,128)(2,1)}, u32[]{:S(2)}) copy-start(bf16[512,128]{1,0:T(8,128)(2,1)} %k_ref.3) | copy-start | bytes 393220
  3.0 40.4 %copy-start.1 = (bf16[512,512]{1,0:T(8,128)(2,1)S(1)}, bf16[512,512]{1,0:T(8,128)(2,1)}, u32[]{:S(2)}) copy-start(bf16[512,512]{1,0:T(8,128)(2,1)} %refs_0_.7) | copy-start | bytes 1572868
  3.0 57.6 %copy-start.2 = (f32[13,16,512]{2,1,0:T(8,128)S(1)}, f32[13,16,512]{2,1,0:T(8,128)}, u32[]{:S(2)}) copy-start(f32[13,16,512]{2,1,0:T(8,128)} %refs_17_.1) | copy-start | bytes 1277956
  3.0 57.6 %copy-start.3 = (bf16[512,128]{1,0:T(8,128)(2,1)S(1)}, bf16[512,128]{1,0:T(8,128)(2,1)}, u32[]{:S(2)}) copy-start(bf16[512,128]{1,0:T(8,128)(2,1)} %refs_16_.1) | copy-start | bytes 393220
  3.0 57.6 %copy-start.6 = (bf16[512,128]{1,0:T(8,128)(2,1)S(1)}, bf16[512,128]{1,0:T(8,128)(2,1)}, u32[]{:S(2)}) copy-start(bf16[512,128]{1,0:T(8,128)(2,1)} %k_ref.3) | copy-start | bytes 393220
  3.3 6.6 %collective-permute-start.3 = (bf16[128,512]{1,0:T(8,128)(2,1)S(1)}, bf16[128,512]{1,0:T(8,128)(2,1)S(1)}, u32[]{:S(2)}, u32[]{:S(2)}) collective-permute-start(bf16[128,512]{1,0:T(8,128)(2,1)S(1)} %get-tuple-element.11), channel_id=1, source_target_pairs={{0,4},{4,0},{8,12},{12,8},{16,20},{20,16},{24,28},{28,24},{1,5},{5... | collective-permute-start | bytes 393224 | tf_op jit(solution)/shard_map/ppermute | solution.py:22
  9.9 6.5 %collective-permute-start.4 = (bf16[128,512]{1,0:T(8,128)(2,1)S(1)}, bf16[128,512]{1,0:T(8,128)(2,1)S(1)}, u32[]{:S(2)}, u32[]{:S(2)}) collective-permute-start(bf16[128,512]{1,0:T(8,128)(2,1)S(1)} %fusion), channel_id=1, source_target_pairs={{0,8},{8,0},{4,12},{12,4},{16,24},{24,16},{20,28},{28,20},{1,9},{9... | collective-permute-start | bytes 393224 | tf_op jit(solution)/shard_map/ppermute | solution.py:22
  11.7 10.2 %collective-permute-start.24 = (bf16[512,256]{1,0:T(8,128)(2,1)S(1)}, bf16[512,256]{1,0:T(8,128)(2,1)S(1)}, u32[]{:S(2)}, u32[]{:S(2)}) collective-permute-start(bf16[512,256]{1,0:T(8,128)(2,1)S(1)} %get-tuple-element.13.refs_4_.refs_8_), channel_id=1, source_target_pairs={{8,0},{16,8},{24,16},{28,24},{20,28},{12,20},{4,12},{0,4},{9,1},{1... | collective-permute-start | bytes 786440 | tf_op jit(solution)/shard_map/ppermute | solution.py:382
  13.2 15.0 %collective-permute-start.1 = (bf16[512,512]{1,0:T(8,128)(2,1)}, bf16[512,512]{1,0:T(8,128)(2,1)S(1)}, u32[]{:S(2)}, u32[]{:S(2)}) collective-permute-start(bf16[512,512]{1,0:T(8,128)(2,1)} %refs_0_.7), channel_id=1, source_target_pairs={{0,2},{2,0},{1,3},{3,1},{4,6},{6,4},{5,7},{7,5},{8,10},{10,8},{9,1... | collective-permute-start | bytes 1572872 | tf_op jit(solution)/shard_map/ppermute | solution.py:22
  14.7 9.2 %collective-permute-start.13 = (bf16[512,256]{1,0:T(8,128)(2,1)S(1)}, bf16[512,256]{1,0:T(8,128)(2,1)S(1)}, u32[]{:S(2)}, u32[]{:S(2)}) collective-permute-start(bf16[512,256]{1,0:T(8,128)(2,1)S(1)} %get-tuple-element.13.refs_4_.refs_8_), channel_id=1, source_target_pairs={{0,8},{8,16},{16,24},{24,28},{28,20},{20,12},{12,4},{4,0},{1,9},{9... | collective-permute-start | bytes 786440 | tf_op jit(solution)/shard_map/ppermute | solution.py:382
  15.2 11.5 %collective-permute-start.21 = (bf16[512,256]{1,0:T(8,128)(2,1)S(1)}, bf16[512,256]{1,0:T(8,128)(2,1)S(1)}, u32[]{:S(2)}, u32[]{:S(2)}) collective-permute-start(bf16[512,256]{1,0:T(8,128)(2,1)S(1)} %get-tuple-element.14.refs_5_.refs_9_), channel_id=1, source_target_pairs={{0,8},{8,16},{16,24},{24,28},{28,20},{20,12},{12,4},{4,0},{1,9},{9... | collective-permute-start | bytes 786440 | tf_op jit(solution)/shard_map/ppermute | solution.py:382
  16.4 10.3 %collective-permute-start.17 = (bf16[512,256]{1,0:T(8,128)(2,1)S(1)}, bf16[512,256]{1,0:T(8,128)(2,1)S(1)}, u32[]{:S(2)}, u32[]{:S(2)}) collective-permute-start(bf16[512,256]{1,0:T(8,128)(2,1)S(1)} %get-tuple-element.14.refs_5_.refs_9_), channel_id=1, source_target_pairs={{8,0},{16,8},{24,16},{28,24},{20,28},{12,20},{4,12},{0,4},{9,1},{1... | collective-permute-start | bytes 786440 | tf_op jit(solution)/shard_map/ppermute | solution.py:382
  21.9 2.5 %collective-permute-start.5 = (bf16[128,512]{1,0:T(8,128)(2,1)S(1)}, bf16[128,512]{1,0:T(8,128)(2,1)S(1)}, u32[]{:S(2)}, u32[]{:S(2)}) collective-permute-start(bf16[128,512]{1,0:T(8,128)(2,1)S(1)} %add_convert_fusion), channel_id=1, source_target_pairs={{8,16},{12,20},{9,17},{13,21},{10,18},{14,22},{11,19},{15,23}} | collective-permute-start | bytes 393224 | tf_op jit(solution)/shard_map/ppermute | solution.py:355
  23.9 9.8 %collective-permute-start.9 = (bf16[256,512]{1,0:T(8,128)(2,1)S(1)}, bf16[256,512]{1,0:T(8,128)(2,1)S(1)}, u32[]{:S(2)}, u32[]{:S(2)}) collective-permute-start(bf16[256,512]{1,0:T(8,128)(2,1)S(1)} %constant_dynamic-update-slice_fusion.refs_0_.refs_4_), channel_id=1, source_target_pairs={{0,2},{2,0},{1,3},{3,1},{4,6},{6,4},{5,7},{7,5},{8,10},{10,8},{9,1... | collective-permute-start | bytes 786440 | tf_op jit(solution)/shard_map/ppermute | solution.py:22
  24.4 6.2 %collective-permute-start.6 = (bf16[128,512]{1,0:T(8,128)(2,1)S(1)}, bf16[128,512]{1,0:T(8,128)(2,1)S(1)}, u32[]{:S(2)}, u32[]{:S(2)}) collective-permute-start(bf16[128,512]{1,0:T(8,128)(2,1)S(1)} %collective-permute-done.5), channel_id=1, source_target_pairs={{16,24},{20,28},{17,25},{21,29},{18,26},{22,30},{19,27},{23,31}} | collective-permute-start | bytes 393224 | tf_op jit(solution)/shard_map/ppermute | solution.py:355
  26.7 7.0 %collective-permute-start.7 = (bf16[256,512]{1,0:T(8,128)(2,1)S(1)}, bf16[256,512]{1,0:T(8,128)(2,1)S(1)}, u32[]{:S(2)}, u32[]{:S(2)}) collective-permute-start(bf16[256,512]{1,0:T(8,128)(2,1)S(1)} %constant_dynamic-update-slice_fusion.refs_0_.refs_4_), channel_id=1, source_target_pairs={{0,1},{1,0},{2,3},{3,2},{4,5},{5,4},{6,7},{7,6},{8,9},{9,8},{10,11... | collective-permute-start | bytes 786440 | tf_op jit(solution)/shard_map/ppermute | solution.py:22
  26.7 11.0 %collective-permute-start.25 = (bf16[512,256]{1,0:T(8,128)(2,1)S(1)}, bf16[512,256]{1,0:T(8,128)(2,1)S(1)}, u32[]{:S(2)}, u32[]{:S(2)}) collective-permute-start(bf16[512,256]{1,0:T(8,128)(2,1)S(1)} %collective-permute-done.24.refs_8_.refs_12_), channel_id=1, source_target_pairs={{8,0},{16,8},{24,16},{28,24},{20,28},{12,20},{4,12},{0,4},{9,1},{1... | collective-permute-start | bytes 786440 | tf_op jit(solution)/shard_map/ppermute | solution.py:382
  28.2 10.0 %collective-permute-start.14 = (bf16[512,256]{1,0:T(8,128)(2,1)S(1)}, bf16[512,256]{1,0:T(8,128)(2,1)S(1)}, u32[]{:S(2)}, u32[]{:S(2)}) collective-permute-start(bf16[512,256]{1,0:T(8,128)(2,1)S(1)} %collective-permute-done.13.refs_6_.refs_10_), channel_id=1, source_target_pairs={{0,8},{8,16},{16,24},{24,28},{28,20},{20,12},{12,4},{4,0},{1,9},{9... | collective-permute-start | bytes 786440 | tf_op jit(solution)/shard_map/ppermute | solution.py:382
  30.6 12.8 %collective-permute-start.22 = (bf16[512,256]{1,0:T(8,128)(2,1)S(1)}, bf16[512,256]{1,0:T(8,128)(2,1)S(1)}, u32[]{:S(2)}, u32[]{:S(2)}) collective-permute-start(bf16[512,256]{1,0:T(8,128)(2,1)S(1)} %collective-permute-done.21.refs_7_.refs_11_), channel_id=1, source_target_pairs={{0,8},{8,16},{16,24},{24,28},{28,20},{20,12},{12,4},{4,0},{1,9},{9... | collective-permute-start | bytes 786440 | tf_op jit(solution)/shard_map/ppermute | solution.py:382
  33.7 9.7 %collective-permute-start.18 = (bf16[512,256]{1,0:T(8,128)(2,1)S(1)}, bf16[512,256]{1,0:T(8,128)(2,1)S(1)}, u32[]{:S(2)}, u32[]{:S(2)}) collective-permute-start(bf16[512,256]{1,0:T(8,128)(2,1)S(1)} %collective-permute-done.17.refs_9_.refs_13_), channel_id=1, source_target_pairs={{8,0},{16,8},{24,16},{28,24},{20,28},{12,20},{4,12},{0,4},{9,1},{1... | collective-permute-start | bytes 786440 | tf_op jit(solution)/shard_map/ppermute | solution.py:382
  33.7 13.2 %collective-permute-start.11 = (bf16[256,512]{1,0:T(8,128)(2,1)S(1)}, bf16[256,512]{1,0:T(8,128)(2,1)S(1)}, u32[]{:S(2)}, u32[]{:S(2)}) collective-permute-start(bf16[256,512]{1,0:T(8,128)(2,1)S(1)} %collective-permute-done.9.refs_4_.refs_8_), channel_id=1, source_target_pairs={{0,1},{1,0},{2,3},{3,2},{4,5},{5,4},{6,7},{7,6},{8,9},{9,8},{10,11... | collective-permute-start | bytes 786440 | tf_op jit(solution)/shard_map/ppermute | solution.py:22
  37.7 11.0 %collective-permute-start.26 = (bf16[512,256]{1,0:T(8,128)(2,1)S(1)}, bf16[512,256]{1,0:T(8,128)(2,1)S(1)}, u32[]{:S(2)}, u32[]{:S(2)}) collective-permute-start(bf16[512,256]{1,0:T(8,128)(2,1)S(1)} %collective-permute-done.25.refs_6_.refs_16_), channel_id=1, source_target_pairs={{8,0},{16,8},{24,16},{28,24},{20,28},{12,20},{4,12},{0,4},{9,1},{1... | collective-permute-start | bytes 786440 | tf_op jit(solution)/shard_map/ppermute | solution.py:382
  38.3 5.6 %collective-permute-start.10 = (bf16[128,512]{1,0:T(8,128)(2,1)S(1)}, bf16[128,512]{1,0:T(8,128)(2,1)S(1)}, u32[]{:S(2)}, u32[]{:S(2)}) collective-permute-start(bf16[128,512]{1,0:T(8,128)(2,1)S(1)} %add.11.refs_1_.refs_5_), channel_id=1, source_target_pairs={{0,2},{2,0},{1,3},{3,1},{4,6},{6,4},{5,7},{7,5},{8,10},{10,8},{9,1... | collective-permute-start | bytes 393224 | tf_op jit(solution)/shard_map/ppermute | solution.py:22
  43.4 1.3 %collective-permute-start.8 = (bf16[128,512]{1,0:T(8,128)(2,1)S(1)}, bf16[128,512]{1,0:T(8,128)(2,1)S(1)}, u32[]{:S(2)}, u32[]{:S(2)}) collective-permute-start(bf16[128,512]{1,0:T(8,128)(2,1)S(1)} %add.11.refs_1_.refs_5_), channel_id=1, source_target_pairs={{0,1},{1,0},{2,3},{3,2},{4,5},{5,4},{6,7},{7,6},{8,9},{9,8},{10,11... | collective-permute-start | bytes 393224 | tf_op jit(solution)/shard_map/ppermute | solution.py:22
  43.4 21.2 %collective-permute-start = (bf16[512,512]{1,0:T(8,128)(2,1)S(1)}, bf16[512,512]{1,0:T(8,128)(2,1)S(1)}, u32[]{:S(2)}, u32[]{:S(2)}) collective-permute-start(bf16[512,512]{1,0:T(8,128)(2,1)S(1)} %copy-done.1), channel_id=1, source_target_pairs={{0,1},{1,0},{2,3},{3,2},{4,5},{5,4},{6,7},{7,6},{8,9},{9,8},{10,11... | collective-permute-start | bytes 1572872 | tf_op jit(solution)/shard_map/ppermute | solution.py:22
  43.9 20.7 %collective-permute-start.2 = (bf16[512,512]{1,0:T(8,128)(2,1)S(1)}, bf16[512,512]{1,0:T(8,128)(2,1)S(1)}, u32[]{:S(2)}, u32[]{:S(2)}) collective-permute-start(bf16[512,512]{1,0:T(8,128)(2,1)S(1)} %collective-permute-done.1.refs_2_), channel_id=1, source_target_pairs={{0,1},{1,0},{2,3},{3,2},{4,5},{5,4},{6,7},{7,6},{8,9},{9,8},{10,11... | collective-permute-start | bytes 1572872 | tf_op jit(solution)/shard_map/ppermute | solution.py:22
  44.7 10.2 %collective-permute-start.15 = (bf16[512,256]{1,0:T(8,128)(2,1)S(1)}, bf16[512,256]{1,0:T(8,128)(2,1)S(1)}, u32[]{:S(2)}, u32[]{:S(2)}) collective-permute-start(bf16[512,256]{1,0:T(8,128)(2,1)S(1)} %collective-permute-done.14.refs_4_.refs_14_), channel_id=1, source_target_pairs={{0,8},{8,16},{16,24},{24,28},{28,20},{20,12},{12,4},{4,0},{1,9},{9... | collective-permute-start | bytes 786440 | tf_op jit(solution)/shard_map/ppermute | solution.py:382
  46.9 9.2 %collective-permute-start.19 = (bf16[512,256]{1,0:T(8,128)(2,1)S(1)}, bf16[512,256]{1,0:T(8,128)(2,1)S(1)}, u32[]{:S(2)}, u32[]{:S(2)}) collective-permute-start(bf16[512,256]{1,0:T(8,128)(2,1)S(1)} %collective-permute-done.18.refs_7_.refs_17_), channel_id=1, source_target_pairs={{8,0},{16,8},{24,16},{28,24},{20,28},{12,20},{4,12},{0,4},{9,1},{1... | collective-permute-start | bytes 786440 | tf_op jit(solution)/shard_map/ppermute | solution.py:382
  48.6 11.9 %collective-permute-start.23 = (bf16[512,256]{1,0:T(8,128)(2,1)S(1)}, bf16[512,256]{1,0:T(8,128)(2,1)S(1)}, u32[]{:S(2)}, u32[]{:S(2)}) collective-permute-start(bf16[512,256]{1,0:T(8,128)(2,1)S(1)} %collective-permute-done.22.refs_5_.refs_15_), channel_id=1, source_target_pairs={{0,8},{8,16},{16,24},{24,28},{28,20},{20,12},{12,4},{4,0},{1,9},{9... | collective-permute-start | bytes 786440 | tf_op jit(solution)/shard_map/ppermute | solution.py:382
  54.9 12.6 %collective-permute-start.16 = (bf16[512,256]{1,0:T(8,128)(2,1)S(1)}, bf16[512,256]{1,0:T(8,128)(2,1)S(1)}, u32[]{:S(2)}, u32[]{:S(2)}) collective-permute-start(bf16[512,256]{1,0:T(8,128)(2,1)S(1)} %collective-permute-done.15.refs_4_.refs_18_), channel_id=1, source_target_pairs={{0,8},{8,16},{16,24},{24,28},{28,20},{20,12},{12,4},{4,0},{1,9},{9... | collective-permute-start | bytes 786440 | tf_op jit(solution)/shard_map/ppermute | solution.py:382
  56.1 11.5 %collective-permute-start.20 = (bf16[512,256]{1,0:T(8,128)(2,1)S(1)}, bf16[512,256]{1,0:T(8,128)(2,1)S(1)}, u32[]{:S(2)}, u32[]{:S(2)}) collective-permute-start(bf16[512,256]{1,0:T(8,128)(2,1)S(1)} %collective-permute-done.19.refs_7_.refs_21_), channel_id=1, source_target_pairs={{8,0},{16,8},{24,16},{28,24},{20,28},{12,20},{4,12},{0,4},{9,1},{1... | collective-permute-start | bytes 786440 | tf_op jit(solution)/shard_map/ppermute | solution.py:382
  60.6 1.6 %collective-permute-start.12 = (bf16[128,512]{1,0:T(8,128)(2,1)S(1)}, bf16[128,512]{1,0:T(8,128)(2,1)S(1)}, u32[]{:S(2)}, u32[]{:S(2)}) collective-permute-start(bf16[128,512]{1,0:T(8,128)(2,1)S(1)} %collective-permute-done.10.refs_5_.refs_9_), channel_id=1, source_target_pairs={{0,1},{1,0},{2,3},{3,2},{4,5},{5,4},{6,7},{7,6},{8,9},{9,8},{10,11... | collective-permute-start | bytes 393224 | tf_op jit(solution)/shard_map/ppermute | solution.py:22

commit v4 on v3

--- a/solution.py
+++ b/solution.py
@@ -129,27 +129,44 @@
     )(queries, key_vectors, level_weight)
 
 
-def begin_kernel(k_ref, token_ref, weight_ref, sum_ref, sent_ref, *part_refs):
+def turn_kernel(weight_ref, *part_refs):
+    share = part_refs[0].shape[0]
+    for num, part_ref in enumerate(part_refs):
+        part_ref[...] = weight_ref[:, num * share : (num + 1) * share].T
+
+
+def turn(weight, split):
+    depth, width = weight.shape
+    return pl.pallas_call(
+        turn_kernel,
+        out_shape=[pltpu.VMEM((width // split, depth), weight.dtype)] * split,
+        compiler_params=pltpu.CompilerParams(vmem_limit_bytes=8 << 20),
+        name="turn",
+    )(weight)
+
+
+def begin_kernel(k_ref, token_ref, sum_ref, sent_ref, held_ref):
+    tokens = token_ref[...]
     total = lax.dot_general(
-        k_ref[...], token_ref[...], (((0,), (0,)), ((), ())), preferred_element_type=F32
+        k_ref[...], tokens, (((0,), (0,)), ((), ())), preferred_element_type=F32
     )
     sum_ref[...] = total
     sent_ref[...] = total.astype(BF16)
-    share = part_refs[0].shape[0]
-    for num, part_ref in enumerate(part_refs):
-        part_ref[...] = weight_ref[:, num * share : (num + 1) * share].T
-
-
-def begin(key_vectors, tokens, weight, split):
-    depth, width = weight.shape
+    held_ref[...] = tokens
+
+
+def begin(key_vectors, tokens):
     shape = (key_vectors.shape[1], tokens.shape[1])
     return pl.pallas_call(
         begin_kernel,
-        out_shape=[pltpu.VMEM(shape, F32), pltpu.VMEM(shape, BF16)]
-        + [pltpu.VMEM((width // split, depth), weight.dtype)] * split,
+        out_shape=[
+            pltpu.VMEM(shape, F32),
+            pltpu.VMEM(shape, BF16),
+            pltpu.VMEM(tokens.shape, tokens.dtype),
+        ],
         compiler_params=pltpu.CompilerParams(vmem_limit_bytes=8 << 20),
         name="begin",
-    )(key_vectors, tokens, weight)
+    )(key_vectors, tokens)
 
 
 def ring_order(count):
@@ -168,28 +185,18 @@
 
 def choose(offsets, pieces, depth, chosen_ref):
     for num, offset in enumerate(offsets):
-        piece, start = place(offset, depth, pieces[0][0].shape[1])
+        piece, start = place(offset, depth, pieces[0].shape[1])
         start = pl.multiple_of(start, 128)
-        for index, parts in enumerate(pieces):
+        for index, ref in enumerate(pieces):
 
             @pl.when(piece == index)
             def _():
-                row = 0
-                for ref in parts:
-                    rows = ref.shape[0]
-                    chosen_ref[row : row + rows, num * depth : (num + 1) * depth] = ref[
-                        :, pl.ds(start, depth)
-                    ]
-                    row += rows
-
-
-def in_parts(refs, count):
-    return [refs[num : num + count] for num in range(0, len(refs), count)]
-
-
-def extend_kernel(piece_count, parts, offsets, split, started, *refs):
+                chosen_ref[:, num * depth : (num + 1) * depth] = ref[:, pl.ds(start, depth)]
+
+
+def extend_kernel(piece_count, offsets, split, started, *refs):
     count = len(offsets)
-    pieces = in_parts(refs[:piece_count], parts)
+    pieces = refs[:piece_count]
     blocks = [refs[piece_count + num * split :][:split] for num in range(count)]
     out_ref, chosen_ref = refs[-2], refs[-1]
     share, depth = blocks[0][0].shape
@@ -211,13 +218,12 @@
     offsets = tuple(offset for offset, _ in parts)
     blocks = [half for _, block in parts for half in block]
     split = len(parts[0][1])
-    rows = sum(part.shape[0] for part in pieces[0])
+    rows = pieces[0].shape[0]
     share, depth = blocks[0].shape
-    flat = [part for piece in pieces for part in piece]
-    arrays = [*flat, *blocks, *([] if total is None else [total])]
+    arrays = [*pieces, *blocks, *([] if total is None else [total])]
     return pl.pallas_call(
         functools.partial(
-            extend_kernel, len(flat), len(pieces[0]), offsets, split, total is not None
+            extend_kernel, len(pieces), offsets, split, total is not None
         ),
         in_specs=[pl.BlockSpec(memory_space=pltpu.VMEM)] * len(arrays),
         out_shape=pltpu.VMEM((share * split, rows), F32),
@@ -226,22 +232,24 @@
     )(*arrays)
 
 
-def finish_kernel(piece_count, sum_parts, offset, last_count, head_size, *refs):
+def finish_kernel(piece_count, groups, offset, last_count, head_size, *refs):
     refs = list(refs)
     take = lambda count: [refs.pop(0) for _ in range(count)]
-    token_refs, sum_refs = take(piece_count), take(piece_count * sum_parts)
+    token_refs, sum_refs = take(piece_count), [take(piece_count) for _ in range(groups)]
     last_refs = take(last_count)
-    value_ref, state_ref, q_ref, w_ref, near_ref, score_ref, out_ref = take(7)
+    value_ref, state_refs = refs.pop(0), take(groups)
+    q_ref, w_ref, near_ref, score_ref, out_ref = take(5)
     length, state_rows = q_ref.shape
     width = value_ref.shape[0]
     near_levels = length.bit_length()
     far_levels = w_ref.shape[0] - near_levels
     rows = near_ref.shape[2]
     if last_count:
-        token_chosen, sum_chosen = refs
+        token_chosen, *sum_chosen = refs
         depth = token_chosen.shape[1]
-        choose([offset], in_parts(token_refs, 1), depth, token_chosen)
-        choose([offset], in_parts(sum_refs, sum_parts), depth, sum_chosen)
+        choose([offset], token_refs, depth, token_chosen)
+        for pieces, chosen in zip(sum_refs, sum_chosen):
+            choose([offset], pieces, depth, chosen)
     mine = lax.axis_index("ctx")
     queries = q_ref[...]
     twice = jnp.concatenate([queries, queries], axis=1)
@@ -251,12 +259,15 @@
         == lax.broadcasted_iota(jnp.int32, (rows, rows), 1)
     ).astype(BF16)
     for c0 in range(0, width, step):
-        values, states = value_ref[c0 : c0 + step, :], state_ref[c0 : c0 + step, :]
+        values = value_ref[c0 : c0 + step, :]
+        states = [ref[c0 : c0 + step, :] for ref in state_refs]
         if last_count:
             share = width // last_count
             left = last_refs[c0 // share][c0 % share : c0 % share + step, :]
             values = values + dot_last(left, token_chosen[...])
-            states = states + dot_last(left, sum_chosen[...])
+            states = [
+                part + dot_last(left, chosen[...]) for part, chosen in zip(states, sum_chosen)
+            ]
         values = values.astype(BF16)
         heads = range(c0 // head_size, (c0 + step) // head_size)
 
@@ -272,6 +283,7 @@
             )
 
         far = None
+        states = jnp.concatenate(states, axis=1)
         for num in range(far_levels):
             state = states[:, num * state_rows : (num + 1) * state_rows]
             state = jnp.where(jnp.right_shift(mine, num) % 2 == 1, state, jnp.zeros_like(state))
@@ -309,17 +321,15 @@
 
 def finish(values, states, offset, last, token_pieces, sum_pieces, queries, level_weight, near, head_size):
     width, length = values.shape
-    sum_parts = len(sum_pieces[0]) if sum_pieces else 1
-    flat_sums = [part for piece in sum_pieces for part in piece]
-    flat_tokens = [piece[0] for piece in token_pieces]
-    arrays = [*flat_tokens, *flat_sums, *last, values, states, queries, level_weight, *near]
+    flat_sums = [piece for pieces in sum_pieces for piece in pieces]
+    arrays = [*token_pieces, *flat_sums, *last, values, *states, queries, level_weight, *near]
     scratch = []
     if last:
         depth = last[0].shape[1]
-        scratch = [pltpu.VMEM((length, depth), BF16), pltpu.VMEM((states.shape[1], depth), BF16)]
+        scratch = [pltpu.VMEM((rows, depth), BF16) for rows in [length, *(s.shape[1] for s in states)]]
     return pl.pallas_call(
         functools.partial(
-            finish_kernel, len(flat_tokens), sum_parts, offset, len(last), head_size
+            finish_kernel, len(token_pieces), len(states), offset, len(last), head_size
         ),
         in_specs=[pl.BlockSpec(memory_space=pltpu.VMEM)] * len(arrays),
         out_shape=jax.ShapeDtypeStruct((length, width), BF16),
@@ -338,7 +348,7 @@
     dev_bits = ctx_count.bit_length() - 1
     near = prepare(queries, key_vectors, level_weight)
 
-    running, sent, *turned = begin(key_vectors, tokens, value_weight, 2)
+    running, sent, held = begin(key_vectors, tokens)
     level_sums = []
     for section_bit in range(dev_bits):
         if section_bit > 0:
@@ -365,17 +375,16 @@
         weight = lax.all_gather(value_weight, "ctx", axis=0, tiled=True)
         values = jnp.einsum("fc,tf->ct", weight, features, preferred_element_type=F32)
         states = jnp.einsum("fc,nf->cn", weight, sums, preferred_element_type=F32)
-        return finish(values, states, 0, [], [], [], queries, level_weight, near, head_size)
+        return finish(values, [states], 0, [], [], [[]], queries, level_weight, near, head_size)
 
     order = ring_order(ctx_count)
     ahead = [(order[i], order[(i + 1) % ctx_count]) for i in range(ctx_count)]
     back = [(b, a) for a, b in ahead]
     half_count = ctx_count // 2
-    token_pieces = [[piece] for piece in on_chip(*gather_pieces(tokens, "head"))]
-    low_pieces = on_chip(*gather_pieces(low_sums, "head"))
-    top_pieces = [on_chip(*gather_pieces(sums, "head")) for sums in top_sums]
-    sum_pieces = list(zip(low_pieces, *top_pieces))
-    cw = ccw = tuple(turned)
+    token_pieces = on_chip(*gather_pieces(held, "head"))
+    sum_pieces = [on_chip(*gather_pieces(low_sums, "head"))]
+    sum_pieces += [on_chip(*gather_pieces(sums, "head")) for sums in top_sums]
+    cw = ccw = tuple(turn(value_weight, 2))
     steps = [[(0, cw)]]
 
     def move(part, route):
@@ -389,7 +398,8 @@
     values = extend(None, token_pieces, steps[0] + steps[1])
     for step in range(2, half_count):
         values = extend(values, token_pieces, steps[step])
-    states = extend(None, sum_pieces, [part for parts in steps for part in parts])
+    every = [part for parts in steps for part in parts]
+    states = [extend(None, pieces, every) for pieces in sum_pieces]
     return finish(
         values,
         states,

time: 72.4 us -> 72.6 us (level)
  starting transfers between devices: 29.6 us -> 25.4 us
  waiting for transfers between devices: 27.5 us -> 31.3 us
    ppermute x11, waiting for transfers between devices: 4.4 us -> 10.9 us  [from_partner(): return lax.ppermute(block, axis, route)]
    ppermute x14, starting transfers between devices: 19.2 us -> 14.2 us  [move(): return lax.ppermute(part, 'ctx', route)]
    ppermute x14, waiting for transfers between devices: 23.1 us -> 20.5 us  [move(): return lax.ppermute(part, 'ctx', route)]
    ppermute x11, starting transfers between devices: 9.09 us -> 9.9 us  [from_partner(): return lax.ppermute(block, axis, route)]
    pallas_call x5 -> x7, Pallas kernels: 9.94 us -> 10.5 us  [the longest x5 5.75 us: extend(): pl.pallas_call(functools.partial(extend_kernel, len(pieces), offsets, spl...]
    unnamed x15 -> x13, local copies, waits for them, and re-layouts: 3.01 us -> 3.06 us
  transfers between devices with their start and end apart: 27 -> 27, of which waited for: 12 -> 10; matrix products, arithmetic and copies ran while one was open for 0% -> 0% of each run, Pallas kernels for 10% -> 10%
where the time goes in v4:
time: 72.6 us; the launch traced here: 72.4 us
  waiting for transfers between devices  31.3 us (43%)
  starting transfers between devices  25.4 us (35%)
  Pallas kernels  12.4 us (17%)
  local copies, waits for them, and re-layouts  3.07 us (4%)
    ppermute x14, waiting for transfers between devices, move(): return lax.ppermute(part, 'ctx', route)  20.5 us
    ppermute x14, starting transfers between devices, move(): return lax.ppermute(part, 'ctx', route)  14.2 us
    ppermute x11, waiting for transfers between devices, from_partner(): return lax.ppermute(block, axis, route)  10.9 us
    ppermute x11, starting transfers between devices, from_partner(): return lax.ppermute(block, axis, route)  9.9 us
    pallas_call x5, Pallas kernels, extend(): pl.pallas_call(functools.partial(extend_kernel, len(pieces), offsets, spl...  5.75 us
    pallas_call x1, Pallas kernels, finish(): pl.pallas_call(functools.partial(finish_kernel, len(token_pieces), len(st...  4.58 us
    unnamed x13, local copies, waits for them, and re-layouts  3.06 us
    pallas_call x1, Pallas kernels, prepare(): pl.pallas_call(prepare_kernel, out_shape=[pltpu.VMEM((heads, length, rows...  1.59 us
  transfers between devices with their start and end apart: 27, of which 10 were waited for; matrix products, arithmetic and copies ran while one was open for 0% of the time, Pallas kernels for 10%

profile of v4, /device:TPU:0, one launch (start us, length us, event | category | flops | bytes accessed | tf_op | source)
XLA Modules:
  0.0 72.4 jit_solution(12369726052657921178)
XLA Ops:
  0.0 1.1 %copy-done.2 = bf16[512,512]{1,0:T(8,128)(2,1)S(1)} copy-done((bf16[512,512]{1,0:T(8,128)(2,1)S(1)}, bf16[512,512]{1,0:T(8,128)(2,1)}, u32[]{:S(2)}) %copy-start.2) | copy-done | bytes 524312
  1.1 0.9 %copy-done.4 = bf16[512,128]{1,0:T(8,128)(2,1)S(1)} copy-done((bf16[512,128]{1,0:T(8,128)(2,1)S(1)}, bf16[512,128]{1,0:T(8,128)(2,1)}, u32[]{:S(2)}) %copy-start.4) | copy-done | bytes 131096
  2.0 0.3 begin.1
  2.3 3.1 %collective-permute-start.3 = (bf16[128,512]{1,0:T(8,128)(2,1)S(1)}, bf16[128,512]{1,0:T(8,128)(2,1)S(1)}, u32[]{:S(2)}, u32[]{:S(2)}) collective-permute-start(bf16[128,512]{1,0:T(8,128)(2,1)S(1)} %get-tuple-element.13), channel_id=1, source_target_pairs={{0,4},{4,0},{8,12},{12,8},{16,20},{20,16},{24,28},{28,24},{1,5},{5... | collective-permute-start | bytes 393224 | tf_op jit(solution)/shard_map/ppermute | solution.py:22
  5.3 3.5 %collective-permute-done.3 = bf16[128,512]{1,0:T(8,128)(2,1)S(1)} collective-permute-done((bf16[128,512]{1,0:T(8,128)(2,1)S(1)}, bf16[128,512]{1,0:T(8,128)(2,1)S(1)}, u32[]{:S(2)}, u32[]{:S(2)}) %collective-permute-start.3) | collective-permute-done | bytes 131104 | tf_op jit(solution)/shard_map/ppermute | solution.py:22
  8.9 1.9 %collective-permute-start.4 = (bf16[128,512]{1,0:T(8,128)(2,1)S(1)}, bf16[128,512]{1,0:T(8,128)(2,1)S(1)}, u32[]{:S(2)}, u32[]{:S(2)}) collective-permute-start(bf16[128,512]{1,0:T(8,128)(2,1)S(1)} %fusion), channel_id=1, source_target_pairs={{0,8},{8,0},{4,12},{12,4},{16,24},{24,16},{20,28},{28,20},{1,9},{9... | collective-permute-start | bytes 393224 | tf_op jit(solution)/shard_map/ppermute | solution.py:22
  10.7 1.0 %copy-done.3 = bf16[256,1024]{1,0:T(8,128)(2,1)S(1)} copy-done((bf16[256,1024]{1,0:T(8,128)(2,1)S(1)}, bf16[256,1024]{1,0:T(8,128)(2,1)}, u32[]{:S(2)}) %copy-start.3) | copy-done | bytes 524312
  11.8 0.2 turn.1
  11.9 1.6 %collective-permute-start.24 = (bf16[512,256]{1,0:T(8,128)(2,1)S(1)}, bf16[512,256]{1,0:T(8,128)(2,1)S(1)}, u32[]{:S(2)}, u32[]{:S(2)}) collective-permute-start(bf16[512,256]{1,0:T(8,128)(2,1)S(1)} %get-tuple-element.15.refs_4_), channel_id=1, source_target_pairs={{8,0},{16,8},{24,16},{28,24},{20,28},{12,20},{4,12},{0,4},{9,1},{1... | collective-permute-start | bytes 786440 | tf_op jit(solution)/shard_map/ppermute | solution.py:391
  13.5 0.5 collective-permute-start.13
  14.0 1.2 %collective-permute-start.21 = (bf16[512,256]{1,0:T(8,128)(2,1)S(1)}, bf16[512,256]{1,0:T(8,128)(2,1)S(1)}, u32[]{:S(2)}, u32[]{:S(2)}) collective-permute-start(bf16[512,256]{1,0:T(8,128)(2,1)S(1)} %get-tuple-element.16.refs_5_), channel_id=1, source_target_pairs={{0,8},{8,16},{16,24},{24,28},{28,20},{20,12},{12,4},{4,0},{1,9},{9... | collective-permute-start | bytes 786440 | tf_op jit(solution)/shard_map/ppermute | solution.py:391
  15.2 0.8 %collective-permute-start.17 = (bf16[512,256]{1,0:T(8,128)(2,1)S(1)}, bf16[512,256]{1,0:T(8,128)(2,1)S(1)}, u32[]{:S(2)}, u32[]{:S(2)}) collective-permute-start(bf16[512,256]{1,0:T(8,128)(2,1)S(1)} %get-tuple-element.16.refs_5_), channel_id=1, source_target_pairs={{8,0},{16,8},{24,16},{28,24},{20,28},{12,20},{4,12},{0,4},{9,1},{1... | collective-permute-start | bytes 786440 | tf_op jit(solution)/shard_map/ppermute | solution.py:391
  16.1 0.0 collective-permute-done.4
  16.1 0.7 collective-permute-start.8
  16.8 4.4 %collective-permute-done.24.refs_8_ = bf16[512,256]{1,0:T(8,128)(2,1)S(1)} collective-permute-done((bf16[512,256]{1,0:T(8,128)(2,1)S(1)}, bf16[512,256]{1,0:T(8,128)(2,1)S(1)}, u32[]{:S(2)}, u32[]{:S(2)}) %collective-permute-start.24) | collective-permute-done | bytes 262176 | tf_op jit(solution)/shard_map/ppermute | solution.py:391
  21.2 1.5 %collective-permute-start.25 = (bf16[512,256]{1,0:T(8,128)(2,1)S(1)}, bf16[512,256]{1,0:T(8,128)(2,1)S(1)}, u32[]{:S(2)}, u32[]{:S(2)}) collective-permute-start(bf16[512,256]{1,0:T(8,128)(2,1)S(1)} %collective-permute-done.24.refs_8_), channel_id=1, source_target_pairs={{8,0},{16,8},{24,16},{28,24},{20,28},{12,20},{4,12},{0,4},{9,1},{1... | collective-permute-start | bytes 786440 | tf_op jit(solution)/shard_map/ppermute | solution.py:391
  22.7 0.5 collective-permute-start.14
  23.2 5.1 %collective-permute-done.21.refs_7_ = bf16[512,256]{1,0:T(8,128)(2,1)S(1)} collective-permute-done((bf16[512,256]{1,0:T(8,128)(2,1)S(1)}, bf16[512,256]{1,0:T(8,128)(2,1)S(1)}, u32[]{:S(2)}, u32[]{:S(2)}) %collective-permute-start.21) | collective-permute-done | bytes 262176 | tf_op jit(solution)/shard_map/ppermute | solution.py:391
  28.3 1.5 %collective-permute-start.1 = (bf16[512,512]{1,0:T(8,128)(2,1)S(1)}, bf16[512,512]{1,0:T(8,128)(2,1)S(1)}, u32[]{:S(2)}, u32[]{:S(2)}) collective-permute-start(bf16[512,512]{1,0:T(8,128)(2,1)S(1)} %get-tuple-element.12.refs_0_), channel_id=1, source_target_pairs={{0,2},{2,0},{1,3},{3,1},{4,6},{6,4},{5,7},{7,5},{8,10},{10,8},{9,1... | collective-permute-start | bytes 1572872 | tf_op jit(solution)/shard_map/ppermute | solution.py:22
  29.8 0.0 collective-permute-done.17.refs_9_
  29.8 0.5 collective-permute-start.22
  30.3 0.0 collective-permute-done.8
  30.3 1.5 %collective-permute-start.18 = (bf16[512,256]{1,0:T(8,128)(2,1)S(1)}, bf16[512,256]{1,0:T(8,128)(2,1)S(1)}, u32[]{:S(2)}, u32[]{:S(2)}) collective-permute-start(bf16[512,256]{1,0:T(8,128)(2,1)S(1)} %collective-permute-done.17.refs_9_), channel_id=1, source_target_pairs={{8,0},{16,8},{24,16},{28,24},{20,28},{12,20},{4,12},{0,4},{9,1},{1... | collective-permute-start | bytes 786440 | tf_op jit(solution)/shard_map/ppermute | solution.py:391
  31.9 0.5 collective-permute-done.25.refs_6_.refs_12_
  32.4 1.5 %collective-permute-start.6 = (bf16[256,512]{1,0:T(8,128)(2,1)S(1)}, bf16[256,512]{1,0:T(8,128)(2,1)S(1)}, u32[]{:S(2)}, u32[]{:S(2)}) collective-permute-start(bf16[256,512]{1,0:T(8,128)(2,1)S(1)} %constant_dynamic-update-slice_fusion.refs_0_.refs_4_), channel_id=1, source_target_pairs={{0,2},{2,0},{1,3},{3,1},{4,6},{6,4},{5,7},{7,5},{8,10},{10,8},{9,1... | collective-permute-start | bytes 786440 | tf_op jit(solution)/shard_map/ppermute | solution.py:22
  33.9 0.0 collective-permute-done.14.refs_4_.refs_10_
  33.9 3.1 %collective-permute-done.22.refs_5_.refs_11_ = bf16[512,256]{1,0:T(8,128)(2,1)S(1)} collective-permute-done((bf16[512,256]{1,0:T(8,128)(2,1)S(1)}, bf16[512,256]{1,0:T(8,128)(2,1)S(1)}, u32[]{:S(2)}, u32[]{:S(2)}) %collective-permute-start.22) | collective-permute-done | bytes 262176 | tf_op jit(solution)/shard_map/ppermute | solution.py:391
  37.0 0.7 collective-permute-start.9
  37.7 1.5 %collective-permute-start.26 = (bf16[512,256]{1,0:T(8,128)(2,1)S(1)}, bf16[512,256]{1,0:T(8,128)(2,1)S(1)}, u32[]{:S(2)}, u32[]{:S(2)}) collective-permute-start(bf16[512,256]{1,0:T(8,128)(2,1)S(1)} %collective-permute-done.25.refs_6_.refs_12_), channel_id=1, source_target_pairs={{8,0},{16,8},{24,16},{28,24},{20,28},{12,20},{4,12},{0,4},{9,1},{1... | collective-permute-start | bytes 786440 | tf_op jit(solution)/shard_map/ppermute | solution.py:391
  39.1 1.0 %collective-permute-start.15 = (bf16[512,256]{1,0:T(8,128)(2,1)S(1)}, bf16[512,256]{1,0:T(8,128)(2,1)S(1)}, u32[]{:S(2)}, u32[]{:S(2)}) collective-permute-start(bf16[512,256]{1,0:T(8,128)(2,1)S(1)} %collective-permute-done.14.refs_4_.refs_10_), channel_id=1, source_target_pairs={{0,8},{8,16},{16,24},{24,28},{28,20},{20,12},{12,4},{4,0},{1,9},{9... | collective-permute-start | bytes 786440 | tf_op jit(solution)/shard_map/ppermute | solution.py:391
  40.1 4.4 %collective-permute-done.6.refs_2_.refs_6_ = bf16[256,512]{1,0:T(8,128)(2,1)S(1)} collective-permute-done((bf16[256,512]{1,0:T(8,128)(2,1)S(1)}, bf16[256,512]{1,0:T(8,128)(2,1)S(1)}, u32[]{:S(2)}, u32[]{:S(2)}) %collective-permute-start.6) | collective-permute-done | bytes 262176 | tf_op jit(solution)/shard_map/ppermute | solution.py:22
  44.5 1.5 %collective-permute-start.11 = (bf16[128,512]{1,0:T(8,128)(2,1)S(1)}, bf16[128,512]{1,0:T(8,128)(2,1)S(1)}, u32[]{:S(2)}, u32[]{:S(2)}) collective-permute-start(bf16[128,512]{1,0:T(8,128)(2,1)S(1)} %add.11.refs_0_.refs_8_), channel_id=1, source_target_pairs={{0,2},{2,0},{1,3},{3,1},{4,6},{6,4},{5,7},{7,5},{8,10},{10,8},{9,1... | collective-permute-start | bytes 393224 | tf_op jit(solution)/shard_map/ppermute | solution.py:22
  46.0 0.5 collective-permute-start
  46.5 3.0 %collective-permute-done.11.refs_2_.refs_10_ = bf16[128,512]{1,0:T(8,128)(2,1)S(1)} collective-permute-done((bf16[128,512]{1,0:T(8,128)(2,1)S(1)}, bf16[128,512]{1,0:T(8,128)(2,1)S(1)}, u32[]{:S(2)}, u32[]{:S(2)}) %collective-permute-start.11) | collective-permute-done | bytes 131104 | tf_op jit(solution)/shard_map/ppermute | solution.py:22
  49.5 1.3 %collective-permute-start.23 = (bf16[512,256]{1,0:T(8,128)(2,1)S(1)}, bf16[512,256]{1,0:T(8,128)(2,1)S(1)}, u32[]{:S(2)}, u32[]{:S(2)}) collective-permute-start(bf16[512,256]{1,0:T(8,128)(2,1)S(1)} %collective-permute-done.22.refs_5_.refs_11_), channel_id=1, source_target_pairs={{0,8},{8,16},{16,24},{24,28},{28,20},{20,12},{12,4},{4,0},{1,9},{9... | collective-permute-start | bytes 786440 | tf_op jit(solution)/shard_map/ppermute | solution.py:391
  50.8 0.7 collective-permute-start.19
  51.5 6.7 %collective-permute-done.23.refs_5_.refs_15_ = bf16[512,256]{1,0:T(8,128)(2,1)S(1)} collective-permute-done((bf16[512,256]{1,0:T(8,128)(2,1)S(1)}, bf16[512,256]{1,0:T(8,128)(2,1)S(1)}, u32[]{:S(2)}, u32[]{:S(2)}) %collective-permute-start.23) | collective-permute-done | bytes 262176 | tf_op jit(solution)/shard_map/ppermute | solution.py:391
  58.2 1.3 %collective-permute-start.16 = (bf16[512,256]{1,0:T(8,128)(2,1)S(1)}, bf16[512,256]{1,0:T(8,128)(2,1)S(1)}, u32[]{:S(2)}, u32[]{:S(2)}) collective-permute-start(bf16[512,256]{1,0:T(8,128)(2,1)S(1)} %collective-permute-done.15.refs_4_.refs_14_), channel_id=1, source_target_pairs={{0,8},{8,16},{16,24},{24,28},{28,20},{20,12},{12,4},{4,0},{1,9},{9... | collective-permute-start | bytes 786440 | tf_op jit(solution)/shard_map/ppermute | solution.py:391
  59.5 0.5 collective-permute-done.19.refs_7_.refs_17_
  60.0 0.2 collective-permute-start.20
  60.3 1.6 %prepare.1 = (bf16[16,512,256]{2,1,0:T(8,128)(2,1)S(1)}, bf16[512,512]{1,0:T(8,128)(2,1)S(1)}) custom-call(bf16[512,128]{1,0:T(8,128)(2,1)S(1)} %copy-done.1, bf16[512,128]{1,0:T(8,128)(2,1)S(1)} %copy-done.5, f32[13,16,512]{2,1,0:T(8,128)S(1)} %copy-done), custom_call_target="tpu_custom_call" | custom-call | tf_op jit(solution)/shard_map/prepare/pallas_call | solution.py:120
  61.9 1.5 %shard_map.58.refs_15_ = f32[1024,256]{1,0:T(8,128)S(1)} custom-call(bf16[256,512]{1,0:T(8,128)(2,1)S(1)} %constant_dynamic-update-slice_fusion.refs_0_.refs_4_, bf16[256,512]{1,0:T(8,128)(2,1)S(1)} %collective-permute-done.5.refs_1_.refs_5_, bf16[256,512]{1,0:T(8,128)(2,1)S(1)} %collective-permute-done.6.refs_2_.refs_6_, ...), custom_call_target="tpu_custom_call" | custom-call | tf_op jit(solution)/shard_map/pallas_call | solution.py:224
  63.3 1.4 %shard_map.59.refs_16_ = f32[1024,128]{1,0:T(8,128)S(1)} custom-call(bf16[128,512]{1,0:T(8,128)(2,1)S(1)} %add.11.refs_0_.refs_8_, bf16[128,512]{1,0:T(8,128)(2,1)S(1)} %collective-permute-done.10.refs_1_.refs_9_, bf16[128,512]{1,0:T(8,128)(2,1)S(1)} %collective-permute-done.11.refs_2_.refs_10_, ...), custom_call_target="tpu_custom_call" | custom-call | tf_op jit(solution)/shard_map/pallas_call | solution.py:224
  64.8 1.2 %shard_map.55.refs_8_ = f32[1024,512]{1,0:T(8,128)S(1)} custom-call(bf16[512,512]{1,0:T(8,128)(2,1)S(1)} %get-tuple-element.12.refs_0_, bf16[512,512]{1,0:T(8,128)(2,1)S(1)} %collective-permute-done.refs_1_, bf16[512,512]{1,0:T(8,128)(2,1)S(1)} %collective-permute-done.1.refs_2_, bf16[512,512]{1,0:T(8,128)(2,1)S(1)} %collective-permute-done.2.refs_3_, ...), custom_call_target="tpu_custom_call" | custom-call | tf_op jit(solution)/shard_map/pallas_call | solution.py:224
  66.0 0.9 %shard_map.56.refs_8_ = f32[1024,512]{1,0:T(8,128)S(1)} custom-call(bf16[512,512]{1,0:T(8,128)(2,1)S(1)} %get-tuple-element.12.refs_0_, bf16[512,512]{1,0:T(8,128)(2,1)S(1)} %collective-permute-done.refs_1_, bf16[512,512]{1,0:T(8,128)(2,1)S(1)} %collective-permute-done.1.refs_2_, bf16[512,512]{1,0:T(8,128)(2,1)S(1)} %collective-permute-done.2.refs_3_, ...), custom_call_target="tpu_custom_call" | custom-call | tf_op jit(solution)/shard_map/pallas_call | solution.py:224
  66.8 0.9 %shard_map.57.refs_14_ = f32[1024,512]{1,0:T(8,128)S(1)} custom-call(bf16[512,512]{1,0:T(8,128)(2,1)S(1)} %get-tuple-element.12.refs_0_, bf16[512,512]{1,0:T(8,128)(2,1)S(1)} %collective-permute-done.refs_1_, bf16[512,512]{1,0:T(8,128)(2,1)S(1)} %collective-permute-done.1.refs_2_, bf16[512,512]{1,0:T(8,128)(2,1)S(1)} %collective-permute-done.2.refs_3_, ...), custom_call_target="tpu_custom_call" | custom-call | tf_op jit(solution)/shard_map/pallas_call | solution.py:224
  67.7 0.2 collective-permute-done.20.refs_13_
  67.9 4.6 %finish.1 = bf16[512,1024]{1,0:T(8,128)(2,1)} custom-call(bf16[512,512]{1,0:T(8,128)(2,1)S(1)} %get-tuple-element.12.refs_0_, bf16[512,512]{1,0:T(8,128)(2,1)S(1)} %collective-permute-done.refs_1_, bf16[512,512]{1,0:T(8,128)(2,1)S(1)} %collective-permute-done.1.refs_2_, bf16[512,512]{1,0:T(8,128)(2,1)S(1)} %collective-permute-done.2.refs_3_, ...), custom_call_target="tpu_custom_call" | custom-call | tf_op jit(solution)/shard_map/finish/pallas_call | solution.py:330
  (32 shorter events, 0.2 us)
Async XLA Ops:
  0.0 60.3 %copy-start = (f32[13,16,512]{2,1,0:T(8,128)S(1)}, f32[13,16,512]{2,1,0:T(8,128)}, u32[]{:S(2)}) copy-start(f32[13,16,512]{2,1,0:T(8,128)} %refs_18_.1) | copy-start | bytes 1277956
  0.0 1.1 %copy-start.2 = (bf16[512,512]{1,0:T(8,128)(2,1)S(1)}, bf16[512,512]{1,0:T(8,128)(2,1)}, u32[]{:S(2)}) copy-start(bf16[512,512]{1,0:T(8,128)(2,1)} %token_ref.1) | copy-start | bytes 1572868
  1.1 0.9 %copy-start.4 = (bf16[512,128]{1,0:T(8,128)(2,1)S(1)}, bf16[512,128]{1,0:T(8,128)(2,1)}, u32[]{:S(2)}) copy-start(bf16[512,128]{1,0:T(8,128)(2,1)} %k_ref.3) | copy-start | bytes 393220
  2.0 58.3 %copy-start.1 = (bf16[512,128]{1,0:T(8,128)(2,1)S(1)}, bf16[512,128]{1,0:T(8,128)(2,1)}, u32[]{:S(2)}) copy-start(bf16[512,128]{1,0:T(8,128)(2,1)} %refs_17_.1) | copy-start | bytes 393220
  2.0 58.3 %copy-start.5 = (bf16[512,128]{1,0:T(8,128)(2,1)S(1)}, bf16[512,128]{1,0:T(8,128)(2,1)}, u32[]{:S(2)}) copy-start(bf16[512,128]{1,0:T(8,128)(2,1)} %k_ref.3) | copy-start | bytes 393220
  2.3 6.6 %collective-permute-start.3 = (bf16[128,512]{1,0:T(8,128)(2,1)S(1)}, bf16[128,512]{1,0:T(8,128)(2,1)S(1)}, u32[]{:S(2)}, u32[]{:S(2)}) collective-permute-start(bf16[128,512]{1,0:T(8,128)(2,1)S(1)} %get-tuple-element.13), channel_id=1, source_target_pairs={{0,4},{4,0},{8,12},{12,8},{16,20},{20,16},{24,28},{28,24},{1,5},{5... | collective-permute-start | bytes 393224 | tf_op jit(solution)/shard_map/ppermute | solution.py:22
  8.9 7.2 %collective-permute-start.4 = (bf16[128,512]{1,0:T(8,128)(2,1)S(1)}, bf16[128,512]{1,0:T(8,128)(2,1)S(1)}, u32[]{:S(2)}, u32[]{:S(2)}) collective-permute-start(bf16[128,512]{1,0:T(8,128)(2,1)S(1)} %fusion), channel_id=1, source_target_pairs={{0,8},{8,0},{4,12},{12,4},{16,24},{24,16},{20,28},{28,20},{1,9},{9... | collective-permute-start | bytes 393224 | tf_op jit(solution)/shard_map/ppermute | solution.py:22
  10.7 1.0 %copy-start.3 = (bf16[256,1024]{1,0:T(8,128)(2,1)S(1)}, bf16[256,1024]{1,0:T(8,128)(2,1)}, u32[]{:S(2)}) copy-start(bf16[256,1024]{1,0:T(8,128)(2,1)} %weight_ref.1) | copy-start | bytes 1572868
  11.9 9.2 %collective-permute-start.24 = (bf16[512,256]{1,0:T(8,128)(2,1)S(1)}, bf16[512,256]{1,0:T(8,128)(2,1)S(1)}, u32[]{:S(2)}, u32[]{:S(2)}) collective-permute-start(bf16[512,256]{1,0:T(8,128)(2,1)S(1)} %get-tuple-element.15.refs_4_), channel_id=1, source_target_pairs={{8,0},{16,8},{24,16},{28,24},{20,28},{12,20},{4,12},{0,4},{9,1},{1... | collective-permute-start | bytes 786440 | tf_op jit(solution)/shard_map/ppermute | solution.py:391
  13.5 9.2 %collective-permute-start.13 = (bf16[512,256]{1,0:T(8,128)(2,1)S(1)}, bf16[512,256]{1,0:T(8,128)(2,1)S(1)}, u32[]{:S(2)}, u32[]{:S(2)}) collective-permute-start(bf16[512,256]{1,0:T(8,128)(2,1)S(1)} %get-tuple-element.15.refs_4_), channel_id=1, source_target_pairs={{0,8},{8,16},{16,24},{24,28},{28,20},{20,12},{12,4},{4,0},{1,9},{9... | collective-permute-start | bytes 786440 | tf_op jit(solution)/shard_map/ppermute | solution.py:391
  14.0 14.3 %collective-permute-start.21 = (bf16[512,256]{1,0:T(8,128)(2,1)S(1)}, bf16[512,256]{1,0:T(8,128)(2,1)S(1)}, u32[]{:S(2)}, u32[]{:S(2)}) collective-permute-start(bf16[512,256]{1,0:T(8,128)(2,1)S(1)} %get-tuple-element.16.refs_5_), channel_id=1, source_target_pairs={{0,8},{8,16},{16,24},{24,28},{28,20},{20,12},{12,4},{4,0},{1,9},{9... | collective-permute-start | bytes 786440 | tf_op jit(solution)/shard_map/ppermute | solution.py:391
  15.2 14.6 %collective-permute-start.17 = (bf16[512,256]{1,0:T(8,128)(2,1)S(1)}, bf16[512,256]{1,0:T(8,128)(2,1)S(1)}, u32[]{:S(2)}, u32[]{:S(2)}) collective-permute-start(bf16[512,256]{1,0:T(8,128)(2,1)S(1)} %get-tuple-element.16.refs_5_), channel_id=1, source_target_pairs={{8,0},{16,8},{24,16},{28,24},{20,28},{12,20},{4,12},{0,4},{9,1},{1... | collective-permute-start | bytes 786440 | tf_op jit(solution)/shard_map/ppermute | solution.py:391
  16.1 14.2 %collective-permute-start.8 = (bf16[128,512]{1,0:T(8,128)(2,1)S(1)}, bf16[128,512]{1,0:T(8,128)(2,1)S(1)}, u32[]{:S(2)}, u32[]{:S(2)}) collective-permute-start(bf16[128,512]{1,0:T(8,128)(2,1)S(1)} %add_convert_fusion), channel_id=1, source_target_pairs={{8,16},{12,20},{9,17},{13,21},{10,18},{14,22},{11,19},{15,23}} | collective-permute-start | bytes 393224 | tf_op jit(solution)/shard_map/ppermute | solution.py:365
  21.2 11.2 %collective-permute-start.25 = (bf16[512,256]{1,0:T(8,128)(2,1)S(1)}, bf16[512,256]{1,0:T(8,128)(2,1)S(1)}, u32[]{:S(2)}, u32[]{:S(2)}) collective-permute-start(bf16[512,256]{1,0:T(8,128)(2,1)S(1)} %collective-permute-done.24.refs_8_), channel_id=1, source_target_pairs={{8,0},{16,8},{24,16},{28,24},{20,28},{12,20},{4,12},{0,4},{9,1},{1... | collective-permute-start | bytes 786440 | tf_op jit(solution)/shard_map/ppermute | solution.py:391
  22.7 11.2 %collective-permute-start.14 = (bf16[512,256]{1,0:T(8,128)(2,1)S(1)}, bf16[512,256]{1,0:T(8,128)(2,1)S(1)}, u32[]{:S(2)}, u32[]{:S(2)}) collective-permute-start(bf16[512,256]{1,0:T(8,128)(2,1)S(1)} %collective-permute-done.13.refs_6_), channel_id=1, source_target_pairs={{0,8},{8,16},{16,24},{24,28},{28,20},{20,12},{12,4},{4,0},{1,9},{9... | collective-permute-start | bytes 786440 | tf_op jit(solution)/shard_map/ppermute | solution.py:391
  28.3 17.7 %collective-permute-start.1 = (bf16[512,512]{1,0:T(8,128)(2,1)S(1)}, bf16[512,512]{1,0:T(8,128)(2,1)S(1)}, u32[]{:S(2)}, u32[]{:S(2)}) collective-permute-start(bf16[512,512]{1,0:T(8,128)(2,1)S(1)} %get-tuple-element.12.refs_0_), channel_id=1, source_target_pairs={{0,2},{2,0},{1,3},{3,1},{4,6},{6,4},{5,7},{7,5},{8,10},{10,8},{9,1... | collective-permute-start | bytes 1572872 | tf_op jit(solution)/shard_map/ppermute | solution.py:22
  29.8 7.2 %collective-permute-start.22 = (bf16[512,256]{1,0:T(8,128)(2,1)S(1)}, bf16[512,256]{1,0:T(8,128)(2,1)S(1)}, u32[]{:S(2)}, u32[]{:S(2)}) collective-permute-start(bf16[512,256]{1,0:T(8,128)(2,1)S(1)} %collective-permute-done.21.refs_7_), channel_id=1, source_target_pairs={{0,8},{8,16},{16,24},{24,28},{28,20},{20,12},{12,4},{4,0},{1,9},{9... | collective-permute-start | bytes 786440 | tf_op jit(solution)/shard_map/ppermute | solution.py:391
  30.3 7.4 %collective-permute-start.18 = (bf16[512,256]{1,0:T(8,128)(2,1)S(1)}, bf16[512,256]{1,0:T(8,128)(2,1)S(1)}, u32[]{:S(2)}, u32[]{:S(2)}) collective-permute-start(bf16[512,256]{1,0:T(8,128)(2,1)S(1)} %collective-permute-done.17.refs_9_), channel_id=1, source_target_pairs={{8,0},{16,8},{24,16},{28,24},{20,28},{12,20},{4,12},{0,4},{9,1},{1... | collective-permute-start | bytes 786440 | tf_op jit(solution)/shard_map/ppermute | solution.py:391
  32.4 12.1 %collective-permute-start.6 = (bf16[256,512]{1,0:T(8,128)(2,1)S(1)}, bf16[256,512]{1,0:T(8,128)(2,1)S(1)}, u32[]{:S(2)}, u32[]{:S(2)}) collective-permute-start(bf16[256,512]{1,0:T(8,128)(2,1)S(1)} %constant_dynamic-update-slice_fusion.refs_0_.refs_4_), channel_id=1, source_target_pairs={{0,2},{2,0},{1,3},{3,1},{4,6},{6,4},{5,7},{7,5},{8,10},{10,8},{9,1... | collective-permute-start | bytes 786440 | tf_op jit(solution)/shard_map/ppermute | solution.py:22
  33.9 12.1 %collective-permute-start.5 = (bf16[256,512]{1,0:T(8,128)(2,1)S(1)}, bf16[256,512]{1,0:T(8,128)(2,1)S(1)}, u32[]{:S(2)}, u32[]{:S(2)}) collective-permute-start(bf16[256,512]{1,0:T(8,128)(2,1)S(1)} %constant_dynamic-update-slice_fusion.refs_0_.refs_4_), channel_id=1, source_target_pairs={{0,1},{1,0},{2,3},{3,2},{4,5},{5,4},{6,7},{7,6},{8,9},{9,8},{10,11... | collective-permute-start | bytes 786440 | tf_op jit(solution)/shard_map/ppermute | solution.py:22
  37.0 2.1 %collective-permute-start.9 = (bf16[128,512]{1,0:T(8,128)(2,1)S(1)}, bf16[128,512]{1,0:T(8,128)(2,1)S(1)}, u32[]{:S(2)}, u32[]{:S(2)}) collective-permute-start(bf16[128,512]{1,0:T(8,128)(2,1)S(1)} %collective-permute-done.8), channel_id=1, source_target_pairs={{16,24},{20,28},{17,25},{21,29},{18,26},{22,30},{19,27},{23,31}} | collective-permute-start | bytes 393224 | tf_op jit(solution)/shard_map/ppermute | solution.py:365
  37.7 13.1 %collective-permute-start.26 = (bf16[512,256]{1,0:T(8,128)(2,1)S(1)}, bf16[512,256]{1,0:T(8,128)(2,1)S(1)}, u32[]{:S(2)}, u32[]{:S(2)}) collective-permute-start(bf16[512,256]{1,0:T(8,128)(2,1)S(1)} %collective-permute-done.25.refs_6_.refs_12_), channel_id=1, source_target_pairs={{8,0},{16,8},{24,16},{28,24},{20,28},{12,20},{4,12},{0,4},{9,1},{1... | collective-permute-start | bytes 786440 | tf_op jit(solution)/shard_map/ppermute | solution.py:391
  39.1 12.4 %collective-permute-start.15 = (bf16[512,256]{1,0:T(8,128)(2,1)S(1)}, bf16[512,256]{1,0:T(8,128)(2,1)S(1)}, u32[]{:S(2)}, u32[]{:S(2)}) collective-permute-start(bf16[512,256]{1,0:T(8,128)(2,1)S(1)} %collective-permute-done.14.refs_4_.refs_10_), channel_id=1, source_target_pairs={{0,8},{8,16},{16,24},{24,28},{28,20},{20,12},{12,4},{4,0},{1,9},{9... | collective-permute-start | bytes 786440 | tf_op jit(solution)/shard_map/ppermute | solution.py:391
  44.5 5.0 %collective-permute-start.11 = (bf16[128,512]{1,0:T(8,128)(2,1)S(1)}, bf16[128,512]{1,0:T(8,128)(2,1)S(1)}, u32[]{:S(2)}, u32[]{:S(2)}) collective-permute-start(bf16[128,512]{1,0:T(8,128)(2,1)S(1)} %add.11.refs_0_.refs_8_), channel_id=1, source_target_pairs={{0,2},{2,0},{1,3},{3,1},{4,6},{6,4},{5,7},{7,5},{8,10},{10,8},{9,1... | collective-permute-start | bytes 393224 | tf_op jit(solution)/shard_map/ppermute | solution.py:22
  46.0 3.5 %collective-permute-start.10 = (bf16[128,512]{1,0:T(8,128)(2,1)S(1)}, bf16[128,512]{1,0:T(8,128)(2,1)S(1)}, u32[]{:S(2)}, u32[]{:S(2)}) collective-permute-start(bf16[128,512]{1,0:T(8,128)(2,1)S(1)} %add.11.refs_0_.refs_8_), channel_id=1, source_target_pairs={{0,1},{1,0},{2,3},{3,2},{4,5},{5,4},{6,7},{7,6},{8,9},{9,8},{10,11... | collective-permute-start | bytes 393224 | tf_op jit(solution)/shard_map/ppermute | solution.py:22
  46.0 18.7 %collective-permute-start = (bf16[512,512]{1,0:T(8,128)(2,1)S(1)}, bf16[512,512]{1,0:T(8,128)(2,1)S(1)}, u32[]{:S(2)}, u32[]{:S(2)}) collective-permute-start(bf16[512,512]{1,0:T(8,128)(2,1)S(1)} %get-tuple-element.12.refs_0_), channel_id=1, source_target_pairs={{0,1},{1,0},{2,3},{3,2},{4,5},{5,4},{6,7},{7,6},{8,9},{9,8},{10,11... | collective-permute-start | bytes 1572872 | tf_op jit(solution)/shard_map/ppermute | solution.py:22
  49.5 15.3 %collective-permute-start.2 = (bf16[512,512]{1,0:T(8,128)(2,1)S(1)}, bf16[512,512]{1,0:T(8,128)(2,1)S(1)}, u32[]{:S(2)}, u32[]{:S(2)}) collective-permute-start(bf16[512,512]{1,0:T(8,128)(2,1)S(1)} %collective-permute-done.1.refs_2_), channel_id=1, source_target_pairs={{0,1},{1,0},{2,3},{3,2},{4,5},{5,4},{6,7},{7,6},{8,9},{9,8},{10,11... | collective-permute-start | bytes 1572872 | tf_op jit(solution)/shard_map/ppermute | solution.py:22
  49.5 8.7 %collective-permute-start.23 = (bf16[512,256]{1,0:T(8,128)(2,1)S(1)}, bf16[512,256]{1,0:T(8,128)(2,1)S(1)}, u32[]{:S(2)}, u32[]{:S(2)}) collective-permute-start(bf16[512,256]{1,0:T(8,128)(2,1)S(1)} %collective-permute-done.22.refs_5_.refs_11_), channel_id=1, source_target_pairs={{0,8},{8,16},{16,24},{24,28},{28,20},{20,12},{12,4},{4,0},{1,9},{9... | collective-permute-start | bytes 786440 | tf_op jit(solution)/shard_map/ppermute | solution.py:391
  50.8 9.2 %collective-permute-start.19 = (bf16[512,256]{1,0:T(8,128)(2,1)S(1)}, bf16[512,256]{1,0:T(8,128)(2,1)S(1)}, u32[]{:S(2)}, u32[]{:S(2)}) collective-permute-start(bf16[512,256]{1,0:T(8,128)(2,1)S(1)} %collective-permute-done.18.refs_7_.refs_13_), channel_id=1, source_target_pairs={{8,0},{16,8},{24,16},{28,24},{20,28},{12,20},{4,12},{0,4},{9,1},{1... | collective-permute-start | bytes 786440 | tf_op jit(solution)/shard_map/ppermute | solution.py:391
  51.5 8.7 %collective-permute-start.7 = (bf16[256,512]{1,0:T(8,128)(2,1)S(1)}, bf16[256,512]{1,0:T(8,128)(2,1)S(1)}, u32[]{:S(2)}, u32[]{:S(2)}) collective-permute-start(bf16[256,512]{1,0:T(8,128)(2,1)S(1)} %collective-permute-done.6.refs_2_.refs_6_), channel_id=1, source_target_pairs={{0,1},{1,0},{2,3},{3,2},{4,5},{5,4},{6,7},{7,6},{8,9},{9,8},{10,11... | collective-permute-start | bytes 786440 | tf_op jit(solution)/shard_map/ppermute | solution.py:22
  58.2 9.5 %collective-permute-start.16 = (bf16[512,256]{1,0:T(8,128)(2,1)S(1)}, bf16[512,256]{1,0:T(8,128)(2,1)S(1)}, u32[]{:S(2)}, u32[]{:S(2)}) collective-permute-start(bf16[512,256]{1,0:T(8,128)(2,1)S(1)} %collective-permute-done.15.refs_4_.refs_14_), channel_id=1, source_target_pairs={{0,8},{8,16},{16,24},{24,28},{28,20},{20,12},{12,4},{4,0},{1,9},{9... | collective-permute-start | bytes 786440 | tf_op jit(solution)/shard_map/ppermute | solution.py:391
  60.0 7.9 %collective-permute-start.20 = (bf16[512,256]{1,0:T(8,128)(2,1)S(1)}, bf16[512,256]{1,0:T(8,128)(2,1)S(1)}, u32[]{:S(2)}, u32[]{:S(2)}) collective-permute-start(bf16[512,256]{1,0:T(8,128)(2,1)S(1)} %collective-permute-done.19.refs_7_.refs_17_), channel_id=1, source_target_pairs={{8,0},{16,8},{24,16},{28,24},{20,28},{12,20},{4,12},{0,4},{9,1},{1... | collective-permute-start | bytes 786440 | tf_op jit(solution)/shard_map/ppermute | solution.py:391
  60.2 3.1 %collective-permute-start.12 = (bf16[128,512]{1,0:T(8,128)(2,1)S(1)}, bf16[128,512]{1,0:T(8,128)(2,1)S(1)}, u32[]{:S(2)}, u32[]{:S(2)}) collective-permute-start(bf16[128,512]{1,0:T(8,128)(2,1)S(1)} %collective-permute-done.11.refs_2_.refs_10_), channel_id=1, source_target_pairs={{0,1},{1,0},{2,3},{3,2},{4,5},{5,4},{6,7},{7,6},{8,9},{9,8},{10,11... | collective-permute-start | bytes 393224 | tf_op jit(solution)/shard_map/ppermute | solution.py:22

commit v5 on v4

--- a/solution.py
+++ b/solution.py
@@ -40,6 +40,10 @@
     return [pltpu.with_memory_space_constraint(array, pltpu.VMEM) for array in arrays]
 
 
+def off_chip(*arrays):
+    return [pltpu.with_memory_space_constraint(array, pltpu.HBM) for array in arrays]
+
+
 def dot_last(left, right):
     return lax.dot_general(left, right, (((1,), (1,)), ((), ())), preferred_element_type=F32)
 
@@ -48,7 +52,15 @@
     return jnp.broadcast_to(row, (count, row.shape[1]))
 
 
-def prepare_kernel(q_ref, k_ref, w_ref, near_ref, score_ref, row_ref):
+def prepare_kernel(q_hbm, k_hbm, w_hbm, near_ref, score_ref, row_ref, q_ref, k_ref, w_ref, sems):
+    loads = [
+        pltpu.make_async_copy(source, target, sems.at[num])
+        for num, (source, target) in enumerate([(q_hbm, q_ref), (k_hbm, k_ref), (w_hbm, w_ref)])
+    ]
+    for load in loads:
+        load.start()
+    for load in loads:
+        load.wait()
     length = q_ref.shape[0]
     heads, _, rows = near_ref.shape
     tile = min(128, length)
@@ -119,54 +131,66 @@
     rows = min(256, length)
     return pl.pallas_call(
         prepare_kernel,
+        in_specs=[pl.BlockSpec(memory_space=pltpu.HBM)] * 3,
         out_shape=[
             pltpu.VMEM((heads, length, rows), BF16),
             pltpu.VMEM((length, length), BF16),
         ],
-        scratch_shapes=[pltpu.VMEM((heads, rows.bit_length(), length), F32)],
+        scratch_shapes=[
+            pltpu.VMEM((heads, rows.bit_length(), length), F32),
+            pltpu.VMEM(queries.shape, queries.dtype),
+            pltpu.VMEM(key_vectors.shape, key_vectors.dtype),
+            pltpu.VMEM(level_weight.shape, level_weight.dtype),
+            pltpu.SemaphoreType.DMA((3,)),
+        ],
         compiler_params=pltpu.CompilerParams(vmem_limit_bytes=16 << 20),
         name="prepare",
-    )(queries, key_vectors, level_weight)
-
-
-def turn_kernel(weight_ref, *part_refs):
+    )(*off_chip(queries, key_vectors, level_weight))
+
+
+def begin_kernel(k_hbm, token_hbm, weight_hbm, sum_ref, sent_ref, held_ref, *rest):
+    part_refs, (k_ref, weight_ref, sems) = rest[:-3], rest[-3:]
+    loads = [
+        pltpu.make_async_copy(source, target, sems.at[num])
+        for num, (source, target) in enumerate(
+            [(k_hbm, k_ref), (token_hbm, held_ref), (weight_hbm, weight_ref)]
+        )
+    ]
+    for load in loads:
+        load.start()
+    loads[0].wait()
+    loads[1].wait()
+    total = lax.dot_general(
+        k_ref[...], held_ref[...], (((0,), (0,)), ((), ())), preferred_element_type=F32
+    )
+    sum_ref[...] = total
+    sent_ref[...] = total.astype(BF16)
+    loads[2].wait()
     share = part_refs[0].shape[0]
     for num, part_ref in enumerate(part_refs):
         part_ref[...] = weight_ref[:, num * share : (num + 1) * share].T
 
 
-def turn(weight, split):
+def begin(key_vectors, tokens, weight, split):
     depth, width = weight.shape
-    return pl.pallas_call(
-        turn_kernel,
-        out_shape=[pltpu.VMEM((width // split, depth), weight.dtype)] * split,
-        compiler_params=pltpu.CompilerParams(vmem_limit_bytes=8 << 20),
-        name="turn",
-    )(weight)
-
-
-def begin_kernel(k_ref, token_ref, sum_ref, sent_ref, held_ref):
-    tokens = token_ref[...]
-    total = lax.dot_general(
-        k_ref[...], tokens, (((0,), (0,)), ((), ())), preferred_element_type=F32
-    )
-    sum_ref[...] = total
-    sent_ref[...] = total.astype(BF16)
-    held_ref[...] = tokens
-
-
-def begin(key_vectors, tokens):
     shape = (key_vectors.shape[1], tokens.shape[1])
     return pl.pallas_call(
         begin_kernel,
+        in_specs=[pl.BlockSpec(memory_space=pltpu.HBM)] * 3,
         out_shape=[
             pltpu.VMEM(shape, F32),
             pltpu.VMEM(shape, BF16),
             pltpu.VMEM(tokens.shape, tokens.dtype),
+        ]
+        + [pltpu.VMEM((width // split, depth), weight.dtype)] * split,
+        scratch_shapes=[
+            pltpu.VMEM(key_vectors.shape, key_vectors.dtype),
+            pltpu.VMEM(weight.shape, weight.dtype),
+            pltpu.SemaphoreType.DMA((3,)),
         ],
         compiler_params=pltpu.CompilerParams(vmem_limit_bytes=8 << 20),
         name="begin",
-    )(key_vectors, tokens)
+    )(*off_chip(key_vectors, tokens, weight))
 
 
 def ring_order(count):
@@ -348,7 +372,7 @@
     dev_bits = ctx_count.bit_length() - 1
     near = prepare(queries, key_vectors, level_weight)
 
-    running, sent, held = begin(key_vectors, tokens)
+    running, sent, held, *turned = begin(key_vectors, tokens, value_weight, 2)
     level_sums = []
     for section_bit in range(dev_bits):
         if section_bit > 0:
@@ -384,7 +408,7 @@
     token_pieces = on_chip(*gather_pieces(held, "head"))
     sum_pieces = [on_chip(*gather_pieces(low_sums, "head"))]
     sum_pieces += [on_chip(*gather_pieces(sums, "head")) for sums in top_sums]
-    cw = ccw = tuple(turn(value_weight, 2))
+    cw = ccw = tuple(turned)
     steps = [[(0, cw)]]
 
     def move(part, route):

time: 72.6 us -> 74.8 us (1.030); the launches traced: 72.4 us -> 73.6 us
  starting transfers between devices: 25.4 us -> 30.9 us
  waiting for transfers between devices: 31.3 us -> 27.5 us
  local copies, waits for them, and re-layouts: 3.07 us -> 0.15 us
  Pallas kernels: 12.4 us -> 14.7 us
    ppermute x14, starting transfers between devices: 14.2 us -> 20 us  [move(): return lax.ppermute(part, 'ctx', route)]
    ppermute x11, waiting for transfers between devices: 10.9 us -> 7 us  [from_partner(): return lax.ppermute(block, axis, route)]
    unnamed x13 -> x5, local copies, waits for them, and re-layouts: 3.06 us -> 0.14 us
    pallas_call x3 -> x2, Pallas kernels: 2.02 us -> 4.38 us  [the longest x1 2.79 us: prepare(): pl.pallas_call(prepare_kernel, in_specs=[pl.BlockSpec(memory_space=pltpu....]
  transfers between devices with their start and end apart: 27 -> 27, of which waited for: 10 -> 11; matrix products, arithmetic and copies ran while one was open for 0% -> 0% of each run, Pallas kernels for 10% -> 12%
where the time goes in v5:
time: 74.8 us; the launch traced here: 73.6 us
  starting transfers between devices  30.9 us (41%)
  waiting for transfers between devices  27.5 us (37%)
  Pallas kernels  14.7 us (20%)
    ppermute x14, waiting for transfers between devices, move(): return lax.ppermute(part, 'ctx', route)  20.5 us
    ppermute x14, starting transfers between devices, move(): return lax.ppermute(part, 'ctx', route)  20 us
    ppermute x11, starting transfers between devices, from_partner(): return lax.ppermute(block, axis, route)  9.6 us
    ppermute x11, waiting for transfers between devices, from_partner(): return lax.ppermute(block, axis, route)  7 us
    pallas_call x5, Pallas kernels, extend(): pl.pallas_call(functools.partial(extend_kernel, len(pieces), offsets, spl...  5.75 us
    pallas_call x1, Pallas kernels, finish(): pl.pallas_call(functools.partial(finish_kernel, len(token_pieces), len(st...  4.59 us
    pallas_call x1, Pallas kernels, prepare(): pl.pallas_call(prepare_kernel, in_specs=[pl.BlockSpec(memory_space=pltpu....  2.79 us
    pallas_call x1, Pallas kernels, begin(): pl.pallas_call(begin_kernel, in_specs=[pl.BlockSpec(memory_space=pltpu.HB...  1.59 us
  transfers between devices with their start and end apart: 27, of which 11 were waited for; matrix products, arithmetic and copies ran while one was open for 0% of the time, Pallas kernels for 12%

profile of v5, /device:TPU:0, one launch (start us, length us, event | category | flops | bytes accessed | tf_op | source)
XLA Modules:
  0.0 73.6 jit_solution(12274445425895097701)
XLA Ops:
  0.0 1.6 %begin.1 = (f32[128,512]{1,0:T(8,128)S(1)}, bf16[128,512]{1,0:T(8,128)(2,1)S(1)}, bf16[512,512]{1,0:T(8,128)(2,1)S(1)}, bf16[512,256]{1,0:T(8,128)(2,1)S(1)}, bf16[512,256]{1,0:T(8,128)(2,1)S(1)}) custom-call(bf16[512,128]{1,0:T(8,128)(2,1)} %k_hbm.3, bf16[512,512]{1,0:T(8,128)(2,1)} %token_hbm.1, bf16[256,1024]{1,0:T(8,128)(2,1)} %weight_hbm.1), custom_call_target="tpu_custom_call" | custom-call | tf_op jit(solution)/shard_map/begin/pallas_call | solution.py:177
  1.6 3.1 %collective-permute-start.3 = (bf16[128,512]{1,0:T(8,128)(2,1)S(1)}, bf16[128,512]{1,0:T(8,128)(2,1)S(1)}, u32[]{:S(2)}, u32[]{:S(2)}) collective-permute-start(bf16[128,512]{1,0:T(8,128)(2,1)S(1)} %get-tuple-element.13), channel_id=1, source_target_pairs={{0,4},{4,0},{8,12},{12,8},{16,20},{20,16},{24,28},{28,24},{1,5},{5... | collective-permute-start | bytes 393224 | tf_op jit(solution)/shard_map/ppermute | solution.py:22
  4.7 3.5 %collective-permute-done.3 = bf16[128,512]{1,0:T(8,128)(2,1)S(1)} collective-permute-done((bf16[128,512]{1,0:T(8,128)(2,1)S(1)}, bf16[128,512]{1,0:T(8,128)(2,1)S(1)}, u32[]{:S(2)}, u32[]{:S(2)}) %collective-permute-start.3) | collective-permute-done | bytes 131104 | tf_op jit(solution)/shard_map/ppermute | solution.py:22
  8.2 1.9 %collective-permute-start.4 = (bf16[128,512]{1,0:T(8,128)(2,1)S(1)}, bf16[128,512]{1,0:T(8,128)(2,1)S(1)}, u32[]{:S(2)}, u32[]{:S(2)}) collective-permute-start(bf16[128,512]{1,0:T(8,128)(2,1)S(1)} %fusion), channel_id=1, source_target_pairs={{0,8},{8,0},{4,12},{12,4},{16,24},{24,16},{20,28},{28,20},{1,9},{9... | collective-permute-start | bytes 393224 | tf_op jit(solution)/shard_map/ppermute | solution.py:22
  10.0 1.5 %collective-permute-start.24 = (bf16[512,256]{1,0:T(8,128)(2,1)S(1)}, bf16[512,256]{1,0:T(8,128)(2,1)S(1)}, u32[]{:S(2)}, u32[]{:S(2)}) collective-permute-start(bf16[512,256]{1,0:T(8,128)(2,1)S(1)} %get-tuple-element.15.refs_4_), channel_id=1, source_target_pairs={{8,0},{16,8},{24,16},{28,24},{20,28},{12,20},{4,12},{0,4},{9,1},{1... | collective-permute-start | bytes 786440 | tf_op jit(solution)/shard_map/ppermute | solution.py:415
  11.6 0.5 collective-permute-start.13
  12.1 1.1 %collective-permute-start.21 = (bf16[512,256]{1,0:T(8,128)(2,1)S(1)}, bf16[512,256]{1,0:T(8,128)(2,1)S(1)}, u32[]{:S(2)}, u32[]{:S(2)}) collective-permute-start(bf16[512,256]{1,0:T(8,128)(2,1)S(1)} %get-tuple-element.16.refs_5_), channel_id=1, source_target_pairs={{0,8},{8,16},{16,24},{24,28},{28,20},{20,12},{12,4},{4,0},{1,9},{9... | collective-permute-start | bytes 786440 | tf_op jit(solution)/shard_map/ppermute | solution.py:415
  13.2 0.9 %collective-permute-start.17 = (bf16[512,256]{1,0:T(8,128)(2,1)S(1)}, bf16[512,256]{1,0:T(8,128)(2,1)S(1)}, u32[]{:S(2)}, u32[]{:S(2)}) collective-permute-start(bf16[512,256]{1,0:T(8,128)(2,1)S(1)} %get-tuple-element.16.refs_5_), channel_id=1, source_target_pairs={{8,0},{16,8},{24,16},{28,24},{20,28},{12,20},{4,12},{0,4},{9,1},{1... | collective-permute-start | bytes 786440 | tf_op jit(solution)/shard_map/ppermute | solution.py:415
  14.1 0.5 collective-permute-done.4
  14.7 0.7 collective-permute-start.8
  15.4 4.9 %collective-permute-done.24.refs_8_ = bf16[512,256]{1,0:T(8,128)(2,1)S(1)} collective-permute-done((bf16[512,256]{1,0:T(8,128)(2,1)S(1)}, bf16[512,256]{1,0:T(8,128)(2,1)S(1)}, u32[]{:S(2)}, u32[]{:S(2)}) %collective-permute-start.24) | collective-permute-done | bytes 262176 | tf_op jit(solution)/shard_map/ppermute | solution.py:415
  20.2 1.7 %collective-permute-start.6 = (bf16[256,512]{1,0:T(8,128)(2,1)S(1)}, bf16[256,512]{1,0:T(8,128)(2,1)S(1)}, u32[]{:S(2)}, u32[]{:S(2)}) collective-permute-start(bf16[256,512]{1,0:T(8,128)(2,1)S(1)} %constant_dynamic-update-slice_fusion.refs_0_.refs_4_), channel_id=1, source_target_pairs={{0,2},{2,0},{1,3},{3,1},{4,6},{6,4},{5,7},{7,5},{8,10},{10,8},{9,1... | collective-permute-start | bytes 786440 | tf_op jit(solution)/shard_map/ppermute | solution.py:22
  22.0 0.0 collective-permute-start.5
  22.0 0.0 collective-permute-done.8
  22.0 0.7 collective-permute-start.9
  22.6 1.2 %collective-permute-done.21.refs_7_ = bf16[512,256]{1,0:T(8,128)(2,1)S(1)} collective-permute-done((bf16[512,256]{1,0:T(8,128)(2,1)S(1)}, bf16[512,256]{1,0:T(8,128)(2,1)S(1)}, u32[]{:S(2)}, u32[]{:S(2)}) %collective-permute-start.21) | collective-permute-done | bytes 262176 | tf_op jit(solution)/shard_map/ppermute | solution.py:415
  23.8 1.5 %collective-permute-start.1 = (bf16[512,512]{1,0:T(8,128)(2,1)S(1)}, bf16[512,512]{1,0:T(8,128)(2,1)S(1)}, u32[]{:S(2)}, u32[]{:S(2)}) collective-permute-start(bf16[512,512]{1,0:T(8,128)(2,1)S(1)} %get-tuple-element.12.refs_0_), channel_id=1, source_target_pairs={{0,2},{2,0},{1,3},{3,1},{4,6},{6,4},{5,7},{7,5},{8,10},{10,8},{9,1... | collective-permute-start | bytes 1572872 | tf_op jit(solution)/shard_map/ppermute | solution.py:22
  25.3 2.4 %collective-permute-start.25 = (bf16[512,256]{1,0:T(8,128)(2,1)S(1)}, bf16[512,256]{1,0:T(8,128)(2,1)S(1)}, u32[]{:S(2)}, u32[]{:S(2)}) collective-permute-start(bf16[512,256]{1,0:T(8,128)(2,1)S(1)} %collective-permute-done.24.refs_8_), channel_id=1, source_target_pairs={{8,0},{16,8},{24,16},{28,24},{20,28},{12,20},{4,12},{0,4},{9,1},{1... | collective-permute-start | bytes 786440 | tf_op jit(solution)/shard_map/ppermute | solution.py:415
  27.7 0.7 collective-permute-start.14
  28.4 0.0 collective-permute-done.6.refs_2_.refs_6_
  28.4 4.4 %collective-permute-start.22 = (bf16[512,256]{1,0:T(8,128)(2,1)S(1)}, bf16[512,256]{1,0:T(8,128)(2,1)S(1)}, u32[]{:S(2)}, u32[]{:S(2)}) collective-permute-start(bf16[512,256]{1,0:T(8,128)(2,1)S(1)} %collective-permute-done.21.refs_7_), channel_id=1, source_target_pairs={{0,8},{8,16},{16,24},{24,28},{28,20},{20,12},{12,4},{4,0},{1,9},{9... | collective-permute-start | bytes 786440 | tf_op jit(solution)/shard_map/ppermute | solution.py:415
  32.7 1.6 %collective-permute-done.25.refs_6_.refs_12_ = bf16[512,256]{1,0:T(8,128)(2,1)S(1)} collective-permute-done((bf16[512,256]{1,0:T(8,128)(2,1)S(1)}, bf16[512,256]{1,0:T(8,128)(2,1)S(1)}, u32[]{:S(2)}, u32[]{:S(2)}) %collective-permute-start.25) | collective-permute-done | bytes 262176 | tf_op jit(solution)/shard_map/ppermute | solution.py:415
  34.4 0.0 collective-permute-start.7
  34.4 2.6 %collective-permute-done.14.refs_4_.refs_10_ = bf16[512,256]{1,0:T(8,128)(2,1)S(1)} collective-permute-done((bf16[512,256]{1,0:T(8,128)(2,1)S(1)}, bf16[512,256]{1,0:T(8,128)(2,1)S(1)}, u32[]{:S(2)}, u32[]{:S(2)}) %collective-permute-start.14) | collective-permute-done | bytes 262176 | tf_op jit(solution)/shard_map/ppermute | solution.py:415
  37.0 2.7 %collective-permute-start.26 = (bf16[512,256]{1,0:T(8,128)(2,1)S(1)}, bf16[512,256]{1,0:T(8,128)(2,1)S(1)}, u32[]{:S(2)}, u32[]{:S(2)}) collective-permute-start(bf16[512,256]{1,0:T(8,128)(2,1)S(1)} %collective-permute-done.25.refs_6_.refs_12_), channel_id=1, source_target_pairs={{8,0},{16,8},{24,16},{28,24},{20,28},{12,20},{4,12},{0,4},{9,1},{1... | collective-permute-start | bytes 786440 | tf_op jit(solution)/shard_map/ppermute | solution.py:415
  39.7 0.1 collective-permute-done.22.refs_5_.refs_11_
  39.8 1.0 %collective-permute-start.11 = (bf16[128,512]{1,0:T(8,128)(2,1)S(1)}, bf16[128,512]{1,0:T(8,128)(2,1)S(1)}, u32[]{:S(2)}, u32[]{:S(2)}) collective-permute-start(bf16[128,512]{1,0:T(8,128)(2,1)S(1)} %add.11.refs_0_.refs_8_), channel_id=1, source_target_pairs={{0,2},{2,0},{1,3},{3,1},{4,6},{6,4},{5,7},{7,5},{8,10},{10,8},{9,1... | collective-permute-start | bytes 393224 | tf_op jit(solution)/shard_map/ppermute | solution.py:22
  40.7 0.5 collective-permute-done.18.refs_7_.refs_13_
  41.3 0.5 collective-permute-start
  41.8 3.0 %collective-permute-done.11.refs_2_.refs_10_ = bf16[128,512]{1,0:T(8,128)(2,1)S(1)} collective-permute-done((bf16[128,512]{1,0:T(8,128)(2,1)S(1)}, bf16[128,512]{1,0:T(8,128)(2,1)S(1)}, u32[]{:S(2)}, u32[]{:S(2)}) %collective-permute-start.11) | collective-permute-done | bytes 131104 | tf_op jit(solution)/shard_map/ppermute | solution.py:22
  44.8 1.2 %collective-permute-start.15 = (bf16[512,256]{1,0:T(8,128)(2,1)S(1)}, bf16[512,256]{1,0:T(8,128)(2,1)S(1)}, u32[]{:S(2)}, u32[]{:S(2)}) collective-permute-start(bf16[512,256]{1,0:T(8,128)(2,1)S(1)} %collective-permute-done.14.refs_4_.refs_10_), channel_id=1, source_target_pairs={{0,8},{8,16},{16,24},{24,28},{28,20},{20,12},{12,4},{4,0},{1,9},{9... | collective-permute-start | bytes 786440 | tf_op jit(solution)/shard_map/ppermute | solution.py:415
  45.9 1.6 %collective-permute-start.19 = (bf16[512,256]{1,0:T(8,128)(2,1)S(1)}, bf16[512,256]{1,0:T(8,128)(2,1)S(1)}, u32[]{:S(2)}, u32[]{:S(2)}) collective-permute-start(bf16[512,256]{1,0:T(8,128)(2,1)S(1)} %collective-permute-done.18.refs_7_.refs_13_), channel_id=1, source_target_pairs={{8,0},{16,8},{24,16},{28,24},{20,28},{12,20},{4,12},{0,4},{9,1},{1... | collective-permute-start | bytes 786440 | tf_op jit(solution)/shard_map/ppermute | solution.py:415
  47.5 1.0 %collective-permute-start.23 = (bf16[512,256]{1,0:T(8,128)(2,1)S(1)}, bf16[512,256]{1,0:T(8,128)(2,1)S(1)}, u32[]{:S(2)}, u32[]{:S(2)}) collective-permute-start(bf16[512,256]{1,0:T(8,128)(2,1)S(1)} %collective-permute-done.22.refs_5_.refs_11_), channel_id=1, source_target_pairs={{0,8},{8,16},{16,24},{24,28},{28,20},{20,12},{12,4},{4,0},{1,9},{9... | collective-permute-start | bytes 786440 | tf_op jit(solution)/shard_map/ppermute | solution.py:415
  48.6 6.0 %collective-permute-done.15.refs_4_.refs_14_ = bf16[512,256]{1,0:T(8,128)(2,1)S(1)} collective-permute-done((bf16[512,256]{1,0:T(8,128)(2,1)S(1)}, bf16[512,256]{1,0:T(8,128)(2,1)S(1)}, u32[]{:S(2)}, u32[]{:S(2)}) %collective-permute-start.15) | collective-permute-done | bytes 262176 | tf_op jit(solution)/shard_map/ppermute | solution.py:415
  54.6 0.6 collective-permute-start.16
  55.2 1.4 %collective-permute-start.20 = (bf16[512,256]{1,0:T(8,128)(2,1)S(1)}, bf16[512,256]{1,0:T(8,128)(2,1)S(1)}, u32[]{:S(2)}, u32[]{:S(2)}) collective-permute-start(bf16[512,256]{1,0:T(8,128)(2,1)S(1)} %collective-permute-done.19.refs_7_.refs_17_), channel_id=1, source_target_pairs={{8,0},{16,8},{24,16},{28,24},{20,28},{12,20},{4,12},{0,4},{9,1},{1... | collective-permute-start | bytes 786440 | tf_op jit(solution)/shard_map/ppermute | solution.py:415
  56.7 3.6 %collective-permute-done.23.refs_5_.refs_15_ = bf16[512,256]{1,0:T(8,128)(2,1)S(1)} collective-permute-done((bf16[512,256]{1,0:T(8,128)(2,1)S(1)}, bf16[512,256]{1,0:T(8,128)(2,1)S(1)}, u32[]{:S(2)}, u32[]{:S(2)}) %collective-permute-start.23) | collective-permute-done | bytes 262176 | tf_op jit(solution)/shard_map/ppermute | solution.py:415
  60.2 2.8 %prepare.1 = (bf16[16,512,256]{2,1,0:T(8,128)(2,1)S(1)}, bf16[512,512]{1,0:T(8,128)(2,1)S(1)}) custom-call(bf16[512,128]{1,0:T(8,128)(2,1)} %refs_17_.1, bf16[512,128]{1,0:T(8,128)(2,1)} %k_hbm.3, f32[13,16,512]{2,1,0:T(8,128)} %refs_18_.1), custom_call_target="tpu_custom_call" | custom-call | tf_op jit(solution)/shard_map/prepare/pallas_call | solution.py:132
  63.0 1.5 %shard_map.58.refs_15_ = f32[1024,256]{1,0:T(8,128)S(1)} custom-call(bf16[256,512]{1,0:T(8,128)(2,1)S(1)} %constant_dynamic-update-slice_fusion.refs_0_.refs_4_, bf16[256,512]{1,0:T(8,128)(2,1)S(1)} %collective-permute-done.5.refs_1_.refs_5_, bf16[256,512]{1,0:T(8,128)(2,1)S(1)} %collective-permute-done.6.refs_2_.refs_6_, ...), custom_call_target="tpu_custom_call" | custom-call | tf_op jit(solution)/shard_map/pallas_call | solution.py:248
  64.5 1.4 %shard_map.59.refs_16_ = f32[1024,128]{1,0:T(8,128)S(1)} custom-call(bf16[128,512]{1,0:T(8,128)(2,1)S(1)} %add.11.refs_0_.refs_8_, bf16[128,512]{1,0:T(8,128)(2,1)S(1)} %collective-permute-done.10.refs_1_.refs_9_, bf16[128,512]{1,0:T(8,128)(2,1)S(1)} %collective-permute-done.11.refs_2_.refs_10_, ...), custom_call_target="tpu_custom_call" | custom-call | tf_op jit(solution)/shard_map/pallas_call | solution.py:248
  65.9 1.2 %shard_map.55.refs_8_ = f32[1024,512]{1,0:T(8,128)S(1)} custom-call(bf16[512,512]{1,0:T(8,128)(2,1)S(1)} %get-tuple-element.12.refs_0_, bf16[512,512]{1,0:T(8,128)(2,1)S(1)} %collective-permute-done.refs_1_, bf16[512,512]{1,0:T(8,128)(2,1)S(1)} %collective-permute-done.1.refs_2_, bf16[512,512]{1,0:T(8,128)(2,1)S(1)} %collective-permute-done.2.refs_3_, ...), custom_call_target="tpu_custom_call" | custom-call | tf_op jit(solution)/shard_map/pallas_call | solution.py:248
  67.1 0.9 %shard_map.56.refs_8_ = f32[1024,512]{1,0:T(8,128)S(1)} custom-call(bf16[512,512]{1,0:T(8,128)(2,1)S(1)} %get-tuple-element.12.refs_0_, bf16[512,512]{1,0:T(8,128)(2,1)S(1)} %collective-permute-done.refs_1_, bf16[512,512]{1,0:T(8,128)(2,1)S(1)} %collective-permute-done.1.refs_2_, bf16[512,512]{1,0:T(8,128)(2,1)S(1)} %collective-permute-done.2.refs_3_, ...), custom_call_target="tpu_custom_call" | custom-call | tf_op jit(solution)/shard_map/pallas_call | solution.py:248
  68.0 0.0 copy-start
  68.0 0.0 copy-start.1
  68.0 0.9 %shard_map.57.refs_14_ = f32[1024,512]{1,0:T(8,128)S(1)} custom-call(bf16[512,512]{1,0:T(8,128)(2,1)S(1)} %get-tuple-element.12.refs_0_, bf16[512,512]{1,0:T(8,128)(2,1)S(1)} %collective-permute-done.refs_1_, bf16[512,512]{1,0:T(8,128)(2,1)S(1)} %collective-permute-done.1.refs_2_, bf16[512,512]{1,0:T(8,128)(2,1)S(1)} %collective-permute-done.2.refs_3_, ...), custom_call_target="tpu_custom_call" | custom-call | tf_op jit(solution)/shard_map/pallas_call | solution.py:248
  68.9 0.1 copy-done
  69.0 0.0 copy-done.1
  69.0 4.6 %finish.1 = bf16[512,1024]{1,0:T(8,128)(2,1)} custom-call(bf16[512,512]{1,0:T(8,128)(2,1)S(1)} %get-tuple-element.12.refs_0_, bf16[512,512]{1,0:T(8,128)(2,1)S(1)} %collective-permute-done.refs_1_, bf16[512,512]{1,0:T(8,128)(2,1)S(1)} %collective-permute-done.1.refs_2_, bf16[512,512]{1,0:T(8,128)(2,1)S(1)} %collective-permute-done.2.refs_3_, ...), custom_call_target="tpu_custom_call" | custom-call | tf_op jit(solution)/shard_map/finish/pallas_call | solution.py:354
  (23 shorter events, 0.2 us)
Async XLA Ops:
  1.6 6.6 %collective-permute-start.3 = (bf16[128,512]{1,0:T(8,128)(2,1)S(1)}, bf16[128,512]{1,0:T(8,128)(2,1)S(1)}, u32[]{:S(2)}, u32[]{:S(2)}) collective-permute-start(bf16[128,512]{1,0:T(8,128)(2,1)S(1)} %get-tuple-element.13), channel_id=1, source_target_pairs={{0,4},{4,0},{8,12},{12,8},{16,20},{20,16},{24,28},{28,24},{1,5},{5... | collective-permute-start | bytes 393224 | tf_op jit(solution)/shard_map/ppermute | solution.py:22
  8.2 6.4 %collective-permute-start.4 = (bf16[128,512]{1,0:T(8,128)(2,1)S(1)}, bf16[128,512]{1,0:T(8,128)(2,1)S(1)}, u32[]{:S(2)}, u32[]{:S(2)}) collective-permute-start(bf16[128,512]{1,0:T(8,128)(2,1)S(1)} %fusion), channel_id=1, source_target_pairs={{0,8},{8,0},{4,12},{12,4},{16,24},{24,16},{20,28},{28,20},{1,9},{9... | collective-permute-start | bytes 393224 | tf_op jit(solution)/shard_map/ppermute | solution.py:22
  10.0 10.2 %collective-permute-start.24 = (bf16[512,256]{1,0:T(8,128)(2,1)S(1)}, bf16[512,256]{1,0:T(8,128)(2,1)S(1)}, u32[]{:S(2)}, u32[]{:S(2)}) collective-permute-start(bf16[512,256]{1,0:T(8,128)(2,1)S(1)} %get-tuple-element.15.refs_4_), channel_id=1, source_target_pairs={{8,0},{16,8},{24,16},{28,24},{20,28},{12,20},{4,12},{0,4},{9,1},{1... | collective-permute-start | bytes 786440 | tf_op jit(solution)/shard_map/ppermute | solution.py:415
  11.6 10.4 %collective-permute-start.13 = (bf16[512,256]{1,0:T(8,128)(2,1)S(1)}, bf16[512,256]{1,0:T(8,128)(2,1)S(1)}, u32[]{:S(2)}, u32[]{:S(2)}) collective-permute-start(bf16[512,256]{1,0:T(8,128)(2,1)S(1)} %get-tuple-element.15.refs_4_), channel_id=1, source_target_pairs={{0,8},{8,16},{16,24},{24,28},{28,20},{20,12},{12,4},{4,0},{1,9},{9... | collective-permute-start | bytes 786440 | tf_op jit(solution)/shard_map/ppermute | solution.py:415
  12.1 11.7 %collective-permute-start.21 = (bf16[512,256]{1,0:T(8,128)(2,1)S(1)}, bf16[512,256]{1,0:T(8,128)(2,1)S(1)}, u32[]{:S(2)}, u32[]{:S(2)}) collective-permute-start(bf16[512,256]{1,0:T(8,128)(2,1)S(1)} %get-tuple-element.16.refs_5_), channel_id=1, source_target_pairs={{0,8},{8,16},{16,24},{24,28},{28,20},{20,12},{12,4},{4,0},{1,9},{9... | collective-permute-start | bytes 786440 | tf_op jit(solution)/shard_map/ppermute | solution.py:415
  13.2 12.1 %collective-permute-start.17 = (bf16[512,256]{1,0:T(8,128)(2,1)S(1)}, bf16[512,256]{1,0:T(8,128)(2,1)S(1)}, u32[]{:S(2)}, u32[]{:S(2)}) collective-permute-start(bf16[512,256]{1,0:T(8,128)(2,1)S(1)} %get-tuple-element.16.refs_5_), channel_id=1, source_target_pairs={{8,0},{16,8},{24,16},{28,24},{20,28},{12,20},{4,12},{0,4},{9,1},{1... | collective-permute-start | bytes 786440 | tf_op jit(solution)/shard_map/ppermute | solution.py:415
  14.7 7.3 %collective-permute-start.8 = (bf16[128,512]{1,0:T(8,128)(2,1)S(1)}, bf16[128,512]{1,0:T(8,128)(2,1)S(1)}, u32[]{:S(2)}, u32[]{:S(2)}) collective-permute-start(bf16[128,512]{1,0:T(8,128)(2,1)S(1)} %add_convert_fusion), channel_id=1, source_target_pairs={{8,16},{12,20},{9,17},{13,21},{10,18},{14,22},{11,19},{15,23}} | collective-permute-start | bytes 393224 | tf_op jit(solution)/shard_map/ppermute | solution.py:389
  20.2 8.1 %collective-permute-start.6 = (bf16[256,512]{1,0:T(8,128)(2,1)S(1)}, bf16[256,512]{1,0:T(8,128)(2,1)S(1)}, u32[]{:S(2)}, u32[]{:S(2)}) collective-permute-start(bf16[256,512]{1,0:T(8,128)(2,1)S(1)} %constant_dynamic-update-slice_fusion.refs_0_.refs_4_), channel_id=1, source_target_pairs={{0,2},{2,0},{1,3},{3,1},{4,6},{6,4},{5,7},{7,5},{8,10},{10,8},{9,1... | collective-permute-start | bytes 786440 | tf_op jit(solution)/shard_map/ppermute | solution.py:22
  22.0 10.8 %collective-permute-start.5 = (bf16[256,512]{1,0:T(8,128)(2,1)S(1)}, bf16[256,512]{1,0:T(8,128)(2,1)S(1)}, u32[]{:S(2)}, u32[]{:S(2)}) collective-permute-start(bf16[256,512]{1,0:T(8,128)(2,1)S(1)} %constant_dynamic-update-slice_fusion.refs_0_.refs_4_), channel_id=1, source_target_pairs={{0,1},{1,0},{2,3},{3,2},{4,5},{5,4},{6,7},{7,6},{8,9},{9,8},{10,11... | collective-permute-start | bytes 786440 | tf_op jit(solution)/shard_map/ppermute | solution.py:22
  22.0 5.7 %collective-permute-start.9 = (bf16[128,512]{1,0:T(8,128)(2,1)S(1)}, bf16[128,512]{1,0:T(8,128)(2,1)S(1)}, u32[]{:S(2)}, u32[]{:S(2)}) collective-permute-start(bf16[128,512]{1,0:T(8,128)(2,1)S(1)} %collective-permute-done.8), channel_id=1, source_target_pairs={{16,24},{20,28},{17,25},{21,29},{18,26},{22,30},{19,27},{23,31}} | collective-permute-start | bytes 393224 | tf_op jit(solution)/shard_map/ppermute | solution.py:389
  23.8 17.5 %collective-permute-start.1 = (bf16[512,512]{1,0:T(8,128)(2,1)S(1)}, bf16[512,512]{1,0:T(8,128)(2,1)S(1)}, u32[]{:S(2)}, u32[]{:S(2)}) collective-permute-start(bf16[512,512]{1,0:T(8,128)(2,1)S(1)} %get-tuple-element.12.refs_0_), channel_id=1, source_target_pairs={{0,2},{2,0},{1,3},{3,1},{4,6},{6,4},{5,7},{7,5},{8,10},{10,8},{9,1... | collective-permute-start | bytes 1572872 | tf_op jit(solution)/shard_map/ppermute | solution.py:22
  25.3 9.1 %collective-permute-start.25 = (bf16[512,256]{1,0:T(8,128)(2,1)S(1)}, bf16[512,256]{1,0:T(8,128)(2,1)S(1)}, u32[]{:S(2)}, u32[]{:S(2)}) collective-permute-start(bf16[512,256]{1,0:T(8,128)(2,1)S(1)} %collective-permute-done.24.refs_8_), channel_id=1, source_target_pairs={{8,0},{16,8},{24,16},{28,24},{20,28},{12,20},{4,12},{0,4},{9,1},{1... | collective-permute-start | bytes 786440 | tf_op jit(solution)/shard_map/ppermute | solution.py:415
  27.7 9.3 %collective-permute-start.14 = (bf16[512,256]{1,0:T(8,128)(2,1)S(1)}, bf16[512,256]{1,0:T(8,128)(2,1)S(1)}, u32[]{:S(2)}, u32[]{:S(2)}) collective-permute-start(bf16[512,256]{1,0:T(8,128)(2,1)S(1)} %collective-permute-done.13.refs_6_), channel_id=1, source_target_pairs={{0,8},{8,16},{16,24},{24,28},{28,20},{20,12},{12,4},{4,0},{1,9},{9... | collective-permute-start | bytes 786440 | tf_op jit(solution)/shard_map/ppermute | solution.py:415
  28.4 11.4 %collective-permute-start.22 = (bf16[512,256]{1,0:T(8,128)(2,1)S(1)}, bf16[512,256]{1,0:T(8,128)(2,1)S(1)}, u32[]{:S(2)}, u32[]{:S(2)}) collective-permute-start(bf16[512,256]{1,0:T(8,128)(2,1)S(1)} %collective-permute-done.21.refs_7_), channel_id=1, source_target_pairs={{0,8},{8,16},{16,24},{24,28},{28,20},{20,12},{12,4},{4,0},{1,9},{9... | collective-permute-start | bytes 786440 | tf_op jit(solution)/shard_map/ppermute | solution.py:415
  32.7 8.5 %collective-permute-start.18 = (bf16[512,256]{1,0:T(8,128)(2,1)S(1)}, bf16[512,256]{1,0:T(8,128)(2,1)S(1)}, u32[]{:S(2)}, u32[]{:S(2)}) collective-permute-start(bf16[512,256]{1,0:T(8,128)(2,1)S(1)} %collective-permute-done.17.refs_9_), channel_id=1, source_target_pairs={{8,0},{16,8},{24,16},{28,24},{20,28},{12,20},{4,12},{0,4},{9,1},{1... | collective-permute-start | bytes 786440 | tf_op jit(solution)/shard_map/ppermute | solution.py:415
  34.4 11.5 %collective-permute-start.7 = (bf16[256,512]{1,0:T(8,128)(2,1)S(1)}, bf16[256,512]{1,0:T(8,128)(2,1)S(1)}, u32[]{:S(2)}, u32[]{:S(2)}) collective-permute-start(bf16[256,512]{1,0:T(8,128)(2,1)S(1)} %collective-permute-done.6.refs_2_.refs_6_), channel_id=1, source_target_pairs={{0,1},{1,0},{2,3},{3,2},{4,5},{5,4},{6,7},{7,6},{8,9},{9,8},{10,11... | collective-permute-start | bytes 786440 | tf_op jit(solution)/shard_map/ppermute | solution.py:22
  37.0 10.6 %collective-permute-start.26 = (bf16[512,256]{1,0:T(8,128)(2,1)S(1)}, bf16[512,256]{1,0:T(8,128)(2,1)S(1)}, u32[]{:S(2)}, u32[]{:S(2)}) collective-permute-start(bf16[512,256]{1,0:T(8,128)(2,1)S(1)} %collective-permute-done.25.refs_6_.refs_12_), channel_id=1, source_target_pairs={{8,0},{16,8},{24,16},{28,24},{20,28},{12,20},{4,12},{0,4},{9,1},{1... | collective-permute-start | bytes 786440 | tf_op jit(solution)/shard_map/ppermute | solution.py:415
  39.8 5.0 %collective-permute-start.11 = (bf16[128,512]{1,0:T(8,128)(2,1)S(1)}, bf16[128,512]{1,0:T(8,128)(2,1)S(1)}, u32[]{:S(2)}, u32[]{:S(2)}) collective-permute-start(bf16[128,512]{1,0:T(8,128)(2,1)S(1)} %add.11.refs_0_.refs_8_), channel_id=1, source_target_pairs={{0,2},{2,0},{1,3},{3,1},{4,6},{6,4},{5,7},{7,5},{8,10},{10,8},{9,1... | collective-permute-start | bytes 393224 | tf_op jit(solution)/shard_map/ppermute | solution.py:22
  41.3 3.5 %collective-permute-start.10 = (bf16[128,512]{1,0:T(8,128)(2,1)S(1)}, bf16[128,512]{1,0:T(8,128)(2,1)S(1)}, u32[]{:S(2)}, u32[]{:S(2)}) collective-permute-start(bf16[128,512]{1,0:T(8,128)(2,1)S(1)} %add.11.refs_0_.refs_8_), channel_id=1, source_target_pairs={{0,1},{1,0},{2,3},{3,2},{4,5},{5,4},{6,7},{7,6},{8,9},{9,8},{10,11... | collective-permute-start | bytes 393224 | tf_op jit(solution)/shard_map/ppermute | solution.py:22
  41.3 24.7 %collective-permute-start = (bf16[512,512]{1,0:T(8,128)(2,1)S(1)}, bf16[512,512]{1,0:T(8,128)(2,1)S(1)}, u32[]{:S(2)}, u32[]{:S(2)}) collective-permute-start(bf16[512,512]{1,0:T(8,128)(2,1)S(1)} %get-tuple-element.12.refs_0_), channel_id=1, source_target_pairs={{0,1},{1,0},{2,3},{3,2},{4,5},{5,4},{6,7},{7,6},{8,9},{9,8},{10,11... | collective-permute-start | bytes 1572872 | tf_op jit(solution)/shard_map/ppermute | solution.py:22
  44.8 21.2 %collective-permute-start.2 = (bf16[512,512]{1,0:T(8,128)(2,1)S(1)}, bf16[512,512]{1,0:T(8,128)(2,1)S(1)}, u32[]{:S(2)}, u32[]{:S(2)}) collective-permute-start(bf16[512,512]{1,0:T(8,128)(2,1)S(1)} %collective-permute-done.1.refs_2_), channel_id=1, source_target_pairs={{0,1},{1,0},{2,3},{3,2},{4,5},{5,4},{6,7},{7,6},{8,9},{9,8},{10,11... | collective-permute-start | bytes 1572872 | tf_op jit(solution)/shard_map/ppermute | solution.py:22
  44.8 9.9 %collective-permute-start.15 = (bf16[512,256]{1,0:T(8,128)(2,1)S(1)}, bf16[512,256]{1,0:T(8,128)(2,1)S(1)}, u32[]{:S(2)}, u32[]{:S(2)}) collective-permute-start(bf16[512,256]{1,0:T(8,128)(2,1)S(1)} %collective-permute-done.14.refs_4_.refs_10_), channel_id=1, source_target_pairs={{0,8},{8,16},{16,24},{24,28},{28,20},{20,12},{12,4},{4,0},{1,9},{9... | collective-permute-start | bytes 786440 | tf_op jit(solution)/shard_map/ppermute | solution.py:415
  45.9 9.3 %collective-permute-start.19 = (bf16[512,256]{1,0:T(8,128)(2,1)S(1)}, bf16[512,256]{1,0:T(8,128)(2,1)S(1)}, u32[]{:S(2)}, u32[]{:S(2)}) collective-permute-start(bf16[512,256]{1,0:T(8,128)(2,1)S(1)} %collective-permute-done.18.refs_7_.refs_13_), channel_id=1, source_target_pairs={{8,0},{16,8},{24,16},{28,24},{20,28},{12,20},{4,12},{0,4},{9,1},{1... | collective-permute-start | bytes 786440 | tf_op jit(solution)/shard_map/ppermute | solution.py:415
  47.5 12.7 %collective-permute-start.23 = (bf16[512,256]{1,0:T(8,128)(2,1)S(1)}, bf16[512,256]{1,0:T(8,128)(2,1)S(1)}, u32[]{:S(2)}, u32[]{:S(2)}) collective-permute-start(bf16[512,256]{1,0:T(8,128)(2,1)S(1)} %collective-permute-done.22.refs_5_.refs_11_), channel_id=1, source_target_pairs={{0,8},{8,16},{16,24},{24,28},{28,20},{20,12},{12,4},{4,0},{1,9},{9... | collective-permute-start | bytes 786440 | tf_op jit(solution)/shard_map/ppermute | solution.py:415
  54.6 14.3 %collective-permute-start.16 = (bf16[512,256]{1,0:T(8,128)(2,1)S(1)}, bf16[512,256]{1,0:T(8,128)(2,1)S(1)}, u32[]{:S(2)}, u32[]{:S(2)}) collective-permute-start(bf16[512,256]{1,0:T(8,128)(2,1)S(1)} %collective-permute-done.15.refs_4_.refs_14_), channel_id=1, source_target_pairs={{0,8},{8,16},{16,24},{24,28},{28,20},{20,12},{12,4},{4,0},{1,9},{9... | collective-permute-start | bytes 786440 | tf_op jit(solution)/shard_map/ppermute | solution.py:415
  55.2 13.7 %collective-permute-start.20 = (bf16[512,256]{1,0:T(8,128)(2,1)S(1)}, bf16[512,256]{1,0:T(8,128)(2,1)S(1)}, u32[]{:S(2)}, u32[]{:S(2)}) collective-permute-start(bf16[512,256]{1,0:T(8,128)(2,1)S(1)} %collective-permute-done.19.refs_7_.refs_17_), channel_id=1, source_target_pairs={{8,0},{16,8},{24,16},{28,24},{20,28},{12,20},{4,12},{0,4},{9,1},{1... | collective-permute-start | bytes 786440 | tf_op jit(solution)/shard_map/ppermute | solution.py:415
  60.2 4.3 %collective-permute-start.12 = (bf16[128,512]{1,0:T(8,128)(2,1)S(1)}, bf16[128,512]{1,0:T(8,128)(2,1)S(1)}, u32[]{:S(2)}, u32[]{:S(2)}) collective-permute-start(bf16[128,512]{1,0:T(8,128)(2,1)S(1)} %collective-permute-done.11.refs_2_.refs_10_), channel_id=1, source_target_pairs={{0,1},{1,0},{2,3},{3,2},{4,5},{5,4},{6,7},{7,6},{8,9},{9,8},{10,11... | collective-permute-start | bytes 393224 | tf_op jit(solution)/shard_map/ppermute | solution.py:22
  68.0 1.0 %copy-start = (f32[13,16,512]{2,1,0:T(8,128)S(1)}, f32[13,16,512]{2,1,0:T(8,128)}, u32[]{:S(2)}) copy-start(f32[13,16,512]{2,1,0:T(8,128)} %refs_18_.1) | copy-start | bytes 1277956
  68.0 1.0 %copy-start.1 = (bf16[512,128]{1,0:T(8,128)(2,1)S(1)}, bf16[512,128]{1,0:T(8,128)(2,1)}, u32[]{:S(2)}) copy-start(bf16[512,128]{1,0:T(8,128)(2,1)} %refs_17_.1) | copy-start | bytes 393220

commit v6 on v5

--- a/solution.py
+++ b/solution.py
@@ -218,40 +218,43 @@
                 chosen_ref[:, num * depth : (num + 1) * depth] = ref[:, pl.ds(start, depth)]
 
 
-def extend_kernel(piece_count, offsets, split, started, *refs):
-    count = len(offsets)
-    pieces = refs[:piece_count]
-    blocks = [refs[piece_count + num * split :][:split] for num in range(count)]
-    out_ref, chosen_ref = refs[-2], refs[-1]
+def extend_kernel(sizes, offsets, split, started, *refs):
+    refs = list(refs)
+    take = lambda count: [refs.pop(0) for _ in range(count)]
+    groups = [take(size) for size in sizes]
+    blocks = [take(split) for _ in offsets]
+    totals = take(len(sizes)) if started else []
+    out_refs, chosen_refs = take(len(sizes)), refs
     share, depth = blocks[0][0].shape
-    choose(offsets, pieces, depth, chosen_ref)
-    width = out_ref.shape[0]
+    for pieces, chosen_ref in zip(groups, chosen_refs):
+        choose(offsets, pieces, depth, chosen_ref)
     step = min(256, share)
-    for c0 in range(0, width, step):
+    for c0 in range(0, share * split, step):
         at = c0 % share
         left = jnp.concatenate(
             [block[c0 // share][at : at + step, :] for block in blocks], axis=1
         )
-        total = dot_last(left, chosen_ref[...])
-        if started:
-            total = total + refs[piece_count + count * split][c0 : c0 + step, :]
-        out_ref[c0 : c0 + step, :] = total
-
-
-def extend(total, pieces, parts):
+        for num, (out_ref, chosen_ref) in enumerate(zip(out_refs, chosen_refs)):
+            total = dot_last(left, chosen_ref[...])
+            if started:
+                total = total + totals[num][c0 : c0 + step, :]
+            out_ref[c0 : c0 + step, :] = total
+
+
+def extend(totals, groups, parts):
     offsets = tuple(offset for offset, _ in parts)
     blocks = [half for _, block in parts for half in block]
     split = len(parts[0][1])
-    rows = pieces[0].shape[0]
     share, depth = blocks[0].shape
-    arrays = [*pieces, *blocks, *([] if total is None else [total])]
+    arrays = [*(piece for pieces in groups for piece in pieces), *blocks, *totals]
+    rows = [pieces[0].shape[0] for pieces in groups]
     return pl.pallas_call(
         functools.partial(
-            extend_kernel, len(pieces), offsets, split, total is not None
+            extend_kernel, [len(pieces) for pieces in groups], offsets, split, len(totals) > 0
         ),
         in_specs=[pl.BlockSpec(memory_space=pltpu.VMEM)] * len(arrays),
-        out_shape=pltpu.VMEM((share * split, rows), F32),
-        scratch_shapes=[pltpu.VMEM((rows, depth * len(parts)), BF16)],
+        out_shape=[pltpu.VMEM((share * split, count), F32) for count in rows],
+        scratch_shapes=[pltpu.VMEM((count, depth * len(parts)), BF16) for count in rows],
         compiler_params=pltpu.CompilerParams(vmem_limit_bytes=12 << 20),
     )(*arrays)
 
@@ -262,7 +265,8 @@
     token_refs, sum_refs = take(piece_count), [take(piece_count) for _ in range(groups)]
     last_refs = take(last_count)
     value_ref, state_refs = refs.pop(0), take(groups)
-    q_ref, w_ref, near_ref, score_ref, out_ref = take(5)
+    q_ref, w_ref, near_ref, score_ref, out_hbm = take(5)
+    out_ref, sems = refs.pop(), refs.pop()
     length, state_rows = q_ref.shape
     width = value_ref.shape[0]
     near_levels = length.bit_length()
@@ -278,10 +282,7 @@
     queries = q_ref[...]
     twice = jnp.concatenate([queries, queries], axis=1)
     step = min(256, width)
-    unit = (
-        lax.broadcasted_iota(jnp.int32, (rows, rows), 0)
-        == lax.broadcasted_iota(jnp.int32, (rows, rows), 1)
-    ).astype(BF16)
+    stores = []
     for c0 in range(0, width, step):
         values = value_ref[c0 : c0 + step, :]
         states = [ref[c0 : c0 + step, :] for ref in state_refs]
@@ -338,9 +339,15 @@
                         preferred_element_type=F32,
                     )
                     total = total + weight(level, t0, t0 + rows) * mixed
-            out_ref[t0 : t0 + rows, c0 : c0 + step] = dot_last(unit, total.astype(BF16)).astype(
-                BF16
+            out_ref[t0 : t0 + rows, c0 : c0 + step] = total.astype(BF16).T
+        stores.append(
+            pltpu.make_async_copy(
+                out_ref.at[:, c0 : c0 + step], out_hbm.at[:, c0 : c0 + step], sems.at[len(stores)]
             )
+        )
+        stores[-1].start()
+    for store in stores:
+        store.wait()
 
 
 def finish(values, states, offset, last, token_pieces, sum_pieces, queries, level_weight, near, head_size):
@@ -351,12 +358,17 @@
     if last:
         depth = last[0].shape[1]
         scratch = [pltpu.VMEM((rows, depth), BF16) for rows in [length, *(s.shape[1] for s in states)]]
+    scratch += [
+        pltpu.SemaphoreType.DMA((max(1, width // 256),)),
+        pltpu.VMEM((length, width), BF16),
+    ]
     return pl.pallas_call(
         functools.partial(
             finish_kernel, len(token_pieces), len(states), offset, len(last), head_size
         ),
         in_specs=[pl.BlockSpec(memory_space=pltpu.VMEM)] * len(arrays),
         out_shape=jax.ShapeDtypeStruct((length, width), BF16),
+        out_specs=pl.BlockSpec(memory_space=pltpu.HBM),
         scratch_shapes=scratch,
         compiler_params=pltpu.CompilerParams(vmem_limit_bytes=24 << 20),
         name="finish",
@@ -419,11 +431,14 @@
         ccw = tuple(move(part, back) for part in ccw)
         steps.append([(-step, on_chip(*cw)), (step, on_chip(*ccw))])
     last = on_chip(move(cw[0], ahead), move(ccw[1], back))
-    values = extend(None, token_pieces, steps[0] + steps[1])
-    for step in range(2, half_count):
-        values = extend(values, token_pieces, steps[step])
-    every = [part for parts in steps for part in parts]
-    states = [extend(None, pieces, every) for pieces in sum_pieces]
+    values = extend([], [token_pieces], steps[0] + steps[1])
+    for step in range(2, half_count - 1):
+        values = extend(values, [token_pieces], steps[step])
+    early = [part for parts in steps[:-1] for part in parts]
+    low = extend([], sum_pieces[:1], early)
+    values, low = extend([*values, *low], [token_pieces, sum_pieces[0]], steps[-1])
+    top = [extend([], [pieces], early + steps[-1])[0] for pieces in sum_pieces[1:]]
+    states = [low, *top]
     return finish(
         values,
         states,

time: 74.8 us -> 73.8 us (0.987)
  Pallas kernels: 14.7 us -> 13.8 us
    pallas_call x1, Pallas kernels: 4.59 us -> 3.71 us  [finish(): pl.pallas_call(functools.partial(finish_kernel, len(token_pieces), len(st...]
where the time goes in v6:
time: 73.8 us; the launch traced here: 72.6 us
  starting transfers between devices  30.9 us (42%)
  waiting for transfers between devices  27.5 us (37%)
  Pallas kernels  13.8 us (19%)
    ppermute x14, waiting for transfers between devices, move(): return lax.ppermute(part, 'ctx', route)  20.5 us
    ppermute x14, starting transfers between devices, move(): return lax.ppermute(part, 'ctx', route)  20 us
    ppermute x11, starting transfers between devices, from_partner(): return lax.ppermute(block, axis, route)  9.6 us
    ppermute x11, waiting for transfers between devices, from_partner(): return lax.ppermute(block, axis, route)  7 us
    pallas_call x5, Pallas kernels, extend(): pl.pallas_call(functools.partial(extend_kernel, [len(pieces) for pieces i...  5.69 us
    pallas_call x1, Pallas kernels, finish(): pl.pallas_call(functools.partial(finish_kernel, len(token_pieces), len(st...  3.71 us
    pallas_call x1, Pallas kernels, prepare(): pl.pallas_call(prepare_kernel, in_specs=[pl.BlockSpec(memory_space=pltpu....  2.79 us
    pallas_call x1, Pallas kernels, begin(): pl.pallas_call(begin_kernel, in_specs=[pl.BlockSpec(memory_space=pltpu.HB...  1.59 us
  transfers between devices with their start and end apart: 27, of which 11 were waited for; matrix products, arithmetic and copies ran while one was open for 0% of the time, Pallas kernels for 12%

profile of v6, /device:TPU:0, one launch (start us, length us, event | category | flops | bytes accessed | tf_op | source)
XLA Modules:
  0.0 72.6 jit_solution(3895973560808988709)
XLA Ops:
  0.0 1.6 %begin.1 = (f32[128,512]{1,0:T(8,128)S(1)}, bf16[128,512]{1,0:T(8,128)(2,1)S(1)}, bf16[512,512]{1,0:T(8,128)(2,1)S(1)}, bf16[512,256]{1,0:T(8,128)(2,1)S(1)}, bf16[512,256]{1,0:T(8,128)(2,1)S(1)}) custom-call(bf16[512,128]{1,0:T(8,128)(2,1)} %k_hbm.3, bf16[512,512]{1,0:T(8,128)(2,1)} %token_hbm.1, bf16[256,1024]{1,0:T(8,128)(2,1)} %weight_hbm.1), custom_call_target="tpu_custom_call" | custom-call | tf_op jit(solution)/shard_map/begin/pallas_call | solution.py:177
  1.6 3.1 %collective-permute-start.3 = (bf16[128,512]{1,0:T(8,128)(2,1)S(1)}, bf16[128,512]{1,0:T(8,128)(2,1)S(1)}, u32[]{:S(2)}, u32[]{:S(2)}) collective-permute-start(bf16[128,512]{1,0:T(8,128)(2,1)S(1)} %get-tuple-element.15), channel_id=1, source_target_pairs={{0,4},{4,0},{8,12},{12,8},{16,20},{20,16},{24,28},{28,24},{1,5},{5... | collective-permute-start | bytes 393224 | tf_op jit(solution)/shard_map/ppermute | solution.py:22
  4.7 3.5 %collective-permute-done.3 = bf16[128,512]{1,0:T(8,128)(2,1)S(1)} collective-permute-done((bf16[128,512]{1,0:T(8,128)(2,1)S(1)}, bf16[128,512]{1,0:T(8,128)(2,1)S(1)}, u32[]{:S(2)}, u32[]{:S(2)}) %collective-permute-start.3) | collective-permute-done | bytes 131104 | tf_op jit(solution)/shard_map/ppermute | solution.py:22
  8.2 1.9 %collective-permute-start.4 = (bf16[128,512]{1,0:T(8,128)(2,1)S(1)}, bf16[128,512]{1,0:T(8,128)(2,1)S(1)}, u32[]{:S(2)}, u32[]{:S(2)}) collective-permute-start(bf16[128,512]{1,0:T(8,128)(2,1)S(1)} %fusion), channel_id=1, source_target_pairs={{0,8},{8,0},{4,12},{12,4},{16,24},{24,16},{20,28},{28,20},{1,9},{9... | collective-permute-start | bytes 393224 | tf_op jit(solution)/shard_map/ppermute | solution.py:22
  10.0 1.5 %collective-permute-start.24 = (bf16[512,256]{1,0:T(8,128)(2,1)S(1)}, bf16[512,256]{1,0:T(8,128)(2,1)S(1)}, u32[]{:S(2)}, u32[]{:S(2)}) collective-permute-start(bf16[512,256]{1,0:T(8,128)(2,1)S(1)} %get-tuple-element.17.refs_4_), channel_id=1, source_target_pairs={{8,0},{16,8},{24,16},{28,24},{20,28},{12,20},{4,12},{0,4},{9,1},{1... | collective-permute-start | bytes 786440 | tf_op jit(solution)/shard_map/ppermute | solution.py:427
  11.6 0.5 collective-permute-start.13
  12.1 1.1 %collective-permute-start.21 = (bf16[512,256]{1,0:T(8,128)(2,1)S(1)}, bf16[512,256]{1,0:T(8,128)(2,1)S(1)}, u32[]{:S(2)}, u32[]{:S(2)}) collective-permute-start(bf16[512,256]{1,0:T(8,128)(2,1)S(1)} %get-tuple-element.18.refs_5_), channel_id=1, source_target_pairs={{0,8},{8,16},{16,24},{24,28},{28,20},{20,12},{12,4},{4,0},{1,9},{9... | collective-permute-start | bytes 786440 | tf_op jit(solution)/shard_map/ppermute | solution.py:427
  13.2 0.9 %collective-permute-start.17 = (bf16[512,256]{1,0:T(8,128)(2,1)S(1)}, bf16[512,256]{1,0:T(8,128)(2,1)S(1)}, u32[]{:S(2)}, u32[]{:S(2)}) collective-permute-start(bf16[512,256]{1,0:T(8,128)(2,1)S(1)} %get-tuple-element.18.refs_5_), channel_id=1, source_target_pairs={{8,0},{16,8},{24,16},{28,24},{20,28},{12,20},{4,12},{0,4},{9,1},{1... | collective-permute-start | bytes 786440 | tf_op jit(solution)/shard_map/ppermute | solution.py:427
  14.1 0.5 collective-permute-done.4
  14.7 0.7 collective-permute-start.8
  15.4 4.9 %collective-permute-done.24.refs_8_ = bf16[512,256]{1,0:T(8,128)(2,1)S(1)} collective-permute-done((bf16[512,256]{1,0:T(8,128)(2,1)S(1)}, bf16[512,256]{1,0:T(8,128)(2,1)S(1)}, u32[]{:S(2)}, u32[]{:S(2)}) %collective-permute-start.24) | collective-permute-done | bytes 262176 | tf_op jit(solution)/shard_map/ppermute | solution.py:427
  20.2 1.7 %collective-permute-start.6 = (bf16[256,512]{1,0:T(8,128)(2,1)S(1)}, bf16[256,512]{1,0:T(8,128)(2,1)S(1)}, u32[]{:S(2)}, u32[]{:S(2)}) collective-permute-start(bf16[256,512]{1,0:T(8,128)(2,1)S(1)} %constant_dynamic-update-slice_fusion.refs_0_.refs_4_), channel_id=1, source_target_pairs={{0,2},{2,0},{1,3},{3,1},{4,6},{6,4},{5,7},{7,5},{8,10},{10,8},{9,1... | collective-permute-start | bytes 786440 | tf_op jit(solution)/shard_map/ppermute | solution.py:22
  22.0 0.0 collective-permute-start.5
  22.0 0.0 collective-permute-done.8
  22.0 0.7 collective-permute-start.9
  22.6 1.2 %collective-permute-done.21.refs_7_ = bf16[512,256]{1,0:T(8,128)(2,1)S(1)} collective-permute-done((bf16[512,256]{1,0:T(8,128)(2,1)S(1)}, bf16[512,256]{1,0:T(8,128)(2,1)S(1)}, u32[]{:S(2)}, u32[]{:S(2)}) %collective-permute-start.21) | collective-permute-done | bytes 262176 | tf_op jit(solution)/shard_map/ppermute | solution.py:427
  23.8 1.5 %collective-permute-start.1 = (bf16[512,512]{1,0:T(8,128)(2,1)S(1)}, bf16[512,512]{1,0:T(8,128)(2,1)S(1)}, u32[]{:S(2)}, u32[]{:S(2)}) collective-permute-start(bf16[512,512]{1,0:T(8,128)(2,1)S(1)} %get-tuple-element.14.refs_0_), channel_id=1, source_target_pairs={{0,2},{2,0},{1,3},{3,1},{4,6},{6,4},{5,7},{7,5},{8,10},{10,8},{9,1... | collective-permute-start | bytes 1572872 | tf_op jit(solution)/shard_map/ppermute | solution.py:22
  25.3 2.4 %collective-permute-start.25 = (bf16[512,256]{1,0:T(8,128)(2,1)S(1)}, bf16[512,256]{1,0:T(8,128)(2,1)S(1)}, u32[]{:S(2)}, u32[]{:S(2)}) collective-permute-start(bf16[512,256]{1,0:T(8,128)(2,1)S(1)} %collective-permute-done.24.refs_8_), channel_id=1, source_target_pairs={{8,0},{16,8},{24,16},{28,24},{20,28},{12,20},{4,12},{0,4},{9,1},{1... | collective-permute-start | bytes 786440 | tf_op jit(solution)/shard_map/ppermute | solution.py:427
  27.7 0.7 collective-permute-start.14
  28.4 0.0 collective-permute-done.6.refs_2_.refs_6_
  28.4 4.4 %collective-permute-start.22 = (bf16[512,256]{1,0:T(8,128)(2,1)S(1)}, bf16[512,256]{1,0:T(8,128)(2,1)S(1)}, u32[]{:S(2)}, u32[]{:S(2)}) collective-permute-start(bf16[512,256]{1,0:T(8,128)(2,1)S(1)} %collective-permute-done.21.refs_7_), channel_id=1, source_target_pairs={{0,8},{8,16},{16,24},{24,28},{28,20},{20,12},{12,4},{4,0},{1,9},{9... | collective-permute-start | bytes 786440 | tf_op jit(solution)/shard_map/ppermute | solution.py:427
  32.7 1.6 %collective-permute-done.25.refs_6_.refs_12_ = bf16[512,256]{1,0:T(8,128)(2,1)S(1)} collective-permute-done((bf16[512,256]{1,0:T(8,128)(2,1)S(1)}, bf16[512,256]{1,0:T(8,128)(2,1)S(1)}, u32[]{:S(2)}, u32[]{:S(2)}) %collective-permute-start.25) | collective-permute-done | bytes 262176 | tf_op jit(solution)/shard_map/ppermute | solution.py:427
  34.4 0.0 collective-permute-start.7
  34.4 2.6 %collective-permute-done.14.refs_4_.refs_10_ = bf16[512,256]{1,0:T(8,128)(2,1)S(1)} collective-permute-done((bf16[512,256]{1,0:T(8,128)(2,1)S(1)}, bf16[512,256]{1,0:T(8,128)(2,1)S(1)}, u32[]{:S(2)}, u32[]{:S(2)}) %collective-permute-start.14) | collective-permute-done | bytes 262176 | tf_op jit(solution)/shard_map/ppermute | solution.py:427
  37.0 2.7 %collective-permute-start.26 = (bf16[512,256]{1,0:T(8,128)(2,1)S(1)}, bf16[512,256]{1,0:T(8,128)(2,1)S(1)}, u32[]{:S(2)}, u32[]{:S(2)}) collective-permute-start(bf16[512,256]{1,0:T(8,128)(2,1)S(1)} %collective-permute-done.25.refs_6_.refs_12_), channel_id=1, source_target_pairs={{8,0},{16,8},{24,16},{28,24},{20,28},{12,20},{4,12},{0,4},{9,1},{1... | collective-permute-start | bytes 786440 | tf_op jit(solution)/shard_map/ppermute | solution.py:427
  39.7 0.1 collective-permute-done.22.refs_5_.refs_11_
  39.8 1.0 %collective-permute-start.11 = (bf16[128,512]{1,0:T(8,128)(2,1)S(1)}, bf16[128,512]{1,0:T(8,128)(2,1)S(1)}, u32[]{:S(2)}, u32[]{:S(2)}) collective-permute-start(bf16[128,512]{1,0:T(8,128)(2,1)S(1)} %add.11.refs_0_.refs_8_), channel_id=1, source_target_pairs={{0,2},{2,0},{1,3},{3,1},{4,6},{6,4},{5,7},{7,5},{8,10},{10,8},{9,1... | collective-permute-start | bytes 393224 | tf_op jit(solution)/shard_map/ppermute | solution.py:22
  40.7 0.5 collective-permute-done.18.refs_7_.refs_13_
  41.3 0.0 collective-permute-start.10
  41.3 0.0 collective-permute-done.1.refs_2_
  41.3 0.5 collective-permute-start
  41.8 3.0 %collective-permute-done.11.refs_2_.refs_10_ = bf16[128,512]{1,0:T(8,128)(2,1)S(1)} collective-permute-done((bf16[128,512]{1,0:T(8,128)(2,1)S(1)}, bf16[128,512]{1,0:T(8,128)(2,1)S(1)}, u32[]{:S(2)}, u32[]{:S(2)}) %collective-permute-start.11) | collective-permute-done | bytes 131104 | tf_op jit(solution)/shard_map/ppermute | solution.py:22
  44.8 1.2 %collective-permute-start.15 = (bf16[512,256]{1,0:T(8,128)(2,1)S(1)}, bf16[512,256]{1,0:T(8,128)(2,1)S(1)}, u32[]{:S(2)}, u32[]{:S(2)}) collective-permute-start(bf16[512,256]{1,0:T(8,128)(2,1)S(1)} %collective-permute-done.14.refs_4_.refs_10_), channel_id=1, source_target_pairs={{0,8},{8,16},{16,24},{24,28},{28,20},{20,12},{12,4},{4,0},{1,9},{9... | collective-permute-start | bytes 786440 | tf_op jit(solution)/shard_map/ppermute | solution.py:427
  45.9 1.6 %collective-permute-start.19 = (bf16[512,256]{1,0:T(8,128)(2,1)S(1)}, bf16[512,256]{1,0:T(8,128)(2,1)S(1)}, u32[]{:S(2)}, u32[]{:S(2)}) collective-permute-start(bf16[512,256]{1,0:T(8,128)(2,1)S(1)} %collective-permute-done.18.refs_7_.refs_13_), channel_id=1, source_target_pairs={{8,0},{16,8},{24,16},{28,24},{20,28},{12,20},{4,12},{0,4},{9,1},{1... | collective-permute-start | bytes 786440 | tf_op jit(solution)/shard_map/ppermute | solution.py:427
  47.5 1.0 %collective-permute-start.23 = (bf16[512,256]{1,0:T(8,128)(2,1)S(1)}, bf16[512,256]{1,0:T(8,128)(2,1)S(1)}, u32[]{:S(2)}, u32[]{:S(2)}) collective-permute-start(bf16[512,256]{1,0:T(8,128)(2,1)S(1)} %collective-permute-done.22.refs_5_.refs_11_), channel_id=1, source_target_pairs={{0,8},{8,16},{16,24},{24,28},{28,20},{20,12},{12,4},{4,0},{1,9},{9... | collective-permute-start | bytes 786440 | tf_op jit(solution)/shard_map/ppermute | solution.py:427
  48.6 6.0 %collective-permute-done.15.refs_8_.refs_14_ = bf16[512,256]{1,0:T(8,128)(2,1)S(1)} collective-permute-done((bf16[512,256]{1,0:T(8,128)(2,1)S(1)}, bf16[512,256]{1,0:T(8,128)(2,1)S(1)}, u32[]{:S(2)}, u32[]{:S(2)}) %collective-permute-start.15) | collective-permute-done | bytes 262176 | tf_op jit(solution)/shard_map/ppermute | solution.py:427
  54.6 0.6 collective-permute-start.16
  55.2 1.4 %collective-permute-start.20 = (bf16[512,256]{1,0:T(8,128)(2,1)S(1)}, bf16[512,256]{1,0:T(8,128)(2,1)S(1)}, u32[]{:S(2)}, u32[]{:S(2)}) collective-permute-start(bf16[512,256]{1,0:T(8,128)(2,1)S(1)} %collective-permute-done.19.refs_11_.refs_17_), channel_id=1, source_target_pairs={{8,0},{16,8},{24,16},{28,24},{20,28},{12,20},{4,12},{0,4},{9,1},{1... | collective-permute-start | bytes 786440 | tf_op jit(solution)/shard_map/ppermute | solution.py:427
  56.7 3.6 %collective-permute-done.23.refs_9_.refs_15_ = bf16[512,256]{1,0:T(8,128)(2,1)S(1)} collective-permute-done((bf16[512,256]{1,0:T(8,128)(2,1)S(1)}, bf16[512,256]{1,0:T(8,128)(2,1)S(1)}, u32[]{:S(2)}, u32[]{:S(2)}) %collective-permute-start.23) | collective-permute-done | bytes 262176 | tf_op jit(solution)/shard_map/ppermute | solution.py:427
  60.2 2.8 %prepare.1 = (bf16[16,512,256]{2,1,0:T(8,128)(2,1)S(1)}, bf16[512,512]{1,0:T(8,128)(2,1)S(1)}) custom-call(bf16[512,128]{1,0:T(8,128)(2,1)} %refs_17_.1, bf16[512,128]{1,0:T(8,128)(2,1)} %k_hbm.3, f32[13,16,512]{2,1,0:T(8,128)} %refs_18_.1), custom_call_target="tpu_custom_call" | custom-call | tf_op jit(solution)/shard_map/prepare/pallas_call | solution.py:132
  63.0 1.1 %shard_map.57.refs_13_ = f32[1024,256]{1,0:T(8,128)S(1)} custom-call(bf16[256,512]{1,0:T(8,128)(2,1)S(1)} %constant_dynamic-update-slice_fusion.refs_0_.refs_4_, bf16[256,512]{1,0:T(8,128)(2,1)S(1)} %collective-permute-done.5.refs_1_.refs_5_, bf16[256,512]{1,0:T(8,128)(2,1)S(1)} %collective-permute-done.6.refs_2_.refs_6_, ...), custom_call_target="tpu_custom_call" | custom-call | tf_op jit(solution)/shard_map/pallas_call | solution.py:251
  64.2 1.4 %shard_map.59.refs_16_ = f32[1024,128]{1,0:T(8,128)S(1)} custom-call(bf16[128,512]{1,0:T(8,128)(2,1)S(1)} %add.11.refs_0_.refs_8_, bf16[128,512]{1,0:T(8,128)(2,1)S(1)} %collective-permute-done.10.refs_1_.refs_9_, bf16[128,512]{1,0:T(8,128)(2,1)S(1)} %collective-permute-done.11.refs_2_.refs_10_, ...), custom_call_target="tpu_custom_call" | custom-call | tf_op jit(solution)/shard_map/pallas_call | solution.py:251
  65.6 1.2 %shard_map.55.refs_8_ = f32[1024,512]{1,0:T(8,128)S(1)} custom-call(bf16[512,512]{1,0:T(8,128)(2,1)S(1)} %get-tuple-element.14.refs_0_, bf16[512,512]{1,0:T(8,128)(2,1)S(1)} %collective-permute-done.refs_1_, bf16[512,512]{1,0:T(8,128)(2,1)S(1)} %collective-permute-done.1.refs_2_, bf16[512,512]{1,0:T(8,128)(2,1)S(1)} %collective-permute-done.2.refs_3_, ...), custom_call_target="tpu_custom_call" | custom-call | tf_op jit(solution)/shard_map/pallas_call | solution.py:251
  66.8 0.9 %shard_map.56.refs_12_ = f32[1024,512]{1,0:T(8,128)S(1)} custom-call(bf16[512,512]{1,0:T(8,128)(2,1)S(1)} %get-tuple-element.14.refs_0_, bf16[512,512]{1,0:T(8,128)(2,1)S(1)} %collective-permute-done.refs_1_, bf16[512,512]{1,0:T(8,128)(2,1)S(1)} %collective-permute-done.1.refs_2_, bf16[512,512]{1,0:T(8,128)(2,1)S(1)} %collective-permute-done.2.refs_3_, ...), custom_call_target="tpu_custom_call" | custom-call | tf_op jit(solution)/shard_map/pallas_call | solution.py:251
  67.6 0.0 copy-start
  67.6 0.0 copy-start.1
  67.6 1.2 %shard_map.58 = (f32[1024,512]{1,0:T(8,128)S(1)}, f32[1024,256]{1,0:T(8,128)S(1)}) custom-call(bf16[512,512]{1,0:T(8,128)(2,1)S(1)} %get-tuple-element.14.refs_0_, bf16[512,512]{1,0:T(8,128)(2,1)S(1)} %collective-permute-done.refs_1_, bf16[512,512]{1,0:T(8,128)(2,1)S(1)} %collective-permute-done.1.refs_2_, ...), custom_call_target="tpu_custom_call" | custom-call | tf_op jit(solution)/shard_map/pallas_call | solution.py:251
  68.9 3.7 %finish.1 = bf16[512,1024]{1,0:T(8,128)(2,1)} custom-call(bf16[512,512]{1,0:T(8,128)(2,1)S(1)} %get-tuple-element.14.refs_0_, bf16[512,512]{1,0:T(8,128)(2,1)S(1)} %collective-permute-done.refs_1_, bf16[512,512]{1,0:T(8,128)(2,1)S(1)} %collective-permute-done.1.refs_2_, bf16[512,512]{1,0:T(8,128)(2,1)S(1)} %collective-permute-done.2.refs_3_, ...), custom_call_target="tpu_custom_call" | custom-call | tf_op jit(solution)/shard_map/finish/pallas_call | solution.py:365
  (23 shorter events, 0.2 us)
Async XLA Ops:
  1.6 6.6 %collective-permute-start.3 = (bf16[128,512]{1,0:T(8,128)(2,1)S(1)}, bf16[128,512]{1,0:T(8,128)(2,1)S(1)}, u32[]{:S(2)}, u32[]{:S(2)}) collective-permute-start(bf16[128,512]{1,0:T(8,128)(2,1)S(1)} %get-tuple-element.15), channel_id=1, source_target_pairs={{0,4},{4,0},{8,12},{12,8},{16,20},{20,16},{24,28},{28,24},{1,5},{5... | collective-permute-start | bytes 393224 | tf_op jit(solution)/shard_map/ppermute | solution.py:22
  8.2 6.4 %collective-permute-start.4 = (bf16[128,512]{1,0:T(8,128)(2,1)S(1)}, bf16[128,512]{1,0:T(8,128)(2,1)S(1)}, u32[]{:S(2)}, u32[]{:S(2)}) collective-permute-start(bf16[128,512]{1,0:T(8,128)(2,1)S(1)} %fusion), channel_id=1, source_target_pairs={{0,8},{8,0},{4,12},{12,4},{16,24},{24,16},{20,28},{28,20},{1,9},{9... | collective-permute-start | bytes 393224 | tf_op jit(solution)/shard_map/ppermute | solution.py:22
  10.0 10.2 %collective-permute-start.24 = (bf16[512,256]{1,0:T(8,128)(2,1)S(1)}, bf16[512,256]{1,0:T(8,128)(2,1)S(1)}, u32[]{:S(2)}, u32[]{:S(2)}) collective-permute-start(bf16[512,256]{1,0:T(8,128)(2,1)S(1)} %get-tuple-element.17.refs_4_), channel_id=1, source_target_pairs={{8,0},{16,8},{24,16},{28,24},{20,28},{12,20},{4,12},{0,4},{9,1},{1... | collective-permute-start | bytes 786440 | tf_op jit(solution)/shard_map/ppermute | solution.py:427
  11.6 10.4 %collective-permute-start.13 = (bf16[512,256]{1,0:T(8,128)(2,1)S(1)}, bf16[512,256]{1,0:T(8,128)(2,1)S(1)}, u32[]{:S(2)}, u32[]{:S(2)}) collective-permute-start(bf16[512,256]{1,0:T(8,128)(2,1)S(1)} %get-tuple-element.17.refs_4_), channel_id=1, source_target_pairs={{0,8},{8,16},{16,24},{24,28},{28,20},{20,12},{12,4},{4,0},{1,9},{9... | collective-permute-start | bytes 786440 | tf_op jit(solution)/shard_map/ppermute | solution.py:427
  12.1 11.7 %collective-permute-start.21 = (bf16[512,256]{1,0:T(8,128)(2,1)S(1)}, bf16[512,256]{1,0:T(8,128)(2,1)S(1)}, u32[]{:S(2)}, u32[]{:S(2)}) collective-permute-start(bf16[512,256]{1,0:T(8,128)(2,1)S(1)} %get-tuple-element.18.refs_5_), channel_id=1, source_target_pairs={{0,8},{8,16},{16,24},{24,28},{28,20},{20,12},{12,4},{4,0},{1,9},{9... | collective-permute-start | bytes 786440 | tf_op jit(solution)/shard_map/ppermute | solution.py:427
  13.2 12.1 %collective-permute-start.17 = (bf16[512,256]{1,0:T(8,128)(2,1)S(1)}, bf16[512,256]{1,0:T(8,128)(2,1)S(1)}, u32[]{:S(2)}, u32[]{:S(2)}) collective-permute-start(bf16[512,256]{1,0:T(8,128)(2,1)S(1)} %get-tuple-element.18.refs_5_), channel_id=1, source_target_pairs={{8,0},{16,8},{24,16},{28,24},{20,28},{12,20},{4,12},{0,4},{9,1},{1... | collective-permute-start | bytes 786440 | tf_op jit(solution)/shard_map/ppermute | solution.py:427
  14.7 7.3 %collective-permute-start.8 = (bf16[128,512]{1,0:T(8,128)(2,1)S(1)}, bf16[128,512]{1,0:T(8,128)(2,1)S(1)}, u32[]{:S(2)}, u32[]{:S(2)}) collective-permute-start(bf16[128,512]{1,0:T(8,128)(2,1)S(1)} %add_convert_fusion), channel_id=1, source_target_pairs={{8,16},{12,20},{9,17},{13,21},{10,18},{14,22},{11,19},{15,23}} | collective-permute-start | bytes 393224 | tf_op jit(solution)/shard_map/ppermute | solution.py:401
  20.2 8.1 %collective-permute-start.6 = (bf16[256,512]{1,0:T(8,128)(2,1)S(1)}, bf16[256,512]{1,0:T(8,128)(2,1)S(1)}, u32[]{:S(2)}, u32[]{:S(2)}) collective-permute-start(bf16[256,512]{1,0:T(8,128)(2,1)S(1)} %constant_dynamic-update-slice_fusion.refs_0_.refs_4_), channel_id=1, source_target_pairs={{0,2},{2,0},{1,3},{3,1},{4,6},{6,4},{5,7},{7,5},{8,10},{10,8},{9,1... | collective-permute-start | bytes 786440 | tf_op jit(solution)/shard_map/ppermute | solution.py:22
  22.0 10.8 %collective-permute-start.5 = (bf16[256,512]{1,0:T(8,128)(2,1)S(1)}, bf16[256,512]{1,0:T(8,128)(2,1)S(1)}, u32[]{:S(2)}, u32[]{:S(2)}) collective-permute-start(bf16[256,512]{1,0:T(8,128)(2,1)S(1)} %constant_dynamic-update-slice_fusion.refs_0_.refs_4_), channel_id=1, source_target_pairs={{0,1},{1,0},{2,3},{3,2},{4,5},{5,4},{6,7},{7,6},{8,9},{9,8},{10,11... | collective-permute-start | bytes 786440 | tf_op jit(solution)/shard_map/ppermute | solution.py:22
  22.0 5.7 %collective-permute-start.9 = (bf16[128,512]{1,0:T(8,128)(2,1)S(1)}, bf16[128,512]{1,0:T(8,128)(2,1)S(1)}, u32[]{:S(2)}, u32[]{:S(2)}) collective-permute-start(bf16[128,512]{1,0:T(8,128)(2,1)S(1)} %collective-permute-done.8), channel_id=1, source_target_pairs={{16,24},{20,28},{17,25},{21,29},{18,26},{22,30},{19,27},{23,31}} | collective-permute-start | bytes 393224 | tf_op jit(solution)/shard_map/ppermute | solution.py:401
  23.8 17.5 %collective-permute-start.1 = (bf16[512,512]{1,0:T(8,128)(2,1)S(1)}, bf16[512,512]{1,0:T(8,128)(2,1)S(1)}, u32[]{:S(2)}, u32[]{:S(2)}) collective-permute-start(bf16[512,512]{1,0:T(8,128)(2,1)S(1)} %get-tuple-element.14.refs_0_), channel_id=1, source_target_pairs={{0,2},{2,0},{1,3},{3,1},{4,6},{6,4},{5,7},{7,5},{8,10},{10,8},{9,1... | collective-permute-start | bytes 1572872 | tf_op jit(solution)/shard_map/ppermute | solution.py:22
  25.3 9.1 %collective-permute-start.25 = (bf16[512,256]{1,0:T(8,128)(2,1)S(1)}, bf16[512,256]{1,0:T(8,128)(2,1)S(1)}, u32[]{:S(2)}, u32[]{:S(2)}) collective-permute-start(bf16[512,256]{1,0:T(8,128)(2,1)S(1)} %collective-permute-done.24.refs_8_), channel_id=1, source_target_pairs={{8,0},{16,8},{24,16},{28,24},{20,28},{12,20},{4,12},{0,4},{9,1},{1... | collective-permute-start | bytes 786440 | tf_op jit(solution)/shard_map/ppermute | solution.py:427
  27.7 9.3 %collective-permute-start.14 = (bf16[512,256]{1,0:T(8,128)(2,1)S(1)}, bf16[512,256]{1,0:T(8,128)(2,1)S(1)}, u32[]{:S(2)}, u32[]{:S(2)}) collective-permute-start(bf16[512,256]{1,0:T(8,128)(2,1)S(1)} %collective-permute-done.13.refs_6_), channel_id=1, source_target_pairs={{0,8},{8,16},{16,24},{24,28},{28,20},{20,12},{12,4},{4,0},{1,9},{9... | collective-permute-start | bytes 786440 | tf_op jit(solution)/shard_map/ppermute | solution.py:427
  28.4 11.4 %collective-permute-start.22 = (bf16[512,256]{1,0:T(8,128)(2,1)S(1)}, bf16[512,256]{1,0:T(8,128)(2,1)S(1)}, u32[]{:S(2)}, u32[]{:S(2)}) collective-permute-start(bf16[512,256]{1,0:T(8,128)(2,1)S(1)} %collective-permute-done.21.refs_7_), channel_id=1, source_target_pairs={{0,8},{8,16},{16,24},{24,28},{28,20},{20,12},{12,4},{4,0},{1,9},{9... | collective-permute-start | bytes 786440 | tf_op jit(solution)/shard_map/ppermute | solution.py:427
  32.7 8.5 %collective-permute-start.18 = (bf16[512,256]{1,0:T(8,128)(2,1)S(1)}, bf16[512,256]{1,0:T(8,128)(2,1)S(1)}, u32[]{:S(2)}, u32[]{:S(2)}) collective-permute-start(bf16[512,256]{1,0:T(8,128)(2,1)S(1)} %collective-permute-done.17.refs_9_), channel_id=1, source_target_pairs={{8,0},{16,8},{24,16},{28,24},{20,28},{12,20},{4,12},{0,4},{9,1},{1... | collective-permute-start | bytes 786440 | tf_op jit(solution)/shard_map/ppermute | solution.py:427
  34.4 11.5 %collective-permute-start.7 = (bf16[256,512]{1,0:T(8,128)(2,1)S(1)}, bf16[256,512]{1,0:T(8,128)(2,1)S(1)}, u32[]{:S(2)}, u32[]{:S(2)}) collective-permute-start(bf16[256,512]{1,0:T(8,128)(2,1)S(1)} %collective-permute-done.6.refs_2_.refs_6_), channel_id=1, source_target_pairs={{0,1},{1,0},{2,3},{3,2},{4,5},{5,4},{6,7},{7,6},{8,9},{9,8},{10,11... | collective-permute-start | bytes 786440 | tf_op jit(solution)/shard_map/ppermute | solution.py:22
  37.0 10.6 %collective-permute-start.26 = (bf16[512,256]{1,0:T(8,128)(2,1)S(1)}, bf16[512,256]{1,0:T(8,128)(2,1)S(1)}, u32[]{:S(2)}, u32[]{:S(2)}) collective-permute-start(bf16[512,256]{1,0:T(8,128)(2,1)S(1)} %collective-permute-done.25.refs_6_.refs_12_), channel_id=1, source_target_pairs={{8,0},{16,8},{24,16},{28,24},{20,28},{12,20},{4,12},{0,4},{9,1},{1... | collective-permute-start | bytes 786440 | tf_op jit(solution)/shard_map/ppermute | solution.py:427
  39.8 5.0 %collective-permute-start.11 = (bf16[128,512]{1,0:T(8,128)(2,1)S(1)}, bf16[128,512]{1,0:T(8,128)(2,1)S(1)}, u32[]{:S(2)}, u32[]{:S(2)}) collective-permute-start(bf16[128,512]{1,0:T(8,128)(2,1)S(1)} %add.11.refs_0_.refs_8_), channel_id=1, source_target_pairs={{0,2},{2,0},{1,3},{3,1},{4,6},{6,4},{5,7},{7,5},{8,10},{10,8},{9,1... | collective-permute-start | bytes 393224 | tf_op jit(solution)/shard_map/ppermute | solution.py:22
  41.3 3.5 %collective-permute-start.10 = (bf16[128,512]{1,0:T(8,128)(2,1)S(1)}, bf16[128,512]{1,0:T(8,128)(2,1)S(1)}, u32[]{:S(2)}, u32[]{:S(2)}) collective-permute-start(bf16[128,512]{1,0:T(8,128)(2,1)S(1)} %add.11.refs_0_.refs_8_), channel_id=1, source_target_pairs={{0,1},{1,0},{2,3},{3,2},{4,5},{5,4},{6,7},{7,6},{8,9},{9,8},{10,11... | collective-permute-start | bytes 393224 | tf_op jit(solution)/shard_map/ppermute | solution.py:22
  41.3 24.3 %collective-permute-start = (bf16[512,512]{1,0:T(8,128)(2,1)S(1)}, bf16[512,512]{1,0:T(8,128)(2,1)S(1)}, u32[]{:S(2)}, u32[]{:S(2)}) collective-permute-start(bf16[512,512]{1,0:T(8,128)(2,1)S(1)} %get-tuple-element.14.refs_0_), channel_id=1, source_target_pairs={{0,1},{1,0},{2,3},{3,2},{4,5},{5,4},{6,7},{7,6},{8,9},{9,8},{10,11... | collective-permute-start | bytes 1572872 | tf_op jit(solution)/shard_map/ppermute | solution.py:22
  44.8 20.8 %collective-permute-start.2 = (bf16[512,512]{1,0:T(8,128)(2,1)S(1)}, bf16[512,512]{1,0:T(8,128)(2,1)S(1)}, u32[]{:S(2)}, u32[]{:S(2)}) collective-permute-start(bf16[512,512]{1,0:T(8,128)(2,1)S(1)} %collective-permute-done.1.refs_2_), channel_id=1, source_target_pairs={{0,1},{1,0},{2,3},{3,2},{4,5},{5,4},{6,7},{7,6},{8,9},{9,8},{10,11... | collective-permute-start | bytes 1572872 | tf_op jit(solution)/shard_map/ppermute | solution.py:22
  44.8 9.9 %collective-permute-start.15 = (bf16[512,256]{1,0:T(8,128)(2,1)S(1)}, bf16[512,256]{1,0:T(8,128)(2,1)S(1)}, u32[]{:S(2)}, u32[]{:S(2)}) collective-permute-start(bf16[512,256]{1,0:T(8,128)(2,1)S(1)} %collective-permute-done.14.refs_4_.refs_10_), channel_id=1, source_target_pairs={{0,8},{8,16},{16,24},{24,28},{28,20},{20,12},{12,4},{4,0},{1,9},{9... | collective-permute-start | bytes 786440 | tf_op jit(solution)/shard_map/ppermute | solution.py:427
  45.9 9.3 %collective-permute-start.19 = (bf16[512,256]{1,0:T(8,128)(2,1)S(1)}, bf16[512,256]{1,0:T(8,128)(2,1)S(1)}, u32[]{:S(2)}, u32[]{:S(2)}) collective-permute-start(bf16[512,256]{1,0:T(8,128)(2,1)S(1)} %collective-permute-done.18.refs_7_.refs_13_), channel_id=1, source_target_pairs={{8,0},{16,8},{24,16},{28,24},{20,28},{12,20},{4,12},{0,4},{9,1},{1... | collective-permute-start | bytes 786440 | tf_op jit(solution)/shard_map/ppermute | solution.py:427
  47.5 12.7 %collective-permute-start.23 = (bf16[512,256]{1,0:T(8,128)(2,1)S(1)}, bf16[512,256]{1,0:T(8,128)(2,1)S(1)}, u32[]{:S(2)}, u32[]{:S(2)}) collective-permute-start(bf16[512,256]{1,0:T(8,128)(2,1)S(1)} %collective-permute-done.22.refs_5_.refs_11_), channel_id=1, source_target_pairs={{0,8},{8,16},{16,24},{24,28},{28,20},{20,12},{12,4},{4,0},{1,9},{9... | collective-permute-start | bytes 786440 | tf_op jit(solution)/shard_map/ppermute | solution.py:427
  54.6 14.2 %collective-permute-start.16 = (bf16[512,256]{1,0:T(8,128)(2,1)S(1)}, bf16[512,256]{1,0:T(8,128)(2,1)S(1)}, u32[]{:S(2)}, u32[]{:S(2)}) collective-permute-start(bf16[512,256]{1,0:T(8,128)(2,1)S(1)} %collective-permute-done.15.refs_8_.refs_14_), channel_id=1, source_target_pairs={{0,8},{8,16},{16,24},{24,28},{28,20},{20,12},{12,4},{4,0},{1,9},{9... | collective-permute-start | bytes 786440 | tf_op jit(solution)/shard_map/ppermute | solution.py:427
  55.2 13.6 %collective-permute-start.20 = (bf16[512,256]{1,0:T(8,128)(2,1)S(1)}, bf16[512,256]{1,0:T(8,128)(2,1)S(1)}, u32[]{:S(2)}, u32[]{:S(2)}) collective-permute-start(bf16[512,256]{1,0:T(8,128)(2,1)S(1)} %collective-permute-done.19.refs_11_.refs_17_), channel_id=1, source_target_pairs={{8,0},{16,8},{24,16},{28,24},{20,28},{12,20},{4,12},{0,4},{9,1},{1... | collective-permute-start | bytes 786440 | tf_op jit(solution)/shard_map/ppermute | solution.py:427
  60.2 3.9 %collective-permute-start.12 = (bf16[128,512]{1,0:T(8,128)(2,1)S(1)}, bf16[128,512]{1,0:T(8,128)(2,1)S(1)}, u32[]{:S(2)}, u32[]{:S(2)}) collective-permute-start(bf16[128,512]{1,0:T(8,128)(2,1)S(1)} %collective-permute-done.11.refs_2_.refs_10_), channel_id=1, source_target_pairs={{0,1},{1,0},{2,3},{3,2},{4,5},{5,4},{6,7},{7,6},{8,9},{9,8},{10,11... | collective-permute-start | bytes 393224 | tf_op jit(solution)/shard_map/ppermute | solution.py:22
  67.6 1.2 %copy-start = (f32[13,16,512]{2,1,0:T(8,128)S(1)}, f32[13,16,512]{2,1,0:T(8,128)}, u32[]{:S(2)}) copy-start(f32[13,16,512]{2,1,0:T(8,128)} %refs_18_.1) | copy-start | bytes 1277956
  67.6 1.2 %copy-start.1 = (bf16[512,128]{1,0:T(8,128)(2,1)S(1)}, bf16[512,128]{1,0:T(8,128)(2,1)}, u32[]{:S(2)}) copy-start(bf16[512,128]{1,0:T(8,128)(2,1)} %refs_17_.1) | copy-start | bytes 393220
